TPU v7x, 32 devices: a whole 2x2x4 slice. The times are simulated.
32 devices in a mesh: cuts: 2 (over y), group: 16 (over z, x, core).
Axes of the slice: x: 2, y: 2, z: 4, core: 2. Of those that a mesh axis runs over, the one named last changes fastest.
Arguments:
- stem_blocks: bfloat16 [2, 64, 1024, 512], P('cuts', None, 'group'), may hold values from -6 to 6
- cap_tensor: bfloat16 [2, 2, 256, 256], P('cuts'), may hold values from -0.1875 to 0.1875
- slot_rows: int32 [64, 1024], P('group'), may hold values from 0 to 1023
- counts: int32 [64], P('group'), may hold values from 128 to 1024, as said below
Outputs:
- amplitudes: bfloat16 [1024, 64, 512], P('cuts', 'group')
Inputs may be any that keep to these rules, and one draw needn't show every extreme that they name: `counts`: some group has exactly 1024 live slots in every draw.
All inputs are finite; a program needn't handle non-finite values.
Results may differ from a plain program's by a relative error of at most 0.0052.
Values may be sent and summed in bfloat16 or wider, within the bound.
No kernel may reach another device: no remote copies, remote signals or barrier semaphores. Data moves between devices by JAX's collectives and lax.ppermute only.
A program may use at most 64 MiB of HBM per device.

v0:
```python
import jax
import jax.numpy as jnp
from jax import lax
from jax.sharding import PartitionSpec as P


def build_matrix(cap_pair):
    real_part = cap_pair[0]
    imag_part = cap_pair[1]
    upper = jnp.concatenate([real_part, imag_part], axis=1)
    lower = jnp.concatenate([-imag_part, real_part], axis=1)
    return jnp.concatenate([upper, lower], axis=0)


def local(stem_blocks, cap_tensor, slot_rows, counts):
    owned_rows = lax.all_to_all(stem_blocks[0], "group", split_axis=0, concat_axis=1, tiled=True)
    matrix = build_matrix(cap_tensor[0])
    slot_total = slot_rows.shape[1]
    share = slot_total // lax.axis_size("cuts")
    positions = jnp.arange(slot_total, dtype=jnp.int32)
    live_mask = positions[None, :] < counts[:, None]
    picked = jnp.take_along_axis(owned_rows, slot_rows[:, :, None], axis=1)
    product = jnp.einsum("gcr,rs->cgs", picked, matrix, preferred_element_type=jnp.float32)
    whole_sum = lax.psum(
        jnp.where(jnp.transpose(live_mask)[:, :, None], product, jnp.float32(0.0)).astype(
            jnp.bfloat16
        ),
        "cuts",
    ).astype(jnp.float32)
    summed = lax.dynamic_slice_in_dim(whole_sum, lax.axis_index("cuts") * share, share, 0)
    return summed.astype(jnp.bfloat16)


def solution(mesh):
    in_specs = (
        P("cuts", None, "group", None),
        P("cuts", None, None, None),
        P("group", None),
        P("group"),
    )
    out_specs = P("cuts", "group", None)
    return jax.shard_map(local, mesh=mesh, in_specs=in_specs, out_specs=out_specs, check_vma=False)
```

profile of v0, /device:TPU:0, one launch (start us, length us, event | category | flops | bytes accessed | tf_op | source)
XLA Modules:
  0.0 309.5 jit_solution(17406738748968861879)
XLA Ops:
  6.5 0.0 copy-start.1
  6.5 0.0 copy-start
  6.5 0.0 copy-start.2
  6.5 7.5 %all-to-all-start = ((bf16[64,64,512]{2,1,0:T(8,128)(2,1)}), bf16[64,64,512]{2,1,0:T(8,128)(2,1)}, u32[]{:S(2)}, u32[]{:S(2)}) async-start(bf16[64,64,512]{2,1,0:T(8,128)(2,1)} %bitcast.29), calls=%async_computation | async-start | bytes 8388608 | tf_op jit(solution)/shard_map/all_to_all | solution.py:16
  14.1 0.0 all-reduce.2.cloned.1.call-start
  14.1 0.0 copy-done.1
  14.2 0.0 copy-done
  14.2 0.1 copy.9
  14.3 0.1 copy.10
  14.4 0.0 copy-done.2
  14.4 0.1 iota_compare_fusion
  14.6 77.2 %all-to-all-done = bf16[64,64,512]{2,1,0:T(8,128)(2,1)} async-done(((bf16[64,64,512]{2,1,0:T(8,128)(2,1)}), bf16[64,64,512]{2,1,0:T(8,128)(2,1)}, u32[]{:S(2)}, u32[]{:S(2)}) %all-to-all-start) | async-done | bytes 4194336 | tf_op jit(solution)/shard_map/all_to_all | solution.py:16
  91.8 4.6 %copy.7 = bf16[16,4,64,512]{3,2,0,1:T(8,128)(2,1)} copy(bf16[16,4,64,512]{3,2,1,0:T(8,128)(2,1)} %bitcast.4) | data formatting | bytes 8388608 | tf_op jit(solution)/shard_map/all_to_all | solution.py:16
  96.4 72.8 %gather_fusion = bf16[4096,512]{1,0:T(8,128)(2,1)} fusion(bf16[4,1024,512]{2,1,0:T(8,128)(2,1)} %bitcast.26, s32[4096]{0:T(1024)S(1)} %bitcast.27), kind=kCustom, calls=%fused_computation | custom fusion | bytes 8421376 | tf_op jit(solution)/shard_map/jit(take_along_axis)/gather | solution.py:22
  169.2 5.8 %fusion = bf16[1024,4,512]{0,2,1:T(8,128)(2,1)} fusion(pred[1024,4]{0,1:T(4,128)(4,1)S(1)} %iota_compare_fusion, bf16[4,1024,512]{2,1,0:T(8,128)(2,1)} %bitcast.28, pred[4,1024]{1,0:T(4,128)(4,1)S(1)} %compare_and_fusion, bf16[256,256]{0,1:T(8,128)(2,1)S(1)} %bitcast.31, bf16[256,256]{0,1:T(8,128)(2,1)S(1)} %bitcast_negate_fusion, ...), kind=kOutput, calls=%fused_computation.2 | convolution fusion | flops 2155872256 | bytes 8790016 | tf_op jit(solution)/shard_map/gcr,rs->cgs/dot_general | solution.py:23
  175.0 0.0 all-reduce.2.cloned.1.call-update
  175.1 122.8 %all-reduce.2.cloned.1.call-done = bf16[1024,4,512]{0,2,1:T(8,128)(2,1)} async-done(((bf16[1024,4,512]{0,2,1:T(8,128)(2,1)}), bf16[1024,4,512]{0,2,1:T(8,128)(2,1)}) %all-reduce.2.cloned.1.call-update) | async-done | bytes 4194320 | tf_op jit(solution)/shard_map/psum | solution.py:24
  297.9 1.7 convert_convert_fusion
  299.6 3.1 copy.8
  (5 shorter events, 0.1 us)
Async XLA Ops:
  6.5 7.6 %copy-start.1 = (s32[4,1024]{1,0:T(4,128)S(1)}, s32[4,1024]{1,0:T(4,128)}, u32[]{:S(2)}) copy-start(s32[4,1024]{1,0:T(4,128)} %param.6) | copy-start | bytes 49156
  6.5 7.6 %copy-start = (bf16[1,2,256,256]{3,2,1,0:T(8,128)(2,1)S(1)}, bf16[1,2,256,256]{3,2,1,0:T(8,128)(2,1)}, u32[]{:S(2)}) copy-start(bf16[1,2,256,256]{3,2,1,0:T(8,128)(2,1)} %param.5) | copy-start | bytes 786436
  6.5 7.9 %copy-start.2 = (s32[4]{0:T(128)S(1)}, s32[4]{0:T(128)}, u32[]{:S(2)}) copy-start(s32[4]{0:T(128)} %param.7) | copy-start | bytes 52
  6.5 85.2 %all-to-all-start = ((bf16[64,64,512]{2,1,0:T(8,128)(2,1)}), bf16[64,64,512]{2,1,0:T(8,128)(2,1)}, u32[]{:S(2)}, u32[]{:S(2)}) async-start(bf16[64,64,512]{2,1,0:T(8,128)(2,1)} %bitcast.29), calls=%async_computation | async-start | bytes 8388608 | tf_op jit(solution)/shard_map/all_to_all | solution.py:16
  14.1 283.8 %all-reduce.2.cloned.1.call-start = ((), (), s32[]{:S(2)}) async-start(), calls=%async_computation.1 | async-start | bytes 8388608 | tf_op jit(solution)/shard_map/psum | solution.py:24
Sparse Core Ops, SparseCore 0:
  175.2 122.6 all-reduce.1
where the time goes:
time: 311 us; the launch traced here: 310 us
  waiting for transfers between devices  200 us (64%)
  local copies, waits for them, and re-layouts  80.7 us (26%)
  between operations  13.5 us (4%)
  starting transfers between devices  7.58 us (2%)
  matrix products  5.84 us (2%)
    psum x1, waiting for transfers between devices, local(): lax.psum(jnp.where(jnp.transpose(live_mask)[:, :, None], product, jnp.flo...  123 us
    all_to_all x1, waiting for transfers between devices, local(): lax.all_to_all(stem_blocks[0], 'group', split_axis=0, concat_axis=1, tile...  77.2 us
    gather x1, local copies, waits for them, and re-layouts, local(): picked = jnp.take_along_axis(owned_rows, slot_rows[:, :, None], axis=1)  72.8 us
    all_to_all x1, starting transfers between devices, local(): lax.all_to_all(stem_blocks[0], 'group', split_axis=0, concat_axis=1, tile...  7.54 us
  transfers between devices with their start and end apart: 2, of which 2 were waited for; matrix products, arithmetic and copies ran while one was open for 0% of the time, Pallas kernels for 0%

commit v1 on v0

v1 whole, which is shorter than its diff:
```python
import functools

import jax
import jax.numpy as jnp
from jax import lax
from jax.experimental import pallas as pl
from jax.experimental.pallas import tpu as pltpu
from jax.sharding import PartitionSpec as P


def build_matrix(cap_pair):
    real_part = cap_pair[0]
    imag_part = cap_pair[1]
    upper = jnp.concatenate([real_part, imag_part], axis=1)
    lower = jnp.concatenate([-imag_part, real_part], axis=1)
    return jnp.concatenate([upper, lower], axis=0)


def select_kernel(block, share, rows_ref, matrix_ref, slots_ref, *refs):
    outs, terms = refs[:-1], refs[-1]
    row_total = rows_ref.shape[0]
    for start in range(0, row_total, block):
        terms[pl.ds(start, block), :] = jnp.dot(
            rows_ref[pl.ds(start, block), :], matrix_ref[...], preferred_element_type=jnp.float32
        ).astype(terms.dtype)
    columns = lax.broadcasted_iota(jnp.int32, (block, row_total), 1)
    for part, out in enumerate(outs):
        for start in range(0, share, block):
            slots = slots_ref[pl.ds(part * share + start, block), :]
            chosen = jnp.where(columns == slots, 1.0, 0.0).astype(terms.dtype)
            out[pl.ds(start, block), :] = jnp.dot(
                chosen, terms[...], preferred_element_type=jnp.float32
            ).astype(out.dtype)


def select(rows, matrix, slots, parts):
    row_total, width = rows.shape
    slot_total = slots.shape[0]
    share = slot_total // parts
    block = min(256, share)
    out = jax.ShapeDtypeStruct((share, matrix.shape[1]), rows.dtype)
    flops = 2 * row_total * matrix.shape[1] * (width + slot_total)
    return pl.pallas_call(
        functools.partial(select_kernel, block, share),
        out_shape=[out] * parts,
        in_specs=[pl.BlockSpec(memory_space=pltpu.VMEM)] * 3,
        out_specs=[pl.BlockSpec(memory_space=pltpu.VMEM)] * parts,
        scratch_shapes=[pltpu.VMEM((row_total, matrix.shape[1]), rows.dtype)],
        cost_estimate=pl.CostEstimate(
            flops=flops,
            bytes_accessed=2 * (rows.size + slot_total * matrix.shape[1]),
            transcendentals=0,
        ),
        compiler_params=pltpu.CompilerParams(vmem_limit_bytes=24 << 20),
    )(rows, matrix, slots)


def local(stem_blocks, cap_tensor, slot_rows, counts):
    cuts, groups = lax.axis_size("cuts"), lax.axis_size("group")
    stem = stem_blocks[0]
    group_total, own_rows, width = stem.shape
    mine = group_total // groups
    slot_total = slot_rows.shape[1]
    share = slot_total // cuts
    matrix = build_matrix(cap_tensor[0])

    positions = jnp.arange(slot_total, dtype=jnp.int32)
    marked = jnp.where(positions[None, :] < counts[:, None], slot_rows, -1)
    me = lax.axis_index("cuts")
    doubled = jnp.concatenate([marked, marked], axis=1)
    turned = lax.dynamic_slice_in_dim(doubled, (me + 1) * share, slot_total, 1)
    by_owner = stem.reshape(groups, mine, own_rows, width)

    sums, selected = [], []
    for k in range(mine):
        outgoing = by_owner[:, k]
        if k >= 2:
            outgoing, selected[k - 2] = lax.optimization_barrier((outgoing, selected[k - 2]))
        got = lax.all_to_all(outgoing, "group", split_axis=0, concat_axis=0, tiled=True)
        parts = select(got.reshape(groups * own_rows, width), matrix, turned[k][:, None], cuts)
        selected.append(parts)
    for parts in selected:
        total = parts[-1].astype(jnp.float32)
        for step in range(1, cuts):
            ring = [(i, (i + step) % cuts) for i in range(cuts)]
            total = total + lax.ppermute(parts[step - 1], "cuts", ring).astype(jnp.float32)
        sums.append(total.astype(stem.dtype))
    return jnp.stack(sums, axis=1)


def solution(mesh):
    in_specs = (
        P("cuts", None, "group", None),
        P("cuts", None, None, None),
        P("group", None),
        P("group"),
    )
    out_specs = P("cuts", "group", None)
    return jax.shard_map(local, mesh=mesh, in_specs=in_specs, out_specs=out_specs, check_vma=False)
```

time: 311 us -> 153 us (0.49)
  waiting for transfers between devices: 200 us -> 64.6 us
  local copies, waits for them, and re-layouts: 80.7 us -> 20.9 us
  blocking collectives: 0 us -> 32.1 us
  starting transfers between devices: 7.58 us -> 23.9 us
  between operations: 13.5 us -> 0.19 us
  Pallas kernels: 0 us -> 7.41 us
  matrix products: 5.84 us -> 0 us
    psum x1 -> x0, waiting for transfers between devices: 123 us -> none  [local(): lax.psum(jnp.where(jnp.transpose(live_mask)[:, :, None], product, jnp.flo...]
    gather x1 -> x0, local copies, waits for them, and re-layouts: 72.8 us -> none  [local(): picked = jnp.take_along_axis(owned_rows, slot_rows[:, :, None], axis=1)]
    all_to_all x1 -> x3, waiting for transfers between devices: 77.2 us -> 41.7 us  [local(): lax.all_to_all(outgoing, 'group', split_axis=0, concat_axis=0, tiled=True)]
    all_to_all x0 -> x1, blocking collectives: none -> 32.1 us  [local(): lax.all_to_all(outgoing, 'group', split_axis=0, concat_axis=0, tiled=True)]
    ppermute x0 -> x4, waiting for transfers between devices: none -> 22.9 us  [local(): lax.ppermute(parts[step - 1], 'cuts', ring).astype(jnp.float32)]
    all_to_all x1 -> x3, starting transfers between devices: 7.54 us -> 18.7 us  [local(): lax.all_to_all(outgoing, 'group', split_axis=0, concat_axis=0, tiled=True)]
    unnamed x9 -> x30, local copies, waits for them, and re-layouts: 0.21 us -> 9.87 us
    pallas_call x0 -> x4, Pallas kernels: none -> 7.41 us  [select(): pl.pallas_call(functools.partial(select_kernel, block, share), out_shape=...]
  transfers between devices with their start and end apart: 2 -> 7, of which waited for: 2 -> 6; matrix products, arithmetic and copies ran while one was open for 0% -> 4% of each run, Pallas kernels for 0% -> 5%
where the time goes in v1:
time: 153 us; the launch traced here: 152 us
  waiting for transfers between devices  64.6 us (42%)
  blocking collectives  32.1 us (21%)
  starting transfers between devices  23.9 us (16%)
  local copies, waits for them, and re-layouts  20.9 us (14%)
  Pallas kernels  7.41 us (5%)
  other arithmetic  3.03 us (2%)
    all_to_all x3, waiting for transfers between devices, local(): lax.all_to_all(outgoing, 'group', split_axis=0, concat_axis=0, tiled=True)  41.7 us
    all_to_all x1, blocking collectives, local(): lax.all_to_all(outgoing, 'group', split_axis=0, concat_axis=0, tiled=True)  32.1 us
    ppermute x4, waiting for transfers between devices, local(): lax.ppermute(parts[step - 1], 'cuts', ring).astype(jnp.float32)  22.9 us
    all_to_all x3, starting transfers between devices, local(): lax.all_to_all(outgoing, 'group', split_axis=0, concat_axis=0, tiled=True)  18.7 us
    unnamed x30, local copies, waits for them, and re-layouts  9.87 us
    pallas_call x4, Pallas kernels, select(): pl.pallas_call(functools.partial(select_kernel, block, share), out_shape=...  7.41 us
    ppermute x4, starting transfers between devices, local(): lax.ppermute(parts[step - 1], 'cuts', ring).astype(jnp.float32)  5.2 us
    another operation x5, local copies, waits for them, and re-layouts, local(): turned[k][:, None]  4.13 us
  transfers between devices with their start and end apart: 7, of which 6 were waited for; matrix products, arithmetic and copies ran while one was open for 4% of the time, Pallas kernels for 5%

profile of v1, /device:TPU:0, one launch (start us, length us, event | category | flops | bytes accessed | tf_op | source)
XLA Modules:
  0.0 152.2 jit_solution(2409920286882408498)
XLA Ops:
  0.0 4.0 %slice_bitcast_fusion.2 = (bf16[16,64,512]{2,1,0:T(8,128)(2,1)}, bf16[16,64,512]{2,1,0:T(8,128)(2,1)}, bf16[16,64,512]{2,1,0:T(8,128)(2,1)}, bf16[16,64,512]{2,1,0:T(8,128)(2,1)S(1)}) fusion(bf16[16,4,64,512]{3,2,1,0:T(8,128)(2,1)} %bitcast.47), kind=kLoop, calls=%fused_computation.3 | loop fusion | bytes 8388608 | tf_op jit(solution)/shard_map/squeeze | solution.py:76
  4.0 32.1 %all_to_all.20 = bf16[16,64,512]{2,1,0:T(8,128)(2,1)S(1)} all-to-all(bf16[16,64,512]{2,1,0:T(8,128)(2,1)S(1)} %get-tuple-element.36), channel_id=1, replica_groups=mesh['cuts'=2,'group'=16] {'group'}, dimensions={0} | all-to-all | bytes 2097152 | tf_op jit(solution)/shard_map/all_to_all | solution.py:79
  36.1 5.0 %all-to-all-start = ((bf16[16,64,512]{2,1,0:T(8,128)(2,1)}), bf16[16,64,512]{2,1,0:T(8,128)(2,1)S(1)}, u32[]{:S(2)}, u32[]{:S(2)}) async-start(bf16[16,64,512]{2,1,0:T(8,128)(2,1)} %get-tuple-element.33), calls=%async_computation | async-start | bytes 2097152 | tf_op jit(solution)/shard_map/all_to_all | solution.py:79
  41.1 0.0 copy-done.13
  41.1 0.0 copy-done.14
  41.1 0.1 fusion.5
  41.3 1.0 copy.15.slots_ref
  42.3 0.0 copy-done.12
  42.4 0.0 copy-start.2
  42.4 0.0 copy-start.7
  42.4 1.2 copy-done.7
  43.6 1.8 %shard_map.47 = (bf16[512,512]{1,0:T(8,128)(2,1)S(1)}, bf16[512,512]{1,0:T(8,128)(2,1)S(1)}) custom-call(bf16[1024,512]{1,0:T(8,128)(2,1)S(1)} %bitcast.44, bf16[512,512]{1,0:T(8,128)(2,1)S(1)} %maximum_maximum_fusion.matrix_ref, s32[1024,1]{1,0:T(8,128)S(1)} %copy-done.7), custom_call_target="tpu_custom_call" | custom-call | flops 1610612736 | bytes 2097152 | tf_op jit(solution)/shard_map/pallas_call | solution.py:43
  45.4 0.0 copy-done.2
  45.4 0.8 copy-done.11
  46.2 17.8 %all-to-all-done = bf16[16,64,512]{2,1,0:T(8,128)(2,1)S(1)} async-done(((bf16[16,64,512]{2,1,0:T(8,128)(2,1)}), bf16[16,64,512]{2,1,0:T(8,128)(2,1)S(1)}, u32[]{:S(2)}, u32[]{:S(2)}) %all-to-all-start) | async-done | bytes 1048608 | tf_op jit(solution)/shard_map/all_to_all | solution.py:79
  64.0 6.9 %all-to-all-start.3 = ((bf16[16,64,512]{2,1,0:T(8,128)(2,1)}), bf16[16,64,512]{2,1,0:T(8,128)(2,1)S(1)}, u32[]{:S(2)}, u32[]{:S(2)}) async-start(bf16[16,64,512]{2,1,0:T(8,128)(2,1)} %get-tuple-element.30), calls=%async_computation.3 | async-start | bytes 2097152 | tf_op jit(solution)/shard_map/all_to_all | solution.py:79
  70.9 1.0 copy.12.slots_ref
  71.9 1.0 copy-done.3
  73.0 1.0 copy-done.9
  74.0 1.8 %shard_map.46 = (bf16[512,512]{1,0:T(8,128)(2,1)S(1)}, bf16[512,512]{1,0:T(8,128)(2,1)S(1)}) custom-call(bf16[1024,512]{1,0:T(8,128)(2,1)S(1)} %bitcast.43, bf16[512,512]{1,0:T(8,128)(2,1)S(1)} %copy-done.3, s32[1024,1]{1,0:T(8,128)S(1)} %copy-done.9), custom_call_target="tpu_custom_call" | custom-call | flops 1610612736 | bytes 2097152 | tf_op jit(solution)/shard_map/pallas_call | solution.py:43
  75.8 0.0 copy-start.10
  75.8 0.8 copy-done.10
  76.6 17.2 %all-to-all-done.3 = bf16[16,64,512]{2,1,0:T(8,128)(2,1)S(1)} async-done(((bf16[16,64,512]{2,1,0:T(8,128)(2,1)}), bf16[16,64,512]{2,1,0:T(8,128)(2,1)S(1)}, u32[]{:S(2)}, u32[]{:S(2)}) %all-to-all-start.3) | async-done | bytes 1048608 | tf_op jit(solution)/shard_map/all_to_all | solution.py:79
  93.9 6.9 %all-to-all-start.2 = ((bf16[16,64,512]{2,1,0:T(8,128)(2,1)}), bf16[16,64,512]{2,1,0:T(8,128)(2,1)S(1)}, u32[]{:S(2)}, u32[]{:S(2)}) async-start(bf16[16,64,512]{2,1,0:T(8,128)(2,1)} %get-tuple-element.27), calls=%async_computation.2 | async-start | bytes 2097152 | tf_op jit(solution)/shard_map/all_to_all | solution.py:79
  100.7 1.6 %collective-permute-start.1 = (bf16[512,512]{1,0:T(8,128)(2,1)}, bf16[512,512]{1,0:T(8,128)(2,1)}, u32[]{:S(2)}, u32[]{:S(2)}) collective-permute-start(bf16[512,512]{1,0:T(8,128)(2,1)} %copy-done.11), channel_id=1, source_target_pairs={{0,16},{16,0},{1,17},{17,1},{2,18},{18,2},{3,19},{19,3},{4,20},{20... | collective-permute-start | bytes 1572872 | tf_op jit(solution)/shard_map/ppermute | solution.py:86
  102.3 1.0 copy.17.slots_ref
  103.3 1.0 copy.16.slots_ref
  104.4 0.5 collective-permute-start
  104.9 1.0 copy-done.4
  105.9 1.0 copy-done.8
  107.0 2.0 %shard_map.49 = (bf16[512,512]{1,0:T(8,128)(2,1)}, bf16[512,512]{1,0:T(8,128)(2,1)S(1)}) custom-call(bf16[1024,512]{1,0:T(8,128)(2,1)S(1)} %bitcast.46, bf16[512,512]{1,0:T(8,128)(2,1)S(1)} %copy-done.4, s32[1024,1]{1,0:T(8,128)S(1)} %copy-done.8), custom_call_target="tpu_custom_call" | custom-call | flops 1610612736 | bytes 2097152 | tf_op jit(solution)/shard_map/pallas_call | solution.py:43
  109.0 0.8 copy-done
  109.8 1.5 collective-permute-start.3
  111.4 4.5 %collective-permute-done.1 = bf16[512,512]{1,0:T(8,128)(2,1)} collective-permute-done((bf16[512,512]{1,0:T(8,128)(2,1)}, bf16[512,512]{1,0:T(8,128)(2,1)}, u32[]{:S(2)}, u32[]{:S(2)}) %collective-permute-start.1) | collective-permute-done | bytes 524320 | tf_op jit(solution)/shard_map/ppermute | solution.py:86
  115.8 1.2 fusion.1
  117.0 6.6 %all-to-all-done.2 = bf16[16,64,512]{2,1,0:T(8,128)(2,1)S(1)} async-done(((bf16[16,64,512]{2,1,0:T(8,128)(2,1)}), bf16[16,64,512]{2,1,0:T(8,128)(2,1)S(1)}, u32[]{:S(2)}, u32[]{:S(2)}) %all-to-all-start.2) | async-done | bytes 1048608 | tf_op jit(solution)/shard_map/all_to_all | solution.py:79
  123.7 1.0 copy-done.5
  124.7 1.0 copy-done.6
  125.8 1.8 %shard_map.48 = (bf16[512,512]{1,0:T(8,128)(2,1)S(1)}, bf16[512,512]{1,0:T(8,128)(2,1)S(1)}) custom-call(bf16[1024,512]{1,0:T(8,128)(2,1)S(1)} %bitcast.45, bf16[512,512]{1,0:T(8,128)(2,1)S(1)} %copy-done.5, s32[1024,1]{1,0:T(8,128)S(1)} %copy-done.6), custom_call_target="tpu_custom_call" | custom-call | flops 1610612736 | bytes 2097152 | tf_op jit(solution)/shard_map/pallas_call | solution.py:43
  127.6 1.6 %collective-permute-start.2 = (bf16[512,512]{1,0:T(8,128)(2,1)S(1)}, bf16[512,512]{1,0:T(8,128)(2,1)S(1)}, u32[]{:S(2)}, u32[]{:S(2)}) collective-permute-start(bf16[512,512]{1,0:T(8,128)(2,1)S(1)} %get-tuple-element.29), channel_id=1, source_target_pairs={{0,16},{16,0},{1,17},{17,1},{2,18},{18,2},{3,19},{19,3},{4,20},{20... | collective-permute-start | bytes 1572872 | tf_op jit(solution)/shard_map/ppermute | solution.py:86
  129.1 0.0 collective-permute-done
  129.1 1.2 fusion
  130.3 7.9 %collective-permute-done.3 = bf16[512,512]{1,0:T(8,128)(2,1)S(1)} collective-permute-done((bf16[512,512]{1,0:T(8,128)(2,1)}, bf16[512,512]{1,0:T(8,128)(2,1)S(1)}, u32[]{:S(2)}, u32[]{:S(2)}) %collective-permute-start.3) | collective-permute-done | bytes 524320 | tf_op jit(solution)/shard_map/ppermute | solution.py:86
  138.2 0.1 fusion.3
  138.4 10.5 %collective-permute-done.2 = bf16[512,512]{1,0:T(8,128)(2,1)S(1)} collective-permute-done((bf16[512,512]{1,0:T(8,128)(2,1)S(1)}, bf16[512,512]{1,0:T(8,128)(2,1)S(1)}, u32[]{:S(2)}, u32[]{:S(2)}) %collective-permute-start.2) | collective-permute-done | bytes 524320 | tf_op jit(solution)/shard_map/ppermute | solution.py:86
  148.9 0.1 fusion.2
  149.0 0.3 pad_maximum_fusion
  149.3 2.9 %copy.18 = bf16[512,4,512]{2,1,0:T(4,128)(2,1)} copy(bf16[512,4,512]{2,0,1:T(8,128)(2,1)S(1)} %pad_maximum_fusion) | data formatting | bytes 4194304 | tf_op jit(solution)/shard_map/stack | solution.py:88
  (18 shorter events, 0.1 us)
Async XLA Ops:
  4.0 37.2 %copy-start.13 = (s32[4,1024]{1,0:T(4,128)S(1)}, s32[4,1024]{1,0:T(4,128)}, u32[]{:S(2)}) copy-start(s32[4,1024]{1,0:T(4,128)} %param.6) | copy-start | bytes 49156
  4.0 37.2 %copy-start.14 = (s32[4]{0:T(128)S(1)}, s32[4]{0:T(128)}, u32[]{:S(2)}) copy-start(s32[4]{0:T(128)} %param.7) | copy-start | bytes 52
  4.0 38.3 %copy-start.12 = (bf16[1,2,256,256]{3,2,1,0:T(8,128)(2,1)S(1)}, bf16[1,2,256,256]{3,2,1,0:T(8,128)(2,1)}, u32[]{:S(2)}) copy-start(bf16[1,2,256,256]{3,2,1,0:T(8,128)(2,1)} %param.5) | copy-start | bytes 786436
  36.1 27.9 %all-to-all-start = ((bf16[16,64,512]{2,1,0:T(8,128)(2,1)}), bf16[16,64,512]{2,1,0:T(8,128)(2,1)S(1)}, u32[]{:S(2)}, u32[]{:S(2)}) async-start(bf16[16,64,512]{2,1,0:T(8,128)(2,1)} %get-tuple-element.33), calls=%async_computation | async-start | bytes 2097152 | tf_op jit(solution)/shard_map/all_to_all | solution.py:79
  42.4 3.0 %copy-start.2 = (bf16[512,512]{1,0:T(8,128)(2,1)}, bf16[512,512]{1,0:T(8,128)(2,1)S(1)}, u32[]{:S(2)}) copy-start(bf16[512,512]{1,0:T(8,128)(2,1)S(1)} %maximum_maximum_fusion.matrix_ref) | copy-start | bytes 1572868
  42.4 1.2 copy-start.7
  45.4 0.8 copy-start.11
  64.0 29.8 %all-to-all-start.3 = ((bf16[16,64,512]{2,1,0:T(8,128)(2,1)}), bf16[16,64,512]{2,1,0:T(8,128)(2,1)S(1)}, u32[]{:S(2)}, u32[]{:S(2)}) async-start(bf16[16,64,512]{2,1,0:T(8,128)(2,1)} %get-tuple-element.30), calls=%async_computation.3 | async-start | bytes 2097152 | tf_op jit(solution)/shard_map/all_to_all | solution.py:79
  71.9 1.0 copy-start.3
  73.0 1.0 copy-start.9
  75.8 0.8 copy-start.10
  93.9 29.8 %all-to-all-start.2 = ((bf16[16,64,512]{2,1,0:T(8,128)(2,1)}), bf16[16,64,512]{2,1,0:T(8,128)(2,1)S(1)}, u32[]{:S(2)}, u32[]{:S(2)}) async-start(bf16[16,64,512]{2,1,0:T(8,128)(2,1)} %get-tuple-element.27), calls=%async_computation.2 | async-start | bytes 2097152 | tf_op jit(solution)/shard_map/all_to_all | solution.py:79
  100.7 15.1 %collective-permute-start.1 = (bf16[512,512]{1,0:T(8,128)(2,1)}, bf16[512,512]{1,0:T(8,128)(2,1)}, u32[]{:S(2)}, u32[]{:S(2)}) collective-permute-start(bf16[512,512]{1,0:T(8,128)(2,1)} %copy-done.11), channel_id=1, source_target_pairs={{0,16},{16,0},{1,17},{17,1},{2,18},{18,2},{3,19},{19,3},{4,20},{20... | collective-permute-start | bytes 1572872 | tf_op jit(solution)/shard_map/ppermute | solution.py:86
  104.4 24.8 %collective-permute-start = (bf16[512,512]{1,0:T(8,128)(2,1)}, bf16[512,512]{1,0:T(8,128)(2,1)}, u32[]{:S(2)}, u32[]{:S(2)}) collective-permute-start(bf16[512,512]{1,0:T(8,128)(2,1)} %copy-done.10), channel_id=1, source_target_pairs={{0,16},{16,0},{1,17},{17,1},{2,18},{18,2},{3,19},{19,3},{4,20},{20... | collective-permute-start | bytes 1572872 | tf_op jit(solution)/shard_map/ppermute | solution.py:86
  104.9 1.0 copy-start.4
  105.9 1.0 copy-start.8
  109.0 0.8 copy-start
  109.8 28.4 %collective-permute-start.3 = (bf16[512,512]{1,0:T(8,128)(2,1)}, bf16[512,512]{1,0:T(8,128)(2,1)S(1)}, u32[]{:S(2)}, u32[]{:S(2)}) collective-permute-start(bf16[512,512]{1,0:T(8,128)(2,1)} %get-tuple-element.32), channel_id=1, source_target_pairs={{0,16},{16,0},{1,17},{17,1},{2,18},{18,2},{3,19},{19,3},{4,20},{20... | collective-permute-start | bytes 1572872 | tf_op jit(solution)/shard_map/ppermute | solution.py:86
  123.7 1.0 copy-start.5
  124.7 1.0 copy-start.6
  125.8 12.5 %copy-start.1 = (bf16[512,512]{1,0:T(8,128)(2,1)S(1)}, bf16[512,512]{1,0:T(8,128)(2,1)}, u32[]{:S(2)}) copy-start(bf16[512,512]{1,0:T(8,128)(2,1)} %copy-done) | copy-start | bytes 1572868
  127.6 21.3 %collective-permute-start.2 = (bf16[512,512]{1,0:T(8,128)(2,1)S(1)}, bf16[512,512]{1,0:T(8,128)(2,1)S(1)}, u32[]{:S(2)}, u32[]{:S(2)}) collective-permute-start(bf16[512,512]{1,0:T(8,128)(2,1)S(1)} %get-tuple-element.29), channel_id=1, source_target_pairs={{0,16},{16,0},{1,17},{17,1},{2,18},{18,2},{3,19},{19,3},{4,20},{20... | collective-permute-start | bytes 1572872 | tf_op jit(solution)/shard_map/ppermute | solution.py:86

commit v2 on v1

--- a/solution.py
+++ b/solution.py
@@ -55,22 +55,11 @@
     )(rows, matrix, slots)
 
 
-def local(stem_blocks, cap_tensor, slot_rows, counts):
-    cuts, groups = lax.axis_size("cuts"), lax.axis_size("group")
-    stem = stem_blocks[0]
+def static_plan(stem, matrix, turned, cuts):
+    groups = lax.axis_size("group")
     group_total, own_rows, width = stem.shape
     mine = group_total // groups
-    slot_total = slot_rows.shape[1]
-    share = slot_total // cuts
-    matrix = build_matrix(cap_tensor[0])
-
-    positions = jnp.arange(slot_total, dtype=jnp.int32)
-    marked = jnp.where(positions[None, :] < counts[:, None], slot_rows, -1)
-    me = lax.axis_index("cuts")
-    doubled = jnp.concatenate([marked, marked], axis=1)
-    turned = lax.dynamic_slice_in_dim(doubled, (me + 1) * share, slot_total, 1)
     by_owner = stem.reshape(groups, mine, own_rows, width)
-
     sums, selected = [], []
     for k in range(mine):
         outgoing = by_owner[:, k]
@@ -88,6 +77,246 @@
     return jnp.stack(sums, axis=1)
 
 
+KINDS = 8
+LANES = 128
+
+
+def dot(a, b):
+    return jnp.dot(a, b, preferred_element_type=jnp.float32)
+
+
+def dot_nt(a, b):
+    return lax.dot_general(a, b, (((1,), (1,)), ((), ())), preferred_element_type=jnp.float32)
+
+
+def iota(shape, dim):
+    return lax.broadcasted_iota(jnp.int32, shape, dim)
+
+
+def mark(condition):
+    return jnp.where(condition, 1.0, 0.0).astype(jnp.bfloat16)
+
+
+def needs_kernel(own_rows, capacity, slots_ref, counts_ref, flags_ref):
+    mine, slot_total = slots_ref.shape
+    side = flags_ref.shape[0]
+    hits = jnp.zeros((side, LANES), jnp.float32)
+    place = iota((1, slot_total), 1)
+    down = iota((side, slot_total), 0)
+    across = iota((LANES, slot_total), 0)
+    per = LANES // own_rows
+    for k in range(mine):
+        slots = slots_ref[k : k + 1, :]
+        half = jnp.where(place >= slot_total // 2, 2, 0)
+        row_key = (slots // own_rows) * KINDS + half + k // per
+        row_key = jnp.where(place < counts_ref[k], row_key, -1)
+        lane_key = slots % own_rows + (k % per) * own_rows
+        hits = hits + dot_nt(mark(down == row_key), mark(across == lane_key))
+    flags = jnp.minimum(hits, 1.0)
+    row, column = iota((side, side), 0), iota((side, side), 1)
+    kind, back = row % KINDS, row - column
+    first = (kind == 4) & ((back == 4) | (back == 3))
+    second = (kind == 5) & ((back == 3) | (back == 2))
+    sums = dot(flags.astype(jnp.bfloat16), jnp.ones((LANES, LANES), jnp.bfloat16))
+    counted = dot(mark(first | second), sums.astype(jnp.bfloat16))
+    kind = iota((side, LANES), 0) % KINDS
+    room = jnp.where(kind == 4, 2.0 * capacity, 1.0 * capacity)
+    spill = jnp.max(jnp.where((kind == 4) | (kind == 5), counted - room, 0.0))
+    flags_ref[...] = jnp.where(kind == 6, jnp.where(spill > 0.0, 1.0, 0.0), flags)
+
+
+def needs(slot_rows, counts, own_rows, capacity, groups):
+    return pl.pallas_call(
+        functools.partial(needs_kernel, own_rows, capacity),
+        out_shape=jax.ShapeDtypeStruct((groups * KINDS, LANES), jnp.float32),
+        in_specs=[pl.BlockSpec(memory_space=pltpu.VMEM), pl.BlockSpec(memory_space=pltpu.SMEM)],
+        out_specs=pl.BlockSpec(memory_space=pltpu.VMEM),
+        cost_estimate=pl.CostEstimate(flops=1 << 28, bytes_accessed=1 << 17, transcendentals=0),
+    )(slot_rows, counts)
+
+
+def keys_of(flags):
+    side = flags.shape[0]
+    marks = flags.astype(jnp.bfloat16)
+    lower = mark(iota((LANES, LANES), 0) < iota((LANES, LANES), 1))
+    inside = dot(marks, lower)
+    totals = dot(marks, jnp.ones((LANES, LANES), jnp.bfloat16))
+    row, column = iota((side, side), 0), iota((side, side), 1)
+    follows = ((row % KINDS == 1) | (row % KINDS == 3)) & (row - column == 1)
+    ranks = inside + dot(mark(follows), totals.astype(jnp.bfloat16))
+    return jnp.where(flags > 0.0, ranks, -1.0)
+
+
+def pack_kernel(capacity, plans, batch, plane_ref, flags_ref, stem_ref, matrix_ref, *refs):
+    outs, keys_ref, picked = refs[: len(plans)], refs[-2], refs[-1]
+    step = pl.program_id(0)
+
+    @pl.when(step == 0)
+    def _():
+        keys_ref[...] = keys_of(flags_ref[...])
+
+    plane = plane_ref[0]
+    rank = iota((capacity, LANES), 0).astype(jnp.float32)
+    for out, plan in zip(outs, plans):
+        for i in range(batch):
+            keys = keys_ref[pl.ds((step * batch + i) * KINDS, KINDS), :]
+            if plan == "early":
+                upper, lower = keys[0:1], keys[1:2]
+            else:
+                second = plane == (0 if plan == "send" else 1)
+                upper = jnp.where(second, keys[2:3], keys[0:1] - capacity)
+                lower = jnp.where(second, keys[3:4], keys[1:2] - capacity)
+            chosen = jnp.concatenate([mark(rank == upper), mark(rank == lower)], axis=1)
+            rows = stem_ref[i]
+            picked[pl.ds(i * capacity, capacity), :] = dot(chosen, rows).astype(picked.dtype)
+        terms = dot(picked[...], matrix_ref[...]).astype(out.dtype)
+        out[...] = terms.reshape(out.shape)
+
+
+def pack(plans, plane, flags, stem, matrix, capacity):
+    groups, rows, width = stem.shape
+    batch = 4 if groups % 4 == 0 else 1
+    out = jax.ShapeDtypeStruct((groups, capacity, matrix.shape[1]), stem.dtype)
+    whole = lambda a: pl.BlockSpec(a.shape, lambda i: (0, 0))
+    return pl.pallas_call(
+        functools.partial(pack_kernel, capacity, plans, batch),
+        grid=(groups // batch,),
+        out_shape=[out] * len(plans),
+        in_specs=[
+            pl.BlockSpec(memory_space=pltpu.SMEM),
+            whole(flags),
+            pl.BlockSpec((batch, rows, width), lambda i: (i, 0, 0)),
+            whole(matrix),
+        ],
+        out_specs=[pl.BlockSpec((batch, capacity, matrix.shape[1]), lambda i: (i, 0, 0))] * len(plans),
+        scratch_shapes=[
+            pltpu.VMEM(flags.shape, jnp.float32),
+            pltpu.VMEM((batch * capacity, width), stem.dtype),
+        ],
+        cost_estimate=pl.CostEstimate(
+            flops=len(plans) * 2 * groups * capacity * (rows + width) * width,
+            bytes_accessed=2 * stem.size,
+            transcendentals=0,
+        ),
+        compiler_params=pltpu.CompilerParams(vmem_limit_bytes=24 << 20),
+    )(plane, flags, stem, matrix)
+
+
+def places_kernel(own_rows, capacity, plane_ref, slots_ref, places_ref):
+    mine, share = slots_ref.shape
+    rows = mine * own_rows
+    down = iota((own_rows, share), 0)
+    across = iota((LANES, share), 0)
+    wanted = []
+    for k in range(mine):
+        slots = slots_ref[k : k + 1, :]
+        source = jnp.where(slots >= 0, slots // own_rows, -1)
+        wanted.append(dot_nt(mark(down == slots % own_rows), mark(across == source)))
+    wanted = jnp.minimum(jnp.concatenate(wanted, axis=0), 1.0)
+    before = mark(iota((rows, rows), 0) > iota((rows, rows), 1))
+    ranks = dot(before, wanted.astype(jnp.bfloat16))
+    shift = (plane_ref[0] * capacity).astype(jnp.float32)
+    places_ref[...] = jnp.where(wanted > 0.0, ranks + shift, -1.0)
+
+
+def places(plane, own_slots, own_rows, capacity):
+    return pl.pallas_call(
+        functools.partial(places_kernel, own_rows, capacity),
+        out_shape=jax.ShapeDtypeStruct((own_slots.shape[0] * own_rows, LANES), jnp.float32),
+        in_specs=[pl.BlockSpec(memory_space=pltpu.SMEM), pl.BlockSpec(memory_space=pltpu.VMEM)],
+        out_specs=pl.BlockSpec(memory_space=pltpu.VMEM),
+        cost_estimate=pl.CostEstimate(flops=1 << 28, bytes_accessed=1 << 17, transcendentals=0),
+    )(plane, own_slots)
+
+
+def spread_kernel(own_rows, places_ref, slots_ref, early_ref, late_ref, out_ref, table):
+    groups, capacity, width = early_ref.shape
+    mine, row_total, _ = table.shape
+    share = slots_ref.shape[0] // mine
+    rank = iota((mine * own_rows, 2 * capacity), 1).astype(jnp.float32)
+    for s in range(groups):
+        chosen = mark(rank == places_ref[:, s : s + 1])
+        rows = dot(chosen[:, :capacity], early_ref[s]) + dot(chosen[:, capacity:], late_ref[s])
+        table[:, s * own_rows : (s + 1) * own_rows, :] = rows.astype(table.dtype).reshape(mine, own_rows, width)
+    block = min(256, share)
+    columns = iota((block, row_total), 1)
+    for k in range(mine):
+        for start in range(0, share, block):
+            chosen = mark(columns == slots_ref[pl.ds(k * share + start, block), :])
+            out_ref[k, pl.ds(start, block), :] = dot(chosen, table[k]).astype(out_ref.dtype)
+
+
+def spread(where, slots, early, late, own_rows):
+    groups, capacity, width = early.shape
+    mine = where.shape[0] // own_rows
+    share = slots.shape[0] // mine
+    return pl.pallas_call(
+        functools.partial(spread_kernel, own_rows),
+        out_shape=jax.ShapeDtypeStruct((mine, share, width), early.dtype),
+        in_specs=[pl.BlockSpec(memory_space=pltpu.VMEM)] * 4,
+        out_specs=pl.BlockSpec(memory_space=pltpu.VMEM),
+        scratch_shapes=[pltpu.VMEM((mine, groups * own_rows, width), early.dtype)],
+        cost_estimate=pl.CostEstimate(
+            flops=4 * mine * share * groups * own_rows * width,
+            bytes_accessed=4 * early.size,
+            transcendentals=0,
+        ),
+        compiler_params=pltpu.CompilerParams(vmem_limit_bytes=32 << 20),
+    )(where, slots, early, late)
+
+
+def exchange(blocks):
+    return lax.all_to_all(blocks, "group", split_axis=0, concat_axis=0, tiled=True)
+
+
+def needed_plan(stem, matrix, flags, own_slots, capacity):
+    groups = lax.axis_size("group")
+    group_total, own_rows, width = stem.shape
+    mine = group_total // groups
+    plane = lax.axis_index("cuts").astype(jnp.int32)[None]
+    by_owner = stem.reshape(groups, mine * own_rows, width)
+    (early,) = pack(("early",), plane, flags, by_owner, matrix, capacity)
+    send, keep = pack(("send", "keep"), plane, flags, by_owner, matrix, capacity)
+    where = places(plane, own_slots, own_rows, capacity)
+    columns = own_slots.reshape(-1, 1)
+
+    early = exchange(early)
+    late = keep.astype(jnp.float32) + lax.ppermute(send, "cuts", [(0, 1), (1, 0)]).astype(jnp.float32)
+    late = exchange(late.astype(stem.dtype))
+    early = early.astype(jnp.float32) + lax.ppermute(early, "cuts", [(1, 0)]).astype(jnp.float32)
+    out = spread(where, columns, early.astype(stem.dtype), late, own_rows)
+    return jnp.transpose(out, (1, 0, 2))
+
+
+def local(stem_blocks, cap_tensor, slot_rows, counts):
+    cuts, groups = lax.axis_size("cuts"), lax.axis_size("group")
+    stem = stem_blocks[0]
+    group_total, own_rows, width = stem.shape
+    mine = group_total // groups
+    slot_total = slot_rows.shape[1]
+    share = slot_total // cuts
+    matrix = build_matrix(cap_tensor[0])
+
+    positions = jnp.arange(slot_total, dtype=jnp.int32)
+    marked = jnp.where(positions[None, :] < counts[:, None], slot_rows, -1)
+    me = lax.axis_index("cuts")
+    doubled = jnp.concatenate([marked, marked], axis=1)
+    turned = lax.dynamic_slice_in_dim(doubled, (me + 1) * share, slot_total, 1)
+
+    if cuts != 2 or mine * own_rows != 2 * LANES or LANES % own_rows or groups > LANES:
+        return static_plan(stem, matrix, turned, cuts)
+    capacity = mine * own_rows // 4
+    flags = needs(slot_rows, counts, own_rows, capacity, groups)
+    flags = exchange(flags.reshape(groups, KINDS, LANES))
+    spilled = jnp.max(flags[:, 6, :]) > 0.0
+    flags = flags.reshape(groups * KINDS, LANES)
+    return lax.cond(
+        spilled,
+        lambda: static_plan(stem, matrix, turned, cuts),
+        lambda: needed_plan(stem, matrix, flags, turned[:, (cuts - 1) * share :], capacity),
+    )
+
+
 def solution(mesh):
     in_specs = (
         P("cuts", None, "group", None),

time: 153 us -> 103 us (0.67)
  blocking collectives: 32.1 us -> 0 us
  local copies, waits for them, and re-layouts: 20.9 us -> 4.9 us
  waiting for transfers between devices: 64.6 us -> 51.2 us
  Pallas kernels: 7.41 us -> 20.3 us
  starting transfers between devices: 23.9 us -> 19.7 us
  other arithmetic: 3.03 us -> 5.57 us
    all_to_all x3, waiting for transfers between devices: 41.7 us -> 4.1 us  [exchange(): lax.all_to_all(blocks, 'group', split_axis=0, concat_axis=0, tiled=True)]
    all_to_all x1 -> x0, blocking collectives: 32.1 us -> none  [local(): lax.all_to_all(outgoing, 'group', split_axis=0, concat_axis=0, tiled=True)]
    ppermute x4 -> x2, waiting for transfers between devices: 22.9 us -> 47.1 us  [the longest x1 23.8 us: needed_plan(): lax.ppermute(send, 'cuts', [(0, 1), (1, 0)]).astype(jnp.float32)]
    pallas_call x4 -> x5, Pallas kernels: 7.41 us -> 20.3 us  [the longest x2 10.6 us: pack(): pl.pallas_call(functools.partial(pack_kernel, capacity, plans, batch), gr...]
    unnamed x30 -> x0, local copies, waits for them, and re-layouts: 9.87 us -> none
    another operation x6 -> x0, local copies, waits for them, and re-layouts: 7.07 us -> none  [the longest x5 4.13 us: local(): turned[k][:, None]]
    squeeze x1 -> x0, local copies, waits for them, and re-layouts: 3.95 us -> none  [local(): outgoing = by_owner[:, k]]
    cond x0 -> x8, local copies, waits for them, and re-layouts: none -> 3.92 us
  transfers between devices with their start and end apart: 7 -> 5, of which waited for: 6 -> 3; matrix products, arithmetic and copies ran while one was open for 4% -> 7% of each run, Pallas kernels for 5% -> 7%
where the time goes in v2:
time: 103 us; the launch traced here: 102 us
  waiting for transfers between devices  51.2 us (50%)
  Pallas kernels  20.3 us (20%)
  starting transfers between devices  19.7 us (19%)
  other arithmetic  5.57 us (5%)
  local copies, waits for them, and re-layouts  4.9 us (5%)
    ppermute x1, waiting for transfers between devices, needed_plan(): lax.ppermute(send, 'cuts', [(0, 1), (1, 0)]).astype(jnp.float32)  23.8 us
    ppermute x1, waiting for transfers between devices, needed_plan(): lax.ppermute(early, 'cuts', [(1, 0)]).astype(jnp.float32)  23.3 us
    all_to_all x3, starting transfers between devices, exchange(): lax.all_to_all(blocks, 'group', split_axis=0, concat_axis=0, tiled=True)  16.8 us
    pallas_call x2, Pallas kernels, pack(): pl.pallas_call(functools.partial(pack_kernel, capacity, plans, batch), gr...  10.6 us
    pallas_call x1, Pallas kernels, spread(): pl.pallas_call(functools.partial(spread_kernel, own_rows), out_shape=jax....  5.41 us
    all_to_all x3, waiting for transfers between devices, exchange(): lax.all_to_all(blocks, 'group', split_axis=0, concat_axis=0, tiled=True)  4.1 us
    cond x8, local copies, waits for them, and re-layouts  3.92 us
    pallas_call x1, Pallas kernels, needs(): pl.pallas_call(functools.partial(needs_kernel, own_rows, capacity), out_s...  2.35 us
  transfers between devices with their start and end apart: 5, of which 3 were waited for; matrix products, arithmetic and copies ran while one was open for 7% of the time, Pallas kernels for 7%

profile of v2, /device:TPU:0, one launch (start us, length us, event | category | flops | bytes accessed | tf_op | source)
XLA Modules:
  0.0 102.5 jit_solution(13414045508223527753)
XLA Ops:
  0.0 2.3 %shard_map.48 = f32[128,128]{1,0:T(8,128)} custom-call(s32[4,1024]{1,0:T(4,128)} %slots_ref.1, s32[4]{0:T(128)} %counts_ref.1), custom_call_target="tpu_custom_call" | custom-call | flops 268435456 | bytes 131072 | tf_op jit(solution)/shard_map/pallas_call | solution.py:129
  2.4 7.4 %all-to-all-start.6 = ((f32[16,8,128]{2,1,0:T(8,128)}), f32[16,8,128]{2,1,0:T(8,128)S(1)}, u32[]{:S(2)}, u32[]{:S(2)}) async-start(f32[16,8,128]{2,1,0:T(8,128)} %bitcast.64), calls=%async_computation.6 | async-start | bytes 131072 | tf_op jit(solution)/shard_map/all_to_all | solution.py:269
  9.7 0.8 fusion.5
  10.5 1.0 slice_bitcast_fusion.9
  11.5 0.9 fusion.6
  12.5 4.1 %all-to-all-done.6 = f32[16,8,128]{2,1,0:T(8,128)S(1)} async-done(((f32[16,8,128]{2,1,0:T(8,128)}), f32[16,8,128]{2,1,0:T(8,128)S(1)}, u32[]{:S(2)}, u32[]{:S(2)}) %all-to-all-start.6) | async-done | bytes 65568 | tf_op jit(solution)/shard_map/all_to_all | solution.py:269
  16.6 0.6 slice_reduce_fusion
  17.9 84.6 %conditional.1 = (bf16[512,4,512]{2,1,0:T(4,128)(2,1)}) conditional(s32[]{:T(128)} %convert_element_type.57, (s32[4,1024]{1,0:T(4,128)S(1)}, f32[16,8,128]{2,1,0:T(8,128)S(1)}, bf16[1,64,64,512]{3,2,1,0:T(8,128)(2,1)}, bf16[512,512]{1,0:T(8,128)(2,1)S(1)}) %tuple.13, (bf16[1,64,64,512]{3,2,1,0:T(8,128)(2,1)}, s32[4,1024]{1,0:T(4,128)S(1)}, ...), branch_computations={%region_1.2_spmd, %region_2.3_spmd} | conditional | flops 6983516160 | bytes 64078340 | solution.py:313
  17.9 5.2 %branch_0_fun.5 = bf16[16,64,512]{2,1,0:T(8,128)(2,1)} custom-call(s32[1]{0:T(128)} %bitcast.plane_ref, f32[128,128]{1,0:T(8,128)S(1)} %bitcast.62, bf16[16,256,512]{2,1,0:T(8,128)(2,1)} %bitcast.59, bf16[512,512]{1,0:T(8,128)(2,1)S(1)} %get-tuple-element.26.matrix_ref), custom_call_target="tpu_custom_call" | custom-call | flops 805306368 | bytes 4194304 | tf_op jit(solution)/shard_map/cond/branch_0_fun/pallas_call | solution.py:181
  23.1 3.7 %all-to-all-start = ((bf16[16,64,512]{2,1,0:T(8,128)(2,1)}), bf16[16,64,512]{2,1,0:T(8,128)(2,1)S(1)}, u32[]{:S(2)}, u32[]{:S(2)}) async-start(bf16[16,64,512]{2,1,0:T(8,128)(2,1)} %branch_0_fun.5), calls=%async_computation | async-start | bytes 2097152 | tf_op jit(solution)/shard_map/cond/branch_0_fun/all_to_all | solution.py:269
  26.8 5.4 %branch_0_fun.6 = (bf16[16,64,512]{2,1,0:T(8,128)(2,1)S(1)}, bf16[16,64,512]{2,1,0:T(8,128)(2,1)S(1)}) custom-call(s32[1]{0:T(128)} %bitcast.plane_ref, f32[128,128]{1,0:T(8,128)S(1)} %bitcast.63, bf16[16,256,512]{2,1,0:T(8,128)(2,1)} %bitcast.60, bf16[512,512]{1,0:T(8,128)(2,1)S(1)} %get-tuple-element.26.matrix_ref), custom_call_target="tpu_custom_call" | custom-call | flops 1610612736 | bytes 4194304 | tf_op jit(solution)/shard_map/cond/branch_0_fun/pallas_call | solution.py:181
  32.2 1.6 %collective-permute-start.1 = (bf16[16,64,512]{2,1,0:T(8,128)(2,1)S(1)}, bf16[16,64,512]{2,1,0:T(8,128)(2,1)S(1)}, u32[]{:S(2)}, u32[]{:S(2)}) collective-permute-start(bf16[16,64,512]{2,1,0:T(8,128)(2,1)S(1)} %get-tuple-element.28), channel_id=1, source_target_pairs={{0,16},{16,0},{1,17},{17,1},{2,18},{18,2},{3,19},{19,3},{4,20},{20... | collective-permute-start | bytes 3145736 | tf_op jit(solution)/shard_map/cond/branch_0_fun/ppermute | solution.py:284
  33.8 23.8 %collective-permute-done.1 = bf16[16,64,512]{2,1,0:T(8,128)(2,1)S(1)} collective-permute-done((bf16[16,64,512]{2,1,0:T(8,128)(2,1)S(1)}, bf16[16,64,512]{2,1,0:T(8,128)(2,1)S(1)}, u32[]{:S(2)}, u32[]{:S(2)}) %collective-permute-start.1) | collective-permute-done | bytes 1048608 | tf_op jit(solution)/shard_map/cond/branch_0_fun/ppermute | solution.py:284
  57.6 1.3 %add_convert_fusion = bf16[16,64,512]{2,1,0:T(8,128)(2,1)} fusion(bf16[16,64,512]{2,1,0:T(8,128)(2,1)S(1)} %collective-permute-done.1, bf16[16,64,512]{2,1,0:T(8,128)(2,1)S(1)} %get-tuple-element.27), kind=kLoop, calls=%fused_computation | loop fusion | flops 2097152 | bytes 3145728 | tf_op jit(solution)/shard_map/cond/branch_0_fun/convert_element_type | solution.py:285
  58.9 0.0 all-to-all-done
  58.9 0.0 copy-start.8
  58.9 5.8 %all-to-all-start.1 = ((bf16[16,64,512]{2,1,0:T(8,128)(2,1)}), bf16[16,64,512]{2,1,0:T(8,128)(2,1)S(1)}, u32[]{:S(2)}, u32[]{:S(2)}) async-start(bf16[16,64,512]{2,1,0:T(8,128)(2,1)} %add_convert_fusion), calls=%async_computation.1 | async-start | bytes 2097152 | tf_op jit(solution)/shard_map/cond/branch_0_fun/all_to_all | solution.py:269
  64.7 1.3 %collective-permute-start = (bf16[16,64,512]{2,1,0:T(8,128)(2,1)S(1)}, bf16[16,64,512]{2,1,0:T(8,128)(2,1)}, u32[]{:S(2)}, u32[]{:S(2)}) collective-permute-start(bf16[16,64,512]{2,1,0:T(8,128)(2,1)S(1)} %all-to-all-done), channel_id=1, source_target_pairs={{16,0},{17,1},{18,2},{19,3},{20,4},{21,5},{22,6},{23,7},{24,8},{25... | collective-permute-start | bytes 3145736 | tf_op jit(solution)/shard_map/cond/branch_0_fun/ppermute | solution.py:286
  66.0 0.6 slice_bitcast_fusion
  66.6 0.4 copy.29
  67.0 1.9 %branch_0_fun.4.places_ref = f32[256,128]{1,0:T(8,128)} custom-call(s32[1]{0:T(128)} %bitcast.plane_ref, s32[4,512]{1,0:T(4,128)} %get-tuple-element.49.slots_ref), custom_call_target="tpu_custom_call" | custom-call | flops 268435456 | bytes 131072 | tf_op jit(solution)/shard_map/cond/branch_0_fun/pallas_call | solution.py:223
  68.9 0.0 copy-done.8
  68.9 0.0 copy-start.7
  68.9 23.3 %collective-permute-done = bf16[16,64,512]{2,1,0:T(8,128)(2,1)} collective-permute-done((bf16[16,64,512]{2,1,0:T(8,128)(2,1)S(1)}, bf16[16,64,512]{2,1,0:T(8,128)(2,1)}, u32[]{:S(2)}, u32[]{:S(2)}) %collective-permute-start) | collective-permute-done | bytes 1048608 | tf_op jit(solution)/shard_map/cond/branch_0_fun/ppermute | solution.py:286
  92.2 1.9 %add_convert_fusion.1.early_ref = bf16[16,64,512]{2,1,0:T(8,128)(2,1)S(1)} fusion(bf16[16,64,512]{2,1,0:T(8,128)(2,1)} %collective-permute-done, bf16[16,64,512]{2,1,0:T(8,128)(2,1)} %copy-done.8), kind=kLoop, calls=%fused_computation.1 | loop fusion | flops 2097152 | bytes 3145728 | tf_op jit(solution)/shard_map/cond/branch_0_fun/convert_element_type | solution.py:287
  94.1 0.0 all-to-all-done.1.late_ref
  94.1 0.0 copy-done.7
  94.1 5.4 %branch_0_fun.7 = bf16[4,512,512]{2,1,0:T(8,128)(2,1)S(1)} custom-call(f32[256,128]{1,0:T(8,128)S(1)} %copy-done.7, s32[2048,1]{1,0:T(8,128)S(1)} %bitcast.57, bf16[16,64,512]{2,1,0:T(8,128)(2,1)S(1)} %add_convert_fusion.1.early_ref, bf16[16,64,512]{2,1,0:T(8,128)(2,1)S(1)} %all-to-all-done.1.late_ref), custom_call_target="tpu_custom_call" | custom-call | flops 4294967296 | bytes 2097152 | tf_op jit(solution)/shard_map/cond/branch_0_fun/pallas_call | solution.py:253
  99.5 2.9 %copy.22 = bf16[512,4,512]{2,1,0:T(4,128)(2,1)} copy(bf16[512,4,512]{2,0,1:T(8,128)(2,1)S(1)} %bitcast.53) | data formatting | bytes 4194304 | tf_op jit(solution)/shard_map/cond
  (3 shorter events, 0.1 us)
Async XLA Ops:
  2.4 14.3 %all-to-all-start.6 = ((f32[16,8,128]{2,1,0:T(8,128)}), f32[16,8,128]{2,1,0:T(8,128)S(1)}, u32[]{:S(2)}, u32[]{:S(2)}) async-start(f32[16,8,128]{2,1,0:T(8,128)} %bitcast.64), calls=%async_computation.6 | async-start | bytes 131072 | tf_op jit(solution)/shard_map/all_to_all | solution.py:269
  23.1 35.8 %all-to-all-start = ((bf16[16,64,512]{2,1,0:T(8,128)(2,1)}), bf16[16,64,512]{2,1,0:T(8,128)(2,1)S(1)}, u32[]{:S(2)}, u32[]{:S(2)}) async-start(bf16[16,64,512]{2,1,0:T(8,128)(2,1)} %branch_0_fun.5), calls=%async_computation | async-start | bytes 2097152 | tf_op jit(solution)/shard_map/cond/branch_0_fun/all_to_all | solution.py:269
  32.2 25.4 %collective-permute-start.1 = (bf16[16,64,512]{2,1,0:T(8,128)(2,1)S(1)}, bf16[16,64,512]{2,1,0:T(8,128)(2,1)S(1)}, u32[]{:S(2)}, u32[]{:S(2)}) collective-permute-start(bf16[16,64,512]{2,1,0:T(8,128)(2,1)S(1)} %get-tuple-element.28), channel_id=1, source_target_pairs={{0,16},{16,0},{1,17},{17,1},{2,18},{18,2},{3,19},{19,3},{4,20},{20... | collective-permute-start | bytes 3145736 | tf_op jit(solution)/shard_map/cond/branch_0_fun/ppermute | solution.py:284
  58.9 10.0 %copy-start.8 = (bf16[16,64,512]{2,1,0:T(8,128)(2,1)}, bf16[16,64,512]{2,1,0:T(8,128)(2,1)S(1)}, u32[]{:S(2)}) copy-start(bf16[16,64,512]{2,1,0:T(8,128)(2,1)S(1)} %all-to-all-done) | copy-start | bytes 3145732 | tf_op jit(solution)/shard_map/cond
  58.9 35.2 %all-to-all-start.1 = ((bf16[16,64,512]{2,1,0:T(8,128)(2,1)}), bf16[16,64,512]{2,1,0:T(8,128)(2,1)S(1)}, u32[]{:S(2)}, u32[]{:S(2)}) async-start(bf16[16,64,512]{2,1,0:T(8,128)(2,1)} %add_convert_fusion), calls=%async_computation.1 | async-start | bytes 2097152 | tf_op jit(solution)/shard_map/cond/branch_0_fun/all_to_all | solution.py:269
  64.7 27.5 %collective-permute-start = (bf16[16,64,512]{2,1,0:T(8,128)(2,1)S(1)}, bf16[16,64,512]{2,1,0:T(8,128)(2,1)}, u32[]{:S(2)}, u32[]{:S(2)}) collective-permute-start(bf16[16,64,512]{2,1,0:T(8,128)(2,1)S(1)} %all-to-all-done), channel_id=1, source_target_pairs={{16,0},{17,1},{18,2},{19,3},{20,4},{21,5},{22,6},{23,7},{24,8},{25... | collective-permute-start | bytes 3145736 | tf_op jit(solution)/shard_map/cond/branch_0_fun/ppermute | solution.py:286
  68.9 25.2 %copy-start.7 = (f32[256,128]{1,0:T(8,128)S(1)}, f32[256,128]{1,0:T(8,128)}, u32[]{:S(2)}) copy-start(f32[256,128]{1,0:T(8,128)} %branch_0_fun.4.places_ref) | copy-start | bytes 393220 | tf_op jit(solution)/shard_map/cond

commit v3 on v2

v3 whole, which is shorter than its diff:
```python
import functools

import jax
import jax.numpy as jnp
from jax import lax
from jax.experimental import pallas as pl
from jax.experimental.pallas import tpu as pltpu
from jax.sharding import PartitionSpec as P


def build_matrix(cap_pair):
    real_part = cap_pair[0]
    imag_part = cap_pair[1]
    upper = jnp.concatenate([real_part, imag_part], axis=1)
    lower = jnp.concatenate([-imag_part, real_part], axis=1)
    return jnp.concatenate([upper, lower], axis=0)


def terms_kernel(rows_ref, matrix_ref, out_ref):
    out_ref[...] = dot(rows_ref[...], matrix_ref[...]).astype(out_ref.dtype)


def terms_of(rows, matrix):
    total, width = rows.shape
    block = min(1024, total)
    return pl.pallas_call(
        terms_kernel,
        grid=(total // block,),
        out_shape=jax.ShapeDtypeStruct((total, matrix.shape[1]), rows.dtype),
        in_specs=[pl.BlockSpec((block, width), lambda i: (i, 0)), pl.BlockSpec(matrix.shape, lambda i: (0, 0))],
        out_specs=pl.BlockSpec((block, matrix.shape[1]), lambda i: (i, 0)),
        cost_estimate=pl.CostEstimate(
            flops=2 * total * width * matrix.shape[1], bytes_accessed=4 * rows.size, transcendentals=0
        ),
    )(rows, matrix)


def select_kernel(block, share, terms_ref, slots_ref, *outs):
    columns = iota((block, terms_ref.shape[0]), 1)
    for part, out in enumerate(outs):
        for start in range(0, share, block):
            chosen = mark(columns == slots_ref[pl.ds(part * share + start, block), :])
            out[pl.ds(start, block), :] = dot(chosen, terms_ref[...]).astype(out.dtype)


def select(terms, slots, parts):
    row_total, width = terms.shape
    slot_total = slots.shape[0]
    share = slot_total // parts
    return pl.pallas_call(
        functools.partial(select_kernel, min(256, share), share),
        out_shape=[jax.ShapeDtypeStruct((share, width), terms.dtype)] * parts,
        in_specs=[pl.BlockSpec(memory_space=pltpu.VMEM)] * 2,
        out_specs=[pl.BlockSpec(memory_space=pltpu.VMEM)] * parts,
        cost_estimate=pl.CostEstimate(
            flops=2 * row_total * width * slot_total,
            bytes_accessed=2 * (terms.size + slot_total * width),
            transcendentals=0,
        ),
        compiler_params=pltpu.CompilerParams(vmem_limit_bytes=24 << 20),
    )(terms, slots)


def static_plan(terms, turned, cuts):
    groups = lax.axis_size("group")
    group_total, own_rows, width = terms.shape
    mine = group_total // groups
    by_owner = terms.reshape(groups, mine, own_rows, width)
    sums, selected = [], []
    for k in range(mine):
        outgoing = by_owner[:, k]
        if k >= 2:
            outgoing, selected[k - 2] = lax.optimization_barrier((outgoing, selected[k - 2]))
        got = lax.all_to_all(outgoing, "group", split_axis=0, concat_axis=0, tiled=True)
        parts = select(got.reshape(groups * own_rows, width), turned[k][:, None], cuts)
        selected.append(parts)
    for parts in selected:
        total = parts[-1].astype(jnp.float32)
        for step in range(1, cuts):
            ring = [(i, (i + step) % cuts) for i in range(cuts)]
            total = total + lax.ppermute(parts[step - 1], "cuts", ring).astype(jnp.float32)
        sums.append(total.astype(terms.dtype))
    return jnp.stack(sums, axis=1)


KINDS = 8
LANES = 128


def dot(a, b):
    return jnp.dot(a, b, preferred_element_type=jnp.float32)


def dot_nt(a, b):
    return lax.dot_general(a, b, (((1,), (1,)), ((), ())), preferred_element_type=jnp.float32)


def iota(shape, dim):
    return lax.broadcasted_iota(jnp.int32, shape, dim)


def mark(condition):
    return jnp.where(condition, 1.0, 0.0).astype(jnp.bfloat16)


def needs_kernel(own_rows, capacity, slots_ref, counts_ref, flags_ref):
    mine, slot_total = slots_ref.shape
    side = flags_ref.shape[0]
    hits = jnp.zeros((side, LANES), jnp.float32)
    place = iota((1, slot_total), 1)
    down = iota((side, slot_total), 0)
    across = iota((LANES, slot_total), 0)
    per = LANES // own_rows
    for k in range(mine):
        slots = slots_ref[k : k + 1, :]
        half = jnp.where(place >= slot_total // 2, 2, 0)
        row_key = (slots // own_rows) * KINDS + half + k // per
        row_key = jnp.where(place < counts_ref[k], row_key, -1)
        lane_key = slots % own_rows + (k % per) * own_rows
        hits = hits + dot_nt(mark(down == row_key), mark(across == lane_key))
    flags = jnp.minimum(hits, 1.0)
    row, column = iota((side, side), 0), iota((side, side), 1)
    kind, back = row % KINDS, row - column
    first = (kind == 4) & ((back == 4) | (back == 3))
    second = (kind == 5) & ((back == 3) | (back == 2))
    sums = dot(flags.astype(jnp.bfloat16), jnp.ones((LANES, LANES), jnp.bfloat16))
    counted = dot(mark(first | second), sums.astype(jnp.bfloat16))
    kind = iota((side, LANES), 0) % KINDS
    room = jnp.where(kind == 4, 2.0 * capacity, 1.0 * capacity)
    spill = jnp.max(jnp.where((kind == 4) | (kind == 5), counted - room, 0.0))
    flags_ref[...] = jnp.where(kind == 6, jnp.where(spill > 0.0, 1.0, 0.0), flags).astype(flags_ref.dtype)


def needs(slot_rows, counts, own_rows, capacity, groups):
    return pl.pallas_call(
        functools.partial(needs_kernel, own_rows, capacity),
        out_shape=jax.ShapeDtypeStruct((groups * KINDS, LANES), jnp.bfloat16),
        in_specs=[pl.BlockSpec(memory_space=pltpu.VMEM), pl.BlockSpec(memory_space=pltpu.SMEM)],
        out_specs=pl.BlockSpec(memory_space=pltpu.VMEM),
        cost_estimate=pl.CostEstimate(flops=1 << 28, bytes_accessed=1 << 17, transcendentals=0),
    )(slot_rows, counts)


def keys_of(flags):
    side = flags.shape[0]
    marks = flags
    lower = mark(iota((LANES, LANES), 0) < iota((LANES, LANES), 1))
    inside = dot(marks, lower)
    totals = dot(marks, jnp.ones((LANES, LANES), jnp.bfloat16))
    row, column = iota((side, side), 0), iota((side, side), 1)
    follows = ((row % KINDS == 1) | (row % KINDS == 3)) & (row - column == 1)
    ranks = inside + dot(mark(follows), totals.astype(jnp.bfloat16))
    return jnp.where(flags.astype(jnp.float32) > 0.0, ranks, -1.0)


def pack_kernel(plane_ref, flags_ref, terms_ref, early_ref, send_ref, keep_ref, keys_ref):
    groups, capacity, _ = early_ref.shape
    keys_ref[...] = keys_of(flags_ref[...])
    rank = iota((capacity, LANES), 0).astype(jnp.float32)

    def one(upper, lower):
        return jnp.concatenate([mark(rank == upper), mark(rank == lower)], axis=1)

    plane = plane_ref[0]
    for d in range(groups):
        keys = keys_ref[d * KINDS : (d + 1) * KINDS, :]
        first, second = (keys[0:1], keys[1:2]), (keys[2:3], keys[3:4])
        beyond = tuple(key - capacity for key in first)
        sent = [jnp.where(plane == 0, b, a) for a, b in zip(beyond, second)]
        kept = [jnp.where(plane == 0, a, b) for a, b in zip(beyond, second)]
        chosen = jnp.concatenate([one(*first), one(*sent), one(*kept)], axis=0)
        packed = dot(chosen, terms_ref[d]).astype(early_ref.dtype)
        early_ref[d] = packed[:capacity]
        send_ref[d] = packed[capacity : 2 * capacity]
        keep_ref[d] = packed[2 * capacity :]


def pack(plane, flags, terms, capacity):
    groups, rows, width = terms.shape
    vmem = pl.BlockSpec(memory_space=pltpu.VMEM)
    return pl.pallas_call(
        pack_kernel,
        out_shape=[jax.ShapeDtypeStruct((groups, capacity, width), terms.dtype)] * 3,
        in_specs=[pl.BlockSpec(memory_space=pltpu.SMEM), vmem, vmem],
        out_specs=[vmem] * 3,
        scratch_shapes=[pltpu.VMEM(flags.shape, jnp.float32)],
        cost_estimate=pl.CostEstimate(
            flops=6 * groups * capacity * rows * width, bytes_accessed=4 * terms.size, transcendentals=0
        ),
        compiler_params=pltpu.CompilerParams(vmem_limit_bytes=24 << 20),
    )(plane, flags, terms)


def places_kernel(own_rows, capacity, plane_ref, slots_ref, column_ref, early_ref, late_ref):
    mine, share = slots_ref.shape
    rows = mine * own_rows
    down = iota((own_rows, share), 0)
    across = iota((LANES, share), 0)
    wanted = []
    for k in range(mine):
        slots = slots_ref[k : k + 1, :]
        source = jnp.where(slots >= 0, slots // own_rows, -1)
        wanted.append(dot_nt(mark(down == slots % own_rows), mark(across == source)))
    wanted = jnp.minimum(jnp.concatenate(wanted, axis=0), 1.0)
    before = mark(iota((rows, rows), 0) > iota((rows, rows), 1))
    ranks = dot(before, wanted.astype(jnp.bfloat16)).astype(jnp.bfloat16)
    shift = plane_ref[0] * capacity
    block = min(512, column_ref.shape[0])
    group = iota((block, 1), 0) % mine
    for start in range(0, column_ref.shape[0], block):
        slots = column_ref[pl.ds(start, block), :]
        source = slots // own_rows
        row = jnp.where(slots >= 0, group * own_rows + slots % own_rows, -1)
        looked = dot(mark(iota((block, rows), 1) == row), ranks)
        found = jnp.where(iota((block, LANES), 1) == source, looked, 0.0)
        rank = jnp.sum(found, axis=1, keepdims=True).astype(jnp.int32) + shift
        base = source * capacity
        live = slots >= 0
        early_ref[pl.ds(start, block), :] = jnp.where(live & (rank < capacity), base + rank, -1)
        late_ref[pl.ds(start, block), :] = jnp.where(live & (rank >= capacity), base + rank - capacity, -1)


def places(plane, own_slots, own_rows, capacity):
    column = own_slots.T.reshape(-1, 1)
    vmem = pl.BlockSpec(memory_space=pltpu.VMEM)
    return pl.pallas_call(
        functools.partial(places_kernel, own_rows, capacity),
        out_shape=[jax.ShapeDtypeStruct(column.shape, jnp.int32)] * 2,
        in_specs=[pl.BlockSpec(memory_space=pltpu.SMEM), vmem, vmem],
        out_specs=[vmem] * 2,
        cost_estimate=pl.CostEstimate(flops=1 << 28, bytes_accessed=1 << 20, transcendentals=0),
    )(plane, own_slots, column)


def early_kernel(places_ref, own_ref, other_ref, out_ref, table):
    groups, capacity, width = own_ref.shape
    both = own_ref[...].astype(jnp.float32) + other_ref[...].astype(jnp.float32)
    table[...] = both.astype(table.dtype).reshape(table.shape)
    block = min(256, out_ref.shape[0])
    columns = iota((block, groups * capacity), 1)
    for start in range(0, out_ref.shape[0], block):
        chosen = mark(columns == places_ref[pl.ds(start, block), :])
        out_ref[pl.ds(start, block), :] = dot(chosen, table[...]).astype(out_ref.dtype)


def late_kernel(places_ref, late_ref, early_ref, out_ref):
    rows, width = early_ref.shape
    share, mine, _ = out_ref.shape
    block = min(256, rows)
    columns = iota((block, late_ref.shape[0]), 1)
    for start in range(0, rows, block):
        chosen = mark(columns == places_ref[pl.ds(start, block), :])
        total = dot(chosen, late_ref[...]) + early_ref[pl.ds(start, block), :].astype(jnp.float32)
        out_ref[pl.ds(start // mine, block // mine)] = total.astype(out_ref.dtype).reshape(block // mine, mine, width)


def early_part(where, own, other):
    groups, capacity, width = own.shape
    vmem = pl.BlockSpec(memory_space=pltpu.VMEM)
    return pl.pallas_call(
        early_kernel,
        out_shape=jax.ShapeDtypeStruct((where.shape[0], width), own.dtype),
        in_specs=[vmem] * 3,
        out_specs=vmem,
        scratch_shapes=[pltpu.VMEM((groups * capacity, width), own.dtype)],
        cost_estimate=pl.CostEstimate(
            flops=2 * where.shape[0] * groups * capacity * width, bytes_accessed=6 * own.size, transcendentals=0
        ),
        compiler_params=pltpu.CompilerParams(vmem_limit_bytes=24 << 20),
    )(where, own, other)


def late_part(where, late, early, mine):
    rows, width = early.shape
    vmem = pl.BlockSpec(memory_space=pltpu.VMEM)
    return pl.pallas_call(
        late_kernel,
        out_shape=jax.ShapeDtypeStruct((rows // mine, mine, width), early.dtype),
        in_specs=[vmem] * 3,
        out_specs=vmem,
        cost_estimate=pl.CostEstimate(
            flops=2 * rows * late.shape[0] * width, bytes_accessed=4 * late.size, transcendentals=0
        ),
        compiler_params=pltpu.CompilerParams(vmem_limit_bytes=24 << 20),
    )(where, late, early)


def exchange(blocks):
    return lax.all_to_all(blocks, "group", split_axis=0, concat_axis=0, tiled=True)


def needed_plan(terms, flags, own_slots, capacity):
    groups = lax.axis_size("group")
    group_total, own_rows, width = terms.shape
    mine = group_total // groups
    plane = lax.axis_index("cuts").astype(jnp.int32)[None]
    early, send, keep = pack(plane, flags, terms.reshape(groups, mine * own_rows, width), capacity)
    late = keep.astype(jnp.float32) + lax.ppermute(send, "cuts", [(0, 1), (1, 0)]).astype(jnp.float32)
    early = exchange(early)
    other = lax.ppermute(early, "cuts", [(1, 0)])
    late = exchange(late.astype(terms.dtype))
    where_early, where_late = places(plane, own_slots, own_rows, capacity)
    out = early_part(where_early, early, other)
    return late_part(where_late, late.reshape(groups * capacity, width), out, mine)


def local(stem_blocks, cap_tensor, slot_rows, counts):
    cuts, groups = lax.axis_size("cuts"), lax.axis_size("group")
    group_total, own_rows, width = stem_blocks.shape[1:]
    mine = group_total // groups
    slot_total = slot_rows.shape[1]
    share = slot_total // cuts
    matrix = build_matrix(cap_tensor[0])
    terms = terms_of(stem_blocks.reshape(group_total * own_rows, width), matrix)
    terms = terms.reshape(group_total, own_rows, matrix.shape[1])

    positions = jnp.arange(slot_total, dtype=jnp.int32)
    marked = jnp.where(positions[None, :] < counts[:, None], slot_rows, -1)
    me = lax.axis_index("cuts")
    doubled = jnp.concatenate([marked, marked], axis=1)
    turned = lax.dynamic_slice_in_dim(doubled, (me + 1) * share, slot_total, 1)

    if cuts != 2 or mine * own_rows != 2 * LANES or LANES % own_rows or groups > LANES:
        return static_plan(terms, turned, cuts)
    capacity = mine * own_rows // 4
    flags = needs(slot_rows, counts, own_rows, capacity, groups)
    flags = exchange(flags.reshape(groups, KINDS, LANES))
    spilled = jnp.max(flags[:, 6, :].astype(jnp.float32)) > 0.0
    flags = flags.reshape(groups * KINDS, LANES)
    return lax.cond(
        spilled,
        lambda: static_plan(terms, turned, cuts),
        lambda: needed_plan(terms, flags, turned[:, (cuts - 1) * share :], capacity),
    )


def solution(mesh):
    in_specs = (
        P("cuts", None, "group", None),
        P("cuts", None, None, None),
        P("group", None),
        P("group"),
    )
    out_specs = P("cuts", "group", None)
    return jax.shard_map(local, mesh=mesh, in_specs=in_specs, out_specs=out_specs, check_vma=False)
```

time: 103 us -> 103 us (level)
  waiting for transfers between devices: 51.2 us -> 43.2 us
  Pallas kernels: 20.3 us -> 23.8 us
  local copies, waits for them, and re-layouts: 4.9 us -> 8.32 us
  starting transfers between devices: 19.7 us -> 22 us
  other arithmetic: 5.57 us -> 4.53 us
    all_to_all x3, waiting for transfers between devices: 4.1 us -> 0.01 us  [exchange(): lax.all_to_all(blocks, 'group', split_axis=0, concat_axis=0, tiled=True)]
    ppermute x1, waiting for transfers between devices: 23.3 us -> 19.3 us  [needed_plan(): other = lax.ppermute(early, 'cuts', [(1, 0)])]
    pallas_call x1, Pallas kernels: 1.9 us -> 4.78 us  [places(): pl.pallas_call(functools.partial(places_kernel, own_rows, capacity), out_...]
    all_to_all x3, starting transfers between devices: 16.8 us -> 19.1 us  [exchange(): lax.all_to_all(blocks, 'group', split_axis=0, concat_axis=0, tiled=True)]
    convert_element_type x2 -> x1, other arithmetic: 3.17 us -> 1.34 us  [needed_plan(): late = exchange(late.astype(terms.dtype))]
    cond x8, local copies, waits for them, and re-layouts: 3.92 us -> 5.35 us
    reshape x0 -> x1, local copies, waits for them, and re-layouts: none -> 1.25 us  [places(): column = own_slots.T.reshape(-1, 1)]
    pallas_call x3 -> x4, Pallas kernels: 16 us -> 16.7 us  [the longest x1 6.17 us: terms_of(): pl.pallas_call(terms_kernel, grid=(total // block,), out_shape=jax.ShapeD...]
  transfers between devices with their start and end apart: 5 -> 5, of which waited for: 3 -> 2; matrix products, arithmetic and copies ran while one was open for 7% -> 7% of each run, Pallas kernels for 7% -> 13%
where the time goes in v3:
time: 103 us
  waiting for transfers between devices  43.2 us (42%)
  Pallas kernels  23.8 us (23%)
  starting transfers between devices  22 us (21%)
  local copies, waits for them, and re-layouts  8.32 us (8%)
  other arithmetic  4.53 us (4%)
    ppermute x1, waiting for transfers between devices, needed_plan(): lax.ppermute(send, 'cuts', [(0, 1), (1, 0)]).astype(jnp.float32)  23.9 us
    ppermute x1, waiting for transfers between devices, needed_plan(): other = lax.ppermute(early, 'cuts', [(1, 0)])  19.3 us
    all_to_all x3, starting transfers between devices, exchange(): lax.all_to_all(blocks, 'group', split_axis=0, concat_axis=0, tiled=True)  19.1 us
    pallas_call x1, Pallas kernels, terms_of(): pl.pallas_call(terms_kernel, grid=(total // block,), out_shape=jax.ShapeD...  6.17 us
    cond x8, local copies, waits for them, and re-layouts  5.35 us
    pallas_call x1, Pallas kernels, places(): pl.pallas_call(functools.partial(places_kernel, own_rows, capacity), out_...  4.78 us
    pallas_call x1, Pallas kernels, pack(): pl.pallas_call(pack_kernel, out_shape=[jax.ShapeDtypeStruct((groups, capa...  4.41 us
    pallas_call x1, Pallas kernels, late_part(): pl.pallas_call(late_kernel, out_shape=jax.ShapeDtypeStruct((rows // mine,...  3.75 us
  transfers between devices with their start and end apart: 5, of which 2 were waited for; matrix products, arithmetic and copies ran while one was open for 7% of the time, Pallas kernels for 13%

profile of v3, /device:TPU:0, one launch (start us, length us, event | category | flops | bytes accessed | tf_op | source)
XLA Modules:
  0.0 102.7 jit_solution(10837489834210229792)
XLA Ops:
  0.0 2.3 %shard_map.48 = bf16[128,128]{1,0:T(8,128)(2,1)} custom-call(s32[4,1024]{1,0:T(4,128)} %slots_ref.1, s32[4]{0:T(128)} %counts_ref.1), custom_call_target="tpu_custom_call" | custom-call | flops 268435456 | bytes 131072 | tf_op jit(solution)/shard_map/pallas_call | solution.py:135
  2.3 7.4 %all-to-all-start.6 = ((bf16[16,8,128]{2,1,0:T(8,128)(2,1)}), bf16[16,8,128]{2,1,0:T(8,128)(2,1)S(1)}, u32[]{:S(2)}, u32[]{:S(2)}) async-start(bf16[16,8,128]{2,1,0:T(8,128)(2,1)} %bitcast.60), calls=%async_computation.6 | async-start | bytes 65536 | tf_op jit(solution)/shard_map/all_to_all | solution.py:289
  9.7 0.8 fusion.5
  10.5 1.0 slice_bitcast_fusion.9
  11.5 0.9 fusion.6
  12.4 0.8 maximum_maximum_fusion.matrix_ref
  13.2 6.2 %shard_map.49 = bf16[4096,512]{1,0:T(8,128)(2,1)} custom-call(bf16[4096,512]{1,0:T(8,128)(2,1)} %bitcast.58, bf16[512,512]{1,0:T(8,128)(2,1)} %maximum_maximum_fusion.matrix_ref), custom_call_target="tpu_custom_call" | custom-call | flops 2147483648 | bytes 8388608 | tf_op jit(solution)/shard_map/pallas_call | solution.py:26
  19.4 0.0 all-to-all-done.6
  19.5 0.6 slice_reduce_fusion
  20.7 81.9 %conditional.1 = (bf16[512,4,512]{2,1,0:T(4,128)(2,1)}) conditional(s32[]{:T(128)} %convert_element_type.49, (s32[4,1024]{1,0:T(4,128)S(1)}, bf16[16,8,128]{2,1,0:T(8,128)(2,1)S(1)}, bf16[4096,512]{1,0:T(8,128)(2,1)}) %tuple.13, (bf16[4096,512]{1,0:T(8,128)(2,1)}, s32[4,1024]{1,0:T(4,128)S(1)}) %tuple.14), branch_computations={%region_1.2_spmd, %region_2.3_spmd} | conditional | flops 5370806272 | bytes 61981160 | solution.py:330
  20.7 4.4 %branch_0_fun.5 = (bf16[16,64,512]{2,1,0:T(8,128)(2,1)}, bf16[16,64,512]{2,1,0:T(8,128)(2,1)S(1)}, bf16[16,64,512]{2,1,0:T(8,128)(2,1)S(1)}) custom-call(s32[1]{0:T(128)} %bitcast.plane_ref, bf16[128,128]{1,0:T(8,128)(2,1)S(1)} %bitcast.59, bf16[16,256,512]{2,1,0:T(8,128)(2,1)} %bitcast.56), custom_call_target="tpu_custom_call" | custom-call | flops 805306368 | bytes 8388608 | tf_op jit(solution)/shard_map/cond/branch_0_fun/pallas_call | solution.py:181
  25.2 6.0 %all-to-all-start.1 = ((bf16[16,64,512]{2,1,0:T(8,128)(2,1)}), bf16[16,64,512]{2,1,0:T(8,128)(2,1)S(1)}, u32[]{:S(2)}, u32[]{:S(2)}) async-start(bf16[16,64,512]{2,1,0:T(8,128)(2,1)} %get-tuple-element.26), calls=%async_computation.1 | async-start | bytes 2097152 | tf_op jit(solution)/shard_map/cond/branch_0_fun/all_to_all | solution.py:289
  31.2 1.6 %collective-permute-start = (bf16[16,64,512]{2,1,0:T(8,128)(2,1)S(1)}, bf16[16,64,512]{2,1,0:T(8,128)(2,1)S(1)}, u32[]{:S(2)}, u32[]{:S(2)}) collective-permute-start(bf16[16,64,512]{2,1,0:T(8,128)(2,1)S(1)} %get-tuple-element.24), channel_id=1, source_target_pairs={{0,16},{16,0},{1,17},{17,1},{2,18},{18,2},{3,19},{19,3},{4,20},{20... | collective-permute-start | bytes 3145736 | tf_op jit(solution)/shard_map/cond/branch_0_fun/ppermute | solution.py:298
  32.7 23.9 %collective-permute-done = bf16[16,64,512]{2,1,0:T(8,128)(2,1)S(1)} collective-permute-done((bf16[16,64,512]{2,1,0:T(8,128)(2,1)S(1)}, bf16[16,64,512]{2,1,0:T(8,128)(2,1)S(1)}, u32[]{:S(2)}, u32[]{:S(2)}) %collective-permute-start) | collective-permute-done | bytes 1048608 | tf_op jit(solution)/shard_map/cond/branch_0_fun/ppermute | solution.py:298
  56.6 1.3 %add_convert_fusion = bf16[16,64,512]{2,1,0:T(8,128)(2,1)} fusion(bf16[16,64,512]{2,1,0:T(8,128)(2,1)S(1)} %collective-permute-done, bf16[16,64,512]{2,1,0:T(8,128)(2,1)S(1)} %get-tuple-element.23), kind=kLoop, calls=%fused_computation | loop fusion | flops 2097152 | bytes 3145728 | tf_op jit(solution)/shard_map/cond/branch_0_fun/convert_element_type | solution.py:301
  58.0 0.0 all-to-all-done.1.own_ref
  58.0 5.8 %all-to-all-start = ((bf16[16,64,512]{2,1,0:T(8,128)(2,1)}), bf16[16,64,512]{2,1,0:T(8,128)(2,1)S(1)}, u32[]{:S(2)}, u32[]{:S(2)}) async-start(bf16[16,64,512]{2,1,0:T(8,128)(2,1)} %add_convert_fusion), calls=%async_computation | async-start | bytes 2097152 | tf_op jit(solution)/shard_map/cond/branch_0_fun/all_to_all | solution.py:289
  63.7 1.3 %collective-permute-start.1 = (bf16[16,64,512]{2,1,0:T(8,128)(2,1)S(1)}, bf16[16,64,512]{2,1,0:T(8,128)(2,1)S(1)}, u32[]{:S(2)}, u32[]{:S(2)}) collective-permute-start(bf16[16,64,512]{2,1,0:T(8,128)(2,1)S(1)} %all-to-all-done.1.own_ref), channel_id=1, source_target_pairs={{16,0},{17,1},{18,2},{19,3},{20,4},{21,5},{22,6},{23,7},{24,8},{25... | collective-permute-start | bytes 3145736 | tf_op jit(solution)/shard_map/cond/branch_0_fun/ppermute | solution.py:300
  65.0 0.6 slice_bitcast_fusion
  65.6 0.1 copy.14
  65.8 1.2 %reshape.35.column_ref = s32[2048,1]{1,0:T(8,128)} reshape(s32[512,4]{1,0:T(8,128)S(1)} %copy.14) | data formatting | bytes 16384 | tf_op jit(solution)/shard_map/cond/branch_0_fun/reshape | solution.py:224
  67.0 4.8 %branch_0_fun.4 = (s32[2048,1]{1,0:T(8,128)}, s32[2048,1]{1,0:T(8,128)}) custom-call(s32[1]{0:T(128)} %bitcast.plane_ref, s32[4,512]{1,0:T(4,128)} %get-tuple-element.48.slots_ref, s32[2048,1]{1,0:T(8,128)} %reshape.35.column_ref), custom_call_target="tpu_custom_call" | custom-call | flops 268435456 | bytes 1048576 | tf_op jit(solution)/shard_map/cond/branch_0_fun/pallas_call | solution.py:226
  71.8 19.3 %collective-permute-done.1.other_ref = bf16[16,64,512]{2,1,0:T(8,128)(2,1)S(1)} collective-permute-done((bf16[16,64,512]{2,1,0:T(8,128)(2,1)S(1)}, bf16[16,64,512]{2,1,0:T(8,128)(2,1)S(1)}, u32[]{:S(2)}, u32[]{:S(2)}) %collective-permute-start.1) | collective-permute-done | bytes 1048608 | tf_op jit(solution)/shard_map/cond/branch_0_fun/ppermute | solution.py:300
  91.1 0.0 copy-start.6
  91.1 1.2 %copy-done.6 = s32[2048,1]{1,0:T(8,128)S(1)} copy-done((s32[2048,1]{1,0:T(8,128)S(1)}, s32[2048,1]{1,0:T(8,128)}, u32[]{:S(2)}) %copy-start.6) | copy-done | bytes 8216 | tf_op jit(solution)/shard_map/cond
  92.4 2.4 %branch_0_fun.6.early_ref = bf16[2048,512]{1,0:T(8,128)(2,1)S(1)} custom-call(s32[2048,1]{1,0:T(8,128)S(1)} %copy-done.6, bf16[16,64,512]{2,1,0:T(8,128)(2,1)S(1)} %all-to-all-done.1.own_ref, bf16[16,64,512]{2,1,0:T(8,128)(2,1)S(1)} %collective-permute-done.1.other_ref), custom_call_target="tpu_custom_call" | custom-call | flops 2147483648 | bytes 3145728 | tf_op jit(solution)/shard_map/cond/branch_0_fun/pallas_call | solution.py:260
  94.8 0.0 copy-start.9
  94.8 1.3 %copy-done.9 = bf16[2048,512]{1,0:T(8,128)(2,1)} copy-done((bf16[2048,512]{1,0:T(8,128)(2,1)}, bf16[2048,512]{1,0:T(8,128)(2,1)S(1)}, u32[]{:S(2)}) %copy-start.9) | copy-done | bytes 2097176 | tf_op jit(solution)/shard_map/cond
  96.1 0.0 all-to-all-done
  96.1 0.0 copy-start.5
  96.1 1.2 %copy-done.5 = s32[2048,1]{1,0:T(8,128)S(1)} copy-done((s32[2048,1]{1,0:T(8,128)S(1)}, s32[2048,1]{1,0:T(8,128)}, u32[]{:S(2)}) %copy-start.5) | copy-done | bytes 8216 | tf_op jit(solution)/shard_map/cond
  97.3 0.0 copy-start.10
  97.3 1.6 %copy-done.10 = bf16[2048,512]{1,0:T(8,128)(2,1)S(1)} copy-done((bf16[2048,512]{1,0:T(8,128)(2,1)S(1)}, bf16[2048,512]{1,0:T(8,128)(2,1)}, u32[]{:S(2)}) %copy-start.10) | copy-done | bytes 2097176 | tf_op jit(solution)/shard_map/cond
  98.9 3.8 %branch_0_fun.7 = bf16[512,4,512]{2,1,0:T(4,128)(2,1)} custom-call(s32[2048,1]{1,0:T(8,128)S(1)} %copy-done.5, bf16[1024,512]{1,0:T(8,128)(2,1)S(1)} %bitcast.53, bf16[2048,512]{1,0:T(8,128)(2,1)S(1)} %copy-done.10), custom_call_target="tpu_custom_call" | custom-call | flops 2147483648 | bytes 2097152 | tf_op jit(solution)/shard_map/cond/branch_0_fun/pallas_call | solution.py:276
  (1 shorter events, 0.0 us)
Async XLA Ops:
  2.3 17.1 %all-to-all-start.6 = ((bf16[16,8,128]{2,1,0:T(8,128)(2,1)}), bf16[16,8,128]{2,1,0:T(8,128)(2,1)S(1)}, u32[]{:S(2)}, u32[]{:S(2)}) async-start(bf16[16,8,128]{2,1,0:T(8,128)(2,1)} %bitcast.60), calls=%async_computation.6 | async-start | bytes 65536 | tf_op jit(solution)/shard_map/all_to_all | solution.py:289
  25.2 32.8 %all-to-all-start.1 = ((bf16[16,64,512]{2,1,0:T(8,128)(2,1)}), bf16[16,64,512]{2,1,0:T(8,128)(2,1)S(1)}, u32[]{:S(2)}, u32[]{:S(2)}) async-start(bf16[16,64,512]{2,1,0:T(8,128)(2,1)} %get-tuple-element.26), calls=%async_computation.1 | async-start | bytes 2097152 | tf_op jit(solution)/shard_map/cond/branch_0_fun/all_to_all | solution.py:289
  31.2 25.5 %collective-permute-start = (bf16[16,64,512]{2,1,0:T(8,128)(2,1)S(1)}, bf16[16,64,512]{2,1,0:T(8,128)(2,1)S(1)}, u32[]{:S(2)}, u32[]{:S(2)}) collective-permute-start(bf16[16,64,512]{2,1,0:T(8,128)(2,1)S(1)} %get-tuple-element.24), channel_id=1, source_target_pairs={{0,16},{16,0},{1,17},{17,1},{2,18},{18,2},{3,19},{19,3},{4,20},{20... | collective-permute-start | bytes 3145736 | tf_op jit(solution)/shard_map/cond/branch_0_fun/ppermute | solution.py:298
  58.0 38.1 %all-to-all-start = ((bf16[16,64,512]{2,1,0:T(8,128)(2,1)}), bf16[16,64,512]{2,1,0:T(8,128)(2,1)S(1)}, u32[]{:S(2)}, u32[]{:S(2)}) async-start(bf16[16,64,512]{2,1,0:T(8,128)(2,1)} %add_convert_fusion), calls=%async_computation | async-start | bytes 2097152 | tf_op jit(solution)/shard_map/cond/branch_0_fun/all_to_all | solution.py:289
  63.7 27.4 %collective-permute-start.1 = (bf16[16,64,512]{2,1,0:T(8,128)(2,1)S(1)}, bf16[16,64,512]{2,1,0:T(8,128)(2,1)S(1)}, u32[]{:S(2)}, u32[]{:S(2)}) collective-permute-start(bf16[16,64,512]{2,1,0:T(8,128)(2,1)S(1)} %all-to-all-done.1.own_ref), channel_id=1, source_target_pairs={{16,0},{17,1},{18,2},{19,3},{20,4},{21,5},{22,6},{23,7},{24,8},{25... | collective-permute-start | bytes 3145736 | tf_op jit(solution)/shard_map/cond/branch_0_fun/ppermute | solution.py:300
  91.1 1.2 %copy-start.6 = (s32[2048,1]{1,0:T(8,128)S(1)}, s32[2048,1]{1,0:T(8,128)}, u32[]{:S(2)}) copy-start(s32[2048,1]{1,0:T(8,128)} %get-tuple-element.25.places_ref) | copy-start | bytes 24580 | tf_op jit(solution)/shard_map/cond
  94.8 1.3 %copy-start.9 = (bf16[2048,512]{1,0:T(8,128)(2,1)}, bf16[2048,512]{1,0:T(8,128)(2,1)S(1)}, u32[]{:S(2)}) copy-start(bf16[2048,512]{1,0:T(8,128)(2,1)S(1)} %branch_0_fun.6.early_ref) | copy-start | bytes 6291460 | tf_op jit(solution)/shard_map/cond
  96.1 1.2 %copy-start.5 = (s32[2048,1]{1,0:T(8,128)S(1)}, s32[2048,1]{1,0:T(8,128)}, u32[]{:S(2)}) copy-start(s32[2048,1]{1,0:T(8,128)} %get-tuple-element.20.places_ref) | copy-start | bytes 24580 | tf_op jit(solution)/shard_map/cond
  97.3 1.6 %copy-start.10 = (bf16[2048,512]{1,0:T(8,128)(2,1)S(1)}, bf16[2048,512]{1,0:T(8,128)(2,1)}, u32[]{:S(2)}) copy-start(bf16[2048,512]{1,0:T(8,128)(2,1)} %copy-done.9) | copy-start | bytes 6291460 | tf_op jit(solution)/shard_map/cond

commit v4 on v3

v4 whole, which is shorter than its diff:
```python
import functools

import jax
import jax.numpy as jnp
from jax import lax
from jax.experimental import pallas as pl
from jax.experimental.pallas import tpu as pltpu
from jax.sharding import PartitionSpec as P


def terms_kernel(rows_ref, pair_ref, out_ref, matrix):
    half = pair_ref.shape[1]

    @pl.when(pl.program_id(0) == 0)
    def _():
        real_part, imag_part = pair_ref[0], pair_ref[1]
        matrix[:half, :half] = real_part
        matrix[:half, half:] = imag_part
        matrix[half:, :half] = -imag_part
        matrix[half:, half:] = real_part

    out_ref[...] = dot(rows_ref[...], matrix[...]).astype(out_ref.dtype)


def terms_of(rows, pair):
    total, width = rows.shape
    block = min(512, total)
    out_width = 2 * pair.shape[2]
    return pl.pallas_call(
        terms_kernel,
        grid=(total // block,),
        out_shape=jax.ShapeDtypeStruct((total, out_width), rows.dtype),
        in_specs=[pl.BlockSpec((block, width), lambda i: (i, 0)), pl.BlockSpec(pair.shape, lambda i: (0, 0, 0))],
        out_specs=pl.BlockSpec((block, out_width), lambda i: (i, 0)),
        scratch_shapes=[pltpu.VMEM((width, out_width), rows.dtype)],
        cost_estimate=pl.CostEstimate(
            flops=2 * total * width * out_width, bytes_accessed=4 * rows.size, transcendentals=0
        ),
    )(rows, pair)


def select_kernel(block, share, terms_ref, slots_ref, *outs):
    columns = iota((block, terms_ref.shape[0]), 1)
    for part, out in enumerate(outs):
        for start in range(0, share, block):
            chosen = mark(columns == slots_ref[pl.ds(part * share + start, block), :])
            out[pl.ds(start, block), :] = dot(chosen, terms_ref[...]).astype(out.dtype)


def select(terms, slots, parts):
    row_total, width = terms.shape
    slot_total = slots.shape[0]
    share = slot_total // parts
    return pl.pallas_call(
        functools.partial(select_kernel, min(256, share), share),
        out_shape=[jax.ShapeDtypeStruct((share, width), terms.dtype)] * parts,
        in_specs=[pl.BlockSpec(memory_space=pltpu.VMEM)] * 2,
        out_specs=[pl.BlockSpec(memory_space=pltpu.VMEM)] * parts,
        cost_estimate=pl.CostEstimate(
            flops=2 * row_total * width * slot_total,
            bytes_accessed=2 * (terms.size + slot_total * width),
            transcendentals=0,
        ),
        compiler_params=pltpu.CompilerParams(vmem_limit_bytes=24 << 20),
    )(terms, slots)


def static_plan(terms, turned, cuts):
    groups = lax.axis_size("group")
    group_total, own_rows, width = terms.shape
    mine = group_total // groups
    by_owner = terms.reshape(groups, mine, own_rows, width)
    sums, selected = [], []
    for k in range(mine):
        outgoing = by_owner[:, k]
        if k >= 2:
            outgoing, selected[k - 2] = lax.optimization_barrier((outgoing, selected[k - 2]))
        got = lax.all_to_all(outgoing, "group", split_axis=0, concat_axis=0, tiled=True)
        parts = select(got.reshape(groups * own_rows, width), turned[k][:, None], cuts)
        selected.append(parts)
    for parts in selected:
        total = parts[-1].astype(jnp.float32)
        for step in range(1, cuts):
            ring = [(i, (i + step) % cuts) for i in range(cuts)]
            total = total + lax.ppermute(parts[step - 1], "cuts", ring).astype(jnp.float32)
        sums.append(total.astype(terms.dtype))
    return jnp.stack(sums, axis=1)


KINDS = 8
LANES = 128
EARLY, LATE = 56, 72


def dot(a, b):
    return jnp.dot(a, b, preferred_element_type=jnp.float32)


def dot_nt(a, b):
    return lax.dot_general(a, b, (((1,), (1,)), ((), ())), preferred_element_type=jnp.float32)


def iota(shape, dim):
    return lax.broadcasted_iota(jnp.int32, shape, dim)


def mark(condition):
    return jnp.where(condition, 1.0, 0.0).astype(jnp.bfloat16)


def needs_kernel(own_rows, early, late, slots_ref, counts_ref, flags_ref):
    mine, slot_total = slots_ref.shape
    side = flags_ref.shape[0]
    hits = jnp.zeros((side, LANES), jnp.float32)
    place = iota((1, slot_total), 1)
    down = iota((side, slot_total), 0)
    across = iota((LANES, slot_total), 0)
    per = LANES // own_rows
    for k in range(mine):
        slots = slots_ref[k : k + 1, :]
        half = jnp.where(place >= slot_total // 2, 2, 0)
        row_key = (slots // own_rows) * KINDS + half + k // per
        row_key = jnp.where(place < counts_ref[k], row_key, -1)
        lane_key = slots % own_rows + (k % per) * own_rows
        hits = hits + dot_nt(mark(down == row_key), mark(across == lane_key))
    flags = jnp.minimum(hits, 1.0)
    row, column = iota((side, side), 0), iota((side, side), 1)
    kind, back = row % KINDS, row - column
    first = (kind == 4) & ((back == 4) | (back == 3))
    second = (kind == 5) & ((back == 3) | (back == 2))
    sums = dot(flags.astype(jnp.bfloat16), jnp.ones((LANES, LANES), jnp.bfloat16))
    counted = dot(mark(first | second), sums.astype(jnp.bfloat16))
    kind = iota((side, LANES), 0) % KINDS
    room = jnp.where(kind == 4, 1.0 * (early + late), 1.0 * late)
    spill = jnp.max(jnp.where((kind == 4) | (kind == 5), counted - room, 0.0))
    flags_ref[...] = jnp.where(kind == 6, jnp.where(spill > 0.0, 1.0, 0.0), flags).astype(flags_ref.dtype)


def needs(slot_rows, counts, own_rows, early, late, groups):
    return pl.pallas_call(
        functools.partial(needs_kernel, own_rows, early, late),
        out_shape=jax.ShapeDtypeStruct((groups * KINDS, LANES), jnp.bfloat16),
        in_specs=[pl.BlockSpec(memory_space=pltpu.VMEM), pl.BlockSpec(memory_space=pltpu.SMEM)],
        out_specs=pl.BlockSpec(memory_space=pltpu.VMEM),
        cost_estimate=pl.CostEstimate(flops=1 << 28, bytes_accessed=1 << 17, transcendentals=0),
    )(slot_rows, counts)


def keys_of(flags):
    side = flags.shape[0]
    marks = flags
    lower = mark(iota((LANES, LANES), 0) < iota((LANES, LANES), 1))
    inside = dot(marks, lower)
    totals = dot(marks, jnp.ones((LANES, LANES), jnp.bfloat16))
    row, column = iota((side, side), 0), iota((side, side), 1)
    follows = ((row % KINDS == 1) | (row % KINDS == 3)) & (row - column == 1)
    ranks = inside + dot(mark(follows), totals.astype(jnp.bfloat16))
    return jnp.where(flags.astype(jnp.float32) > 0.0, ranks, -1.0)


def chosen_rows(capacity, upper, lower):
    rank = iota((capacity, LANES), 0).astype(jnp.float32)
    return jnp.concatenate([mark(rank == upper), mark(rank == lower)], axis=1)


def pack_late_kernel(first_rank, plane_ref, flags_ref, terms_ref, send_ref, keep_ref, keys_ref):
    batch, capacity, _ = send_ref.shape
    step = pl.program_id(0)

    @pl.when(step == 0)
    def _():
        keys_ref[...] = keys_of(flags_ref[...])

    plane = plane_ref[0]
    for i in range(batch):
        keys = keys_ref[pl.ds((step * batch + i) * KINDS, KINDS), :]
        second = keys[2:3], keys[3:4]
        beyond = keys[0:1] - first_rank, keys[1:2] - first_rank
        sent = [jnp.where(plane == 0, b, a) for a, b in zip(beyond, second)]
        kept = [jnp.where(plane == 0, a, b) for a, b in zip(beyond, second)]
        chosen = jnp.concatenate([chosen_rows(capacity, *sent), chosen_rows(capacity, *kept)], axis=0)
        packed = dot(chosen, terms_ref[i]).astype(send_ref.dtype)
        send_ref[i] = packed[:capacity]
        keep_ref[i] = packed[capacity:]


def pack_late(plane, flags, terms, first_rank, capacity):
    groups, rows, width = terms.shape
    batch = 4 if groups % 4 == 0 else 1
    out = jax.ShapeDtypeStruct((groups, capacity, width), terms.dtype)
    block = pl.BlockSpec((batch, capacity, width), lambda i: (i, 0, 0))
    table = pl.BlockSpec(flags.shape, lambda i: (0, 0))
    return pl.pallas_call(
        functools.partial(pack_late_kernel, first_rank),
        grid=(groups // batch,),
        out_shape=[out, out, jax.ShapeDtypeStruct(flags.shape, jnp.float32)],
        in_specs=[
            pl.BlockSpec(memory_space=pltpu.SMEM),
            table,
            pl.BlockSpec((batch, rows, width), lambda i: (i, 0, 0)),
        ],
        out_specs=[block, block, table],
        cost_estimate=pl.CostEstimate(
            flops=4 * groups * capacity * rows * width, bytes_accessed=4 * terms.size, transcendentals=0
        ),
    )(plane, flags, terms)


def pack_early_kernel(keys_ref, terms_ref, out_ref):
    batch, capacity, _ = out_ref.shape
    step = pl.program_id(0)
    for i in range(batch):
        keys = keys_ref[pl.ds((step * batch + i) * KINDS, KINDS), :]
        chosen = chosen_rows(capacity, keys[0:1], keys[1:2])
        out_ref[i] = dot(chosen, terms_ref[i]).astype(out_ref.dtype)


def pack_early(keys, terms, capacity):
    groups, rows, width = terms.shape
    batch = 4 if groups % 4 == 0 else 1
    return pl.pallas_call(
        pack_early_kernel,
        grid=(groups // batch,),
        out_shape=jax.ShapeDtypeStruct((groups, capacity, width), terms.dtype),
        in_specs=[
            pl.BlockSpec(keys.shape, lambda i: (0, 0)),
            pl.BlockSpec((batch, rows, width), lambda i: (i, 0, 0)),
        ],
        out_specs=pl.BlockSpec((batch, capacity, width), lambda i: (i, 0, 0)),
        cost_estimate=pl.CostEstimate(
            flops=2 * groups * capacity * rows * width, bytes_accessed=3 * terms.size, transcendentals=0
        ),
    )(keys, terms)


def places_kernel(own_rows, early, late, plane_ref, slots_ref, column_ref, early_ref, late_ref):
    mine, share = slots_ref.shape
    rows = mine * own_rows
    down = iota((own_rows, share), 0)
    across = iota((LANES, share), 0)
    wanted = []
    for k in range(mine):
        slots = slots_ref[k : k + 1, :]
        source = jnp.where(slots >= 0, slots // own_rows, -1)
        wanted.append(dot_nt(mark(down == slots % own_rows), mark(across == source)))
    wanted = jnp.minimum(jnp.concatenate(wanted, axis=0), 1.0)
    before = mark(iota((rows, rows), 0) > iota((rows, rows), 1))
    ranks = dot(before, wanted.astype(jnp.bfloat16)).astype(jnp.bfloat16)
    shift = plane_ref[0] * early
    group = iota((LANES, 1), 0) % mine
    lane = iota((LANES, LANES), 1)
    in_early = jnp.full((LANES, LANES), -1, jnp.int32)
    in_late = in_early
    for block in range(mine * share // LANES):
        slots = column_ref[:, block : block + 1]
        source = slots // own_rows
        row = jnp.where(slots >= 0, group * own_rows + slots % own_rows, -1)
        looked = dot(mark(iota((LANES, rows), 1) == row), ranks)
        found = jnp.where(lane == source, looked, 0.0)
        rank = jnp.sum(found, axis=1, keepdims=True).astype(jnp.int32) + shift
        live, low = slots >= 0, rank < early
        in_early = jnp.where((lane == block) & live & low, source * early + rank, in_early)
        in_late = jnp.where((lane == block) & live & ~low, source * late + rank - early, in_late)
    early_ref[...] = in_early
    late_ref[...] = in_late


def places(plane, own_slots, own_rows, early, late):
    column = own_slots.T.reshape(-1, LANES).T
    vmem = pl.BlockSpec(memory_space=pltpu.VMEM)
    return pl.pallas_call(
        functools.partial(places_kernel, own_rows, early, late),
        out_shape=[jax.ShapeDtypeStruct((LANES, LANES), jnp.int32)] * 2,
        in_specs=[pl.BlockSpec(memory_space=pltpu.SMEM), vmem, vmem],
        out_specs=[vmem] * 2,
        cost_estimate=pl.CostEstimate(flops=1 << 28, bytes_accessed=1 << 18, transcendentals=0),
    )(plane, own_slots, column)


def early_kernel(places_ref, own_ref, other_ref, out_ref, table):
    both = own_ref[...].astype(jnp.float32) + other_ref[...].astype(jnp.float32)
    table[...] = both.astype(table.dtype)
    columns = iota((LANES, table.shape[0]), 1)
    for block in range(out_ref.shape[0] // LANES):
        chosen = mark(columns == places_ref[:, block : block + 1])
        out_ref[block * LANES : (block + 1) * LANES, :] = dot(chosen, table[...]).astype(out_ref.dtype)


def late_kernel(places_ref, late_ref, early_ref, out_ref):
    rows, width = early_ref.shape
    share, mine, _ = out_ref.shape
    per = LANES // mine
    columns = iota((LANES, late_ref.shape[0]), 1)
    for block in range(rows // LANES):
        chosen = mark(columns == places_ref[:, block : block + 1])
        early = early_ref[block * LANES : (block + 1) * LANES, :].astype(jnp.float32)
        total = (dot(chosen, late_ref[...]) + early).astype(out_ref.dtype)
        out_ref[block * per : (block + 1) * per] = total.reshape(per, mine, width)


def early_part(where, own, other, slots):
    rows, width = own.shape
    vmem = pl.BlockSpec(memory_space=pltpu.VMEM)
    return pl.pallas_call(
        early_kernel,
        out_shape=jax.ShapeDtypeStruct((slots, width), own.dtype),
        in_specs=[vmem] * 3,
        out_specs=vmem,
        scratch_shapes=[pltpu.VMEM((rows, width), own.dtype)],
        cost_estimate=pl.CostEstimate(
            flops=2 * slots * rows * width, bytes_accessed=6 * own.size, transcendentals=0
        ),
        compiler_params=pltpu.CompilerParams(vmem_limit_bytes=12 << 20),
    )(where, own, other)


def late_part(where, late, early, mine):
    rows, width = early.shape
    vmem = pl.BlockSpec(memory_space=pltpu.VMEM)
    return pl.pallas_call(
        late_kernel,
        out_shape=jax.ShapeDtypeStruct((rows // mine, mine, width), early.dtype),
        in_specs=[vmem] * 3,
        out_specs=vmem,
        cost_estimate=pl.CostEstimate(
            flops=2 * rows * late.shape[0] * width, bytes_accessed=4 * late.size, transcendentals=0
        ),
        compiler_params=pltpu.CompilerParams(vmem_limit_bytes=12 << 20),
    )(where, late, early)


def exchange(blocks):
    return lax.all_to_all(blocks, "group", split_axis=0, concat_axis=0, tiled=True)


def local(stem_blocks, cap_tensor, slot_rows, counts):
    cuts, groups = lax.axis_size("cuts"), lax.axis_size("group")
    group_total, own_rows, width = stem_blocks.shape[1:]
    mine = group_total // groups
    slot_total = slot_rows.shape[1]
    share = slot_total // cuts
    terms = terms_of(stem_blocks.reshape(group_total * own_rows, width), cap_tensor[0])
    width = terms.shape[1]

    positions = jnp.arange(slot_total, dtype=jnp.int32)
    marked = jnp.where(positions[None, :] < counts[:, None], slot_rows, -1)
    me = lax.axis_index("cuts").astype(jnp.int32)
    doubled = jnp.concatenate([marked, marked], axis=1)
    turned = lax.dynamic_slice_in_dim(doubled, (me + 1) * share, slot_total, 1)

    def all_rows():
        return static_plan(terms.reshape(group_total, own_rows, width), turned, cuts)

    if cuts != 2 or mine * own_rows != 2 * LANES or LANES % own_rows or groups > LANES:
        return all_rows()

    early, late = EARLY, LATE
    plane = me[None]
    flags = needs(slot_rows, counts, own_rows, early, late, groups)
    flags = exchange(flags.reshape(groups, KINDS, LANES))
    spilled = jnp.max(flags[:, 6, :].astype(jnp.float32)) > 0.0
    by_owner = terms.reshape(groups, mine * own_rows, width)
    send, keep, keys = pack_late(plane, flags.reshape(groups * KINDS, LANES), by_owner, early, late)
    other = lax.ppermute(send, "cuts", [(0, 1), (1, 0)])
    own_early = exchange(pack_early(keys, by_owner, early)).reshape(groups * early, width)
    summed = (keep.astype(jnp.float32) + other.astype(jnp.float32)).astype(terms.dtype)
    other_early = lax.ppermute(own_early, "cuts", [(1, 0)])
    own_late = exchange(summed).reshape(groups * late, width)
    where_early, where_late = places(plane, turned[:, (cuts - 1) * share :], own_rows, early, late)
    sums = early_part(where_early, own_early, other_early, share * mine)
    return lax.cond(spilled, all_rows, lambda: late_part(where_late, own_late, sums, mine))


def solution(mesh):
    in_specs = (
        P("cuts", None, "group", None),
        P("cuts", None, None, None),
        P("group", None),
        P("group"),
    )
    out_specs = P("cuts", "group", None)
    return jax.shard_map(local, mesh=mesh, in_specs=in_specs, out_specs=out_specs, check_vma=False)
```

time: 103 us -> 106 us (1.029)
  Pallas kernels: 23.8 us -> 36.3 us
  local copies, waits for them, and re-layouts: 8.32 us -> 3.1 us
  waiting for transfers between devices: 43.2 us -> 39.7 us
  other arithmetic: 4.53 us -> 2.87 us
    pallas_call x4 -> x5, Pallas kernels: 13.9 us -> 22.4 us  [the longest x1 6.49 us: places(): pl.pallas_call(functools.partial(places_kernel, own_rows, early, late), o...]
    cond x8 -> x0, local copies, waits for them, and re-layouts: 5.35 us -> none
    ppermute x2, waiting for transfers between devices: 43.2 us -> 39.7 us  [the longest x1 26.8 us: local(): other = lax.ppermute(send, 'cuts', [(0, 1), (1, 0)])]
    pallas_call x1, Pallas kernels: 3.75 us -> 5.86 us  [late_part(): pl.pallas_call(late_kernel, out_shape=jax.ShapeDtypeStruct((rows // mine,...]
    pallas_call x1, Pallas kernels: 6.17 us -> 8.12 us  [terms_of(): pl.pallas_call(terms_kernel, grid=(total // block,), out_shape=jax.ShapeD...]
    unnamed x0 -> x12, local copies, waits for them, and re-layouts: none -> 1.46 us
  transfers between devices with their start and end apart: 5 -> 5, of which waited for: 2 -> 2; matrix products, arithmetic and copies ran while one was open for 7% -> 4% of each run, Pallas kernels for 13% -> 18%
where the time goes in v4:
time: 106 us; the launch traced here: 105 us
  waiting for transfers between devices  39.7 us (37%)
  Pallas kernels  36.3 us (34%)
  starting transfers between devices  22.1 us (21%)
  local copies, waits for them, and re-layouts  3.1 us (3%)
  other arithmetic  2.87 us (3%)
    ppermute x1, waiting for transfers between devices, local(): other = lax.ppermute(send, 'cuts', [(0, 1), (1, 0)])  26.8 us
    all_to_all x3, starting transfers between devices, exchange(): lax.all_to_all(blocks, 'group', split_axis=0, concat_axis=0, tiled=True)  19.2 us
    ppermute x1, waiting for transfers between devices, local(): other_early = lax.ppermute(own_early, 'cuts', [(1, 0)])  12.9 us
    pallas_call x1, Pallas kernels, terms_of(): pl.pallas_call(terms_kernel, grid=(total // block,), out_shape=jax.ShapeD...  8.12 us
    pallas_call x1, Pallas kernels, places(): pl.pallas_call(functools.partial(places_kernel, own_rows, early, late), o...  6.49 us
    pallas_call x1, Pallas kernels, late_part(): pl.pallas_call(late_kernel, out_shape=jax.ShapeDtypeStruct((rows // mine,...  5.86 us
    pallas_call x1, Pallas kernels, pack_late(): pl.pallas_call(functools.partial(pack_late_kernel, first_rank), grid=(gro...  5.09 us
    pallas_call x1, Pallas kernels, pack_early(): pl.pallas_call(pack_early_kernel, grid=(groups // batch,), out_shape=jax....  4.61 us
  transfers between devices with their start and end apart: 5, of which 2 were waited for; matrix products, arithmetic and copies ran while one was open for 4% of the time, Pallas kernels for 18%

profile of v4, /device:TPU:0, one launch (start us, length us, event | category | flops | bytes accessed | tf_op | source)
XLA Modules:
  0.0 104.9 jit_solution(6350950474683222328)
XLA Ops:
  0.0 2.3 %shard_map.48 = bf16[128,128]{1,0:T(8,128)(2,1)} custom-call(s32[4,1024]{1,0:T(4,128)} %slots_ref.1, s32[4]{0:T(128)} %counts_ref.1), custom_call_target="tpu_custom_call" | custom-call | flops 268435456 | bytes 131072 | tf_op jit(solution)/shard_map/pallas_call | solution.py:140
  2.3 7.4 %all-to-all-start.4 = ((bf16[16,8,128]{2,1,0:T(8,128)(2,1)}), bf16[16,8,128]{2,1,0:T(8,128)(2,1)S(1)}, u32[]{:S(2)}, u32[]{:S(2)}) async-start(bf16[16,8,128]{2,1,0:T(8,128)(2,1)} %bitcast.62), calls=%async_computation.4 | async-start | bytes 65536 | tf_op jit(solution)/shard_map/all_to_all | solution.py:333
  9.7 8.1 %shard_map.49 = bf16[4096,512]{1,0:T(8,128)(2,1)} custom-call(bf16[4096,512]{1,0:T(8,128)(2,1)} %bitcast.57, bf16[2,256,256]{2,1,0:T(8,128)(2,1)} %bitcast.59), custom_call_target="tpu_custom_call" | custom-call | flops 2147483648 | bytes 8388608 | tf_op jit(solution)/shard_map/pallas_call | solution.py:29
  17.8 0.0 all-to-all-done.4
  17.8 0.0 copy-start.10
  17.8 0.6 copy-done.10
  18.4 5.1 %shard_map.50 = (bf16[16,72,512]{2,1,0:T(8,128)(2,1)}, bf16[16,72,512]{2,1,0:T(8,128)(2,1)}, f32[128,128]{1,0:T(8,128)}) custom-call(s32[1]{0:T(128)} %bitcast.19.plane_ref, bf16[128,128]{1,0:T(8,128)(2,1)} %bitcast.60, bf16[16,256,512]{2,1,0:T(8,128)(2,1)} %bitcast.54), custom_call_target="tpu_custom_call" | custom-call | flops 603979776 | bytes 8388608 | tf_op jit(solution)/shard_map/pallas_call | solution.py:193
  23.5 0.0 copy-start.13
  23.5 4.6 %shard_map.52 = bf16[16,56,512]{2,1,0:T(8,128)(2,1)} custom-call(f32[128,128]{1,0:T(8,128)} %get-tuple-element.47.keys_ref, bf16[16,256,512]{2,1,0:T(8,128)(2,1)} %bitcast.55), custom_call_target="tpu_custom_call" | custom-call | flops 234881024 | bytes 6291456 | tf_op jit(solution)/shard_map/pallas_call | solution.py:221
  28.1 0.0 copy-start.9
  28.1 6.1 %all-to-all-start.6 = ((bf16[16,56,512]{2,1,0:T(8,128)(2,1)}), bf16[16,56,512]{2,1,0:T(8,128)(2,1)S(1)}, u32[]{:S(2)}, u32[]{:S(2)}) async-start(bf16[16,56,512]{2,1,0:T(8,128)(2,1)} %shard_map.52), calls=%async_computation.6 | async-start | bytes 1835008 | tf_op jit(solution)/shard_map/all_to_all | solution.py:333
  34.3 0.0 copy-done.13
  34.3 1.6 %collective-permute-start.4 = (bf16[16,72,512]{2,1,0:T(8,128)(2,1)S(1)}, bf16[16,72,512]{2,1,0:T(8,128)(2,1)S(1)}, u32[]{:S(2)}, u32[]{:S(2)}) collective-permute-start(bf16[16,72,512]{2,1,0:T(8,128)(2,1)S(1)} %copy-done.13), channel_id=1, source_target_pairs={{0,16},{16,0},{1,17},{17,1},{2,18},{18,2},{3,19},{19,3},{4,20},{20... | collective-permute-start | bytes 3538952 | tf_op jit(solution)/shard_map/ppermute | solution.py:364
  35.9 26.8 %collective-permute-done.4 = bf16[16,72,512]{2,1,0:T(8,128)(2,1)S(1)} collective-permute-done((bf16[16,72,512]{2,1,0:T(8,128)(2,1)S(1)}, bf16[16,72,512]{2,1,0:T(8,128)(2,1)S(1)}, u32[]{:S(2)}, u32[]{:S(2)}) %collective-permute-start.4) | collective-permute-done | bytes 1179680 | tf_op jit(solution)/shard_map/ppermute | solution.py:364
  62.7 0.0 copy-done.9
  62.7 0.0 copy-start.11
  62.7 0.0 copy-start.12
  62.7 1.4 %add_convert_fusion.4 = bf16[16,72,512]{2,1,0:T(8,128)(2,1)} fusion(bf16[16,72,512]{2,1,0:T(8,128)(2,1)S(1)} %collective-permute-done.4, bf16[16,72,512]{2,1,0:T(8,128)(2,1)S(1)} %copy-done.9), kind=kLoop, calls=%fused_computation.17 | loop fusion | flops 2359296 | bytes 3538944 | tf_op jit(solution)/shard_map/convert_element_type | solution.py:366
  64.0 0.0 all-to-all-done.6
  64.0 5.7 %all-to-all-start.5 = ((bf16[16,72,512]{2,1,0:T(8,128)(2,1)}), bf16[16,72,512]{2,1,0:T(8,128)(2,1)S(1)}, u32[]{:S(2)}, u32[]{:S(2)}) async-start(bf16[16,72,512]{2,1,0:T(8,128)(2,1)} %add_convert_fusion.4), calls=%async_computation.5 | async-start | bytes 2359296 | tf_op jit(solution)/shard_map/all_to_all | solution.py:333
  69.8 1.3 %collective-permute-start.5 = (bf16[896,512]{1,0:T(8,128)(2,1)S(1)}, bf16[896,512]{1,0:T(8,128)(2,1)S(1)}, u32[]{:S(2)}, u32[]{:S(2)}) collective-permute-start(bf16[896,512]{1,0:T(8,128)(2,1)S(1)} %bitcast.52), channel_id=1, source_target_pairs={{16,0},{17,1},{18,2},{19,3},{20,4},{21,5},{22,6},{23,7},{24,8},{25... | collective-permute-start | bytes 2752520 | tf_op jit(solution)/shard_map/ppermute | solution.py:367
  71.1 0.0 copy-done.11
  71.1 0.0 copy-done.12
  71.1 0.1 fusion.5
  71.2 0.6 slice_bitcast_fusion.8
  71.8 0.1 copy.22
  72.0 0.2 reshape.42
  72.1 0.7 copy.23
  72.9 6.5 %shard_map.51 = (s32[128,128]{1,0:T(8,128)}, s32[128,128]{1,0:T(8,128)S(1)}) custom-call(s32[1]{0:T(128)} %bitcast.19.plane_ref, s32[4,512]{1,0:T(4,128)} %get-tuple-element.61.slots_ref, s32[128,16]{1,0:T(8,128)} %bitcast.61), custom_call_target="tpu_custom_call" | custom-call | flops 268435456 | bytes 262144 | tf_op jit(solution)/shard_map/pallas_call | solution.py:271
  79.3 1.4 %slice_reduce_fusion = bf16[]{:T(256)} fusion(bf16[16,8,128]{2,1,0:T(8,128)(2,1)} %copy-done.10), kind=kLoop, calls=%fused_computation.23 | loop fusion | flops 2047 | bytes 4098 | tf_op jit(solution)/shard_map/reduce_max | solution.py:361
  81.4 12.9 %collective-permute-done.5.other_ref = bf16[896,512]{1,0:T(8,128)(2,1)S(1)} collective-permute-done((bf16[896,512]{1,0:T(8,128)(2,1)S(1)}, bf16[896,512]{1,0:T(8,128)(2,1)S(1)}, u32[]{:S(2)}, u32[]{:S(2)}) %collective-permute-start.5) | collective-permute-done | bytes 917536 | tf_op jit(solution)/shard_map/ppermute | solution.py:367
  94.3 0.0 copy-start.7
  94.3 0.8 copy-done.7
  95.2 3.8 %shard_map.53 = bf16[2048,512]{1,0:T(8,128)(2,1)} custom-call(s32[128,128]{1,0:T(8,128)S(1)} %copy-done.7, bf16[896,512]{1,0:T(8,128)(2,1)S(1)} %bitcast.53, bf16[896,512]{1,0:T(8,128)(2,1)S(1)} %collective-permute-done.5.other_ref), custom_call_target="tpu_custom_call" | custom-call | flops 1879048192 | bytes 2752512 | tf_op jit(solution)/shard_map/pallas_call | solution.py:304
  99.0 0.0 all-to-all-done.5
  99.0 5.9 %conditional.1 = (bf16[512,4,512]{2,1,0:T(4,128)(2,1)}) conditional(s32[]{:T(128)} %convert_element_type.49, (bf16[16,72,512]{2,1,0:T(8,128)(2,1)S(1)}, s32[128,128]{1,0:T(8,128)S(1)}, bf16[2048,512]{1,0:T(8,128)(2,1)}) %tuple.13, (bf16[4096,512]{1,0:T(8,128)(2,1)}, s32[4,1024]{1,0:T(4,128)S(1)}) %tuple.14), branch_computations={%region_1.2_spmd, %region_2.3_spmd} | conditional | flops 4302307328 | bytes 61981160 | solution.py:371
  99.0 5.9 %branch_0_fun.1 = bf16[512,4,512]{2,1,0:T(4,128)(2,1)} custom-call(s32[128,128]{1,0:T(8,128)S(1)} %get-tuple-element.19.places_ref, bf16[1152,512]{1,0:T(8,128)(2,1)S(1)} %bitcast.58, bf16[2048,512]{1,0:T(8,128)(2,1)} %get-tuple-element.21.early_ref), custom_call_target="tpu_custom_call" | custom-call | flops 2415919104 | bytes 2359296 | tf_op jit(solution)/shard_map/cond/branch_0_fun/pallas_call | solution.py:320
  (1 shorter events, 0.0 us)
Async XLA Ops:
  2.3 15.5 %all-to-all-start.4 = ((bf16[16,8,128]{2,1,0:T(8,128)(2,1)}), bf16[16,8,128]{2,1,0:T(8,128)(2,1)S(1)}, u32[]{:S(2)}, u32[]{:S(2)}) async-start(bf16[16,8,128]{2,1,0:T(8,128)(2,1)} %bitcast.62), calls=%async_computation.4 | async-start | bytes 65536 | tf_op jit(solution)/shard_map/all_to_all | solution.py:333
  17.8 0.6 copy-start.10
  23.5 10.8 %copy-start.13 = (bf16[16,72,512]{2,1,0:T(8,128)(2,1)S(1)}, bf16[16,72,512]{2,1,0:T(8,128)(2,1)}, u32[]{:S(2)}) copy-start(bf16[16,72,512]{2,1,0:T(8,128)(2,1)} %get-tuple-element.44) | copy-start | bytes 3538948
  28.1 34.5 %copy-start.9 = (bf16[16,72,512]{2,1,0:T(8,128)(2,1)S(1)}, bf16[16,72,512]{2,1,0:T(8,128)(2,1)}, u32[]{:S(2)}) copy-start(bf16[16,72,512]{2,1,0:T(8,128)(2,1)} %get-tuple-element.43) | copy-start | bytes 3538948
  28.1 35.9 %all-to-all-start.6 = ((bf16[16,56,512]{2,1,0:T(8,128)(2,1)}), bf16[16,56,512]{2,1,0:T(8,128)(2,1)S(1)}, u32[]{:S(2)}, u32[]{:S(2)}) async-start(bf16[16,56,512]{2,1,0:T(8,128)(2,1)} %shard_map.52), calls=%async_computation.6 | async-start | bytes 1835008 | tf_op jit(solution)/shard_map/all_to_all | solution.py:333
  34.3 28.4 %collective-permute-start.4 = (bf16[16,72,512]{2,1,0:T(8,128)(2,1)S(1)}, bf16[16,72,512]{2,1,0:T(8,128)(2,1)S(1)}, u32[]{:S(2)}, u32[]{:S(2)}) collective-permute-start(bf16[16,72,512]{2,1,0:T(8,128)(2,1)S(1)} %copy-done.13), channel_id=1, source_target_pairs={{0,16},{16,0},{1,17},{17,1},{2,18},{18,2},{3,19},{19,3},{4,20},{20... | collective-permute-start | bytes 3538952 | tf_op jit(solution)/shard_map/ppermute | solution.py:364
  62.7 8.4 %copy-start.11 = (s32[4,1024]{1,0:T(4,128)S(1)}, s32[4,1024]{1,0:T(4,128)}, u32[]{:S(2)}) copy-start(s32[4,1024]{1,0:T(4,128)} %slots_ref.1) | copy-start | bytes 49156
  62.7 8.4 %copy-start.12 = (s32[4]{0:T(128)S(1)}, s32[4]{0:T(128)}, u32[]{:S(2)}) copy-start(s32[4]{0:T(128)} %counts_ref.1) | copy-start | bytes 52
  64.0 35.0 %all-to-all-start.5 = ((bf16[16,72,512]{2,1,0:T(8,128)(2,1)}), bf16[16,72,512]{2,1,0:T(8,128)(2,1)S(1)}, u32[]{:S(2)}, u32[]{:S(2)}) async-start(bf16[16,72,512]{2,1,0:T(8,128)(2,1)} %add_convert_fusion.4), calls=%async_computation.5 | async-start | bytes 2359296 | tf_op jit(solution)/shard_map/all_to_all | solution.py:333
  69.8 24.6 %collective-permute-start.5 = (bf16[896,512]{1,0:T(8,128)(2,1)S(1)}, bf16[896,512]{1,0:T(8,128)(2,1)S(1)}, u32[]{:S(2)}, u32[]{:S(2)}) collective-permute-start(bf16[896,512]{1,0:T(8,128)(2,1)S(1)} %bitcast.52), channel_id=1, source_target_pairs={{16,0},{17,1},{18,2},{19,3},{20,4},{21,5},{22,6},{23,7},{24,8},{25... | collective-permute-start | bytes 2752520 | tf_op jit(solution)/shard_map/ppermute | solution.py:367
  94.3 0.8 copy-start.7

commit v5 on v4

--- a/solution.py
+++ b/solution.py
@@ -24,7 +24,7 @@
 
 def terms_of(rows, pair):
     total, width = rows.shape
-    block = min(512, total)
+    block = min(2048, total)
     out_width = 2 * pair.shape[2]
     return pl.pallas_call(
         terms_kernel,
@@ -36,6 +36,7 @@
         cost_estimate=pl.CostEstimate(
             flops=2 * total * width * out_width, bytes_accessed=4 * rows.size, transcendentals=0
         ),
+        compiler_params=pltpu.CompilerParams(vmem_limit_bytes=16 << 20),
     )(rows, pair)
 
 
@@ -89,7 +90,8 @@
 
 KINDS = 8
 LANES = 128
-EARLY, LATE = 56, 72
+EARLY, LATE = 64, 64
+ADD_BYTES, EARLY_BYTES = 1<<34, 1<<34
 
 
 def dot(a, b):
@@ -163,8 +165,9 @@
     return jnp.concatenate([mark(rank == upper), mark(rank == lower)], axis=1)
 
 
-def pack_late_kernel(first_rank, plane_ref, flags_ref, terms_ref, send_ref, keep_ref, keys_ref):
-    batch, capacity, _ = send_ref.shape
+def pack_kernel(plane_ref, flags_ref, terms_ref, early_ref, send_ref, keep_ref, keys_ref):
+    batch, early, _ = early_ref.shape
+    late = send_ref.shape[1]
     step = pl.program_id(0)
 
     @pl.when(step == 0)
@@ -175,62 +178,57 @@
     for i in range(batch):
         keys = keys_ref[pl.ds((step * batch + i) * KINDS, KINDS), :]
         second = keys[2:3], keys[3:4]
-        beyond = keys[0:1] - first_rank, keys[1:2] - first_rank
+        beyond = keys[0:1] - early, keys[1:2] - early
         sent = [jnp.where(plane == 0, b, a) for a, b in zip(beyond, second)]
         kept = [jnp.where(plane == 0, a, b) for a, b in zip(beyond, second)]
-        chosen = jnp.concatenate([chosen_rows(capacity, *sent), chosen_rows(capacity, *kept)], axis=0)
-        packed = dot(chosen, terms_ref[i]).astype(send_ref.dtype)
-        send_ref[i] = packed[:capacity]
-        keep_ref[i] = packed[capacity:]
-
-
-def pack_late(plane, flags, terms, first_rank, capacity):
+        chosen = [chosen_rows(late, *sent), chosen_rows(late, *kept), chosen_rows(early, keys[0:1], keys[1:2])]
+        packed = dot(jnp.concatenate(chosen, axis=0), terms_ref[i]).astype(early_ref.dtype)
+        send_ref[i] = packed[:late]
+        keep_ref[i] = packed[late : 2 * late]
+        early_ref[i] = packed[2 * late :]
+
+
+def pack(plane, flags, terms, early, late):
     groups, rows, width = terms.shape
-    batch = 4 if groups % 4 == 0 else 1
-    out = jax.ShapeDtypeStruct((groups, capacity, width), terms.dtype)
-    block = pl.BlockSpec((batch, capacity, width), lambda i: (i, 0, 0))
-    table = pl.BlockSpec(flags.shape, lambda i: (0, 0))
-    return pl.pallas_call(
-        functools.partial(pack_late_kernel, first_rank),
+    batch = 8 if groups % 8 == 0 else 1
+
+    def out(capacity):
+        block = pl.BlockSpec((batch, capacity, width), lambda i: (i, 0, 0))
+        return jax.ShapeDtypeStruct((groups, capacity, width), terms.dtype), block
+
+    shapes, blocks = zip(out(early), out(late), out(late))
+    return pl.pallas_call(
+        pack_kernel,
         grid=(groups // batch,),
-        out_shape=[out, out, jax.ShapeDtypeStruct(flags.shape, jnp.float32)],
+        out_shape=shapes,
         in_specs=[
             pl.BlockSpec(memory_space=pltpu.SMEM),
-            table,
+            pl.BlockSpec(flags.shape, lambda i: (0, 0)),
             pl.BlockSpec((batch, rows, width), lambda i: (i, 0, 0)),
         ],
-        out_specs=[block, block, table],
-        cost_estimate=pl.CostEstimate(
-            flops=4 * groups * capacity * rows * width, bytes_accessed=4 * terms.size, transcendentals=0
-        ),
+        out_specs=blocks,
+        scratch_shapes=[pltpu.VMEM(flags.shape, jnp.float32)],
+        cost_estimate=pl.CostEstimate(
+            flops=2 * groups * (early + 2 * late) * rows * width, bytes_accessed=4 * terms.size, transcendentals=0
+        ),
+        compiler_params=pltpu.CompilerParams(vmem_limit_bytes=16 << 20),
     )(plane, flags, terms)
 
 
-def pack_early_kernel(keys_ref, terms_ref, out_ref):
-    batch, capacity, _ = out_ref.shape
-    step = pl.program_id(0)
-    for i in range(batch):
-        keys = keys_ref[pl.ds((step * batch + i) * KINDS, KINDS), :]
-        chosen = chosen_rows(capacity, keys[0:1], keys[1:2])
-        out_ref[i] = dot(chosen, terms_ref[i]).astype(out_ref.dtype)
-
-
-def pack_early(keys, terms, capacity):
-    groups, rows, width = terms.shape
-    batch = 4 if groups % 4 == 0 else 1
-    return pl.pallas_call(
-        pack_early_kernel,
-        grid=(groups // batch,),
-        out_shape=jax.ShapeDtypeStruct((groups, capacity, width), terms.dtype),
-        in_specs=[
-            pl.BlockSpec(keys.shape, lambda i: (0, 0)),
-            pl.BlockSpec((batch, rows, width), lambda i: (i, 0, 0)),
-        ],
-        out_specs=pl.BlockSpec((batch, capacity, width), lambda i: (i, 0, 0)),
-        cost_estimate=pl.CostEstimate(
-            flops=2 * groups * capacity * rows * width, bytes_accessed=3 * terms.size, transcendentals=0
-        ),
-    )(keys, terms)
+def add_kernel(a_ref, b_ref, out_ref):
+    out_ref[...] = (a_ref[...].astype(jnp.float32) + b_ref[...].astype(jnp.float32)).astype(out_ref.dtype)
+
+
+def add(a, b):
+    vmem = pl.BlockSpec(memory_space=pltpu.VMEM)
+    return pl.pallas_call(
+        add_kernel,
+        out_shape=jax.ShapeDtypeStruct(a.shape, a.dtype),
+        in_specs=[vmem] * 2,
+        out_specs=vmem,
+        cost_estimate=pl.CostEstimate(flops=ADD_BYTES, bytes_accessed=ADD_BYTES, transcendentals=0),
+        compiler_params=pltpu.CompilerParams(vmem_limit_bytes=8 << 20),
+    )(a, b)
 
 
 def places_kernel(own_rows, early, late, plane_ref, slots_ref, column_ref, early_ref, late_ref):
@@ -277,23 +275,31 @@
     )(plane, own_slots, column)
 
 
+BLOCK = 2 * LANES
+
+
+def chosen_places(places_ref, block, total):
+    columns = iota((LANES, total), 1)
+    first = block * BLOCK // LANES
+    picks = [mark(columns == places_ref[:, first + i : first + i + 1]) for i in range(BLOCK // LANES)]
+    return jnp.concatenate(picks, axis=0)
+
+
 def early_kernel(places_ref, own_ref, other_ref, out_ref, table):
     both = own_ref[...].astype(jnp.float32) + other_ref[...].astype(jnp.float32)
     table[...] = both.astype(table.dtype)
-    columns = iota((LANES, table.shape[0]), 1)
-    for block in range(out_ref.shape[0] // LANES):
-        chosen = mark(columns == places_ref[:, block : block + 1])
-        out_ref[block * LANES : (block + 1) * LANES, :] = dot(chosen, table[...]).astype(out_ref.dtype)
+    for block in range(out_ref.shape[0] // BLOCK):
+        chosen = chosen_places(places_ref, block, table.shape[0])
+        out_ref[block * BLOCK : (block + 1) * BLOCK, :] = dot(chosen, table[...]).astype(out_ref.dtype)
 
 
 def late_kernel(places_ref, late_ref, early_ref, out_ref):
     rows, width = early_ref.shape
     share, mine, _ = out_ref.shape
-    per = LANES // mine
-    columns = iota((LANES, late_ref.shape[0]), 1)
-    for block in range(rows // LANES):
-        chosen = mark(columns == places_ref[:, block : block + 1])
-        early = early_ref[block * LANES : (block + 1) * LANES, :].astype(jnp.float32)
+    per = BLOCK // mine
+    for block in range(rows // BLOCK):
+        chosen = chosen_places(places_ref, block, late_ref.shape[0])
+        early = early_ref[block * BLOCK : (block + 1) * BLOCK, :].astype(jnp.float32)
         total = (dot(chosen, late_ref[...]) + early).astype(out_ref.dtype)
         out_ref[block * per : (block + 1) * per] = total.reshape(per, mine, width)
 
@@ -308,7 +314,7 @@
         out_specs=vmem,
         scratch_shapes=[pltpu.VMEM((rows, width), own.dtype)],
         cost_estimate=pl.CostEstimate(
-            flops=2 * slots * rows * width, bytes_accessed=6 * own.size, transcendentals=0
+            flops=EARLY_BYTES, bytes_accessed=EARLY_BYTES, transcendentals=0
         ),
         compiler_params=pltpu.CompilerParams(vmem_limit_bytes=12 << 20),
     )(where, own, other)
@@ -339,8 +345,8 @@
     mine = group_total // groups
     slot_total = slot_rows.shape[1]
     share = slot_total // cuts
-    terms = terms_of(stem_blocks.reshape(group_total * own_rows, width), cap_tensor[0])
-    width = terms.shape[1]
+    stem = stem_blocks.reshape(group_total * own_rows, width)
+    width = 2 * cap_tensor.shape[3]
 
     positions = jnp.arange(slot_total, dtype=jnp.int32)
     marked = jnp.where(positions[None, :] < counts[:, None], slot_rows, -1)
@@ -349,6 +355,7 @@
     turned = lax.dynamic_slice_in_dim(doubled, (me + 1) * share, slot_total, 1)
 
     def all_rows():
+        terms = terms_of(stem, cap_tensor[0])
         return static_plan(terms.reshape(group_total, own_rows, width), turned, cuts)
 
     if cuts != 2 or mine * own_rows != 2 * LANES or LANES % own_rows or groups > LANES:
@@ -356,14 +363,15 @@
 
     early, late = EARLY, LATE
     plane = me[None]
+    terms = terms_of(stem, cap_tensor[0])
     flags = needs(slot_rows, counts, own_rows, early, late, groups)
     flags = exchange(flags.reshape(groups, KINDS, LANES))
     spilled = jnp.max(flags[:, 6, :].astype(jnp.float32)) > 0.0
     by_owner = terms.reshape(groups, mine * own_rows, width)
-    send, keep, keys = pack_late(plane, flags.reshape(groups * KINDS, LANES), by_owner, early, late)
+    first, send, keep = pack(plane, flags.reshape(groups * KINDS, LANES), by_owner, early, late)
     other = lax.ppermute(send, "cuts", [(0, 1), (1, 0)])
-    own_early = exchange(pack_early(keys, by_owner, early)).reshape(groups * early, width)
-    summed = (keep.astype(jnp.float32) + other.astype(jnp.float32)).astype(terms.dtype)
+    own_early = exchange(first).reshape(groups * early, width)
+    own_early, summed = lax.optimization_barrier((own_early, add(keep, other)))
     other_early = lax.ppermute(own_early, "cuts", [(1, 0)])
     own_late = exchange(summed).reshape(groups * late, width)
     where_early, where_late = places(plane, turned[:, (cuts - 1) * share :], own_rows, early, late)

time: 106 us -> 90.7 us (0.86)
  the two profiles are of different devices: /device:TPU:0 before, /device:TPU:15 now
where the time goes in v5:
time: 90.7 us; the launch traced here: 90.1 us
  waiting for transfers between devices  33.4 us (37%)
  Pallas kernels  27.2 us (30%)
  starting transfers between devices  21.5 us (24%)
  local copies, waits for them, and re-layouts  6.63 us (7%)
    all_to_all x3, starting transfers between devices, exchange(): lax.all_to_all(blocks, 'group', split_axis=0, concat_axis=0, tiled=True)  18.1 us
    ppermute x1, waiting for transfers between devices, local(): other = lax.ppermute(send, 'cuts', [(0, 1), (1, 0)])  18 us
    all_to_all x3, waiting for transfers between devices, exchange(): lax.all_to_all(blocks, 'group', split_axis=0, concat_axis=0, tiled=True)  7.89 us
    ppermute x1, waiting for transfers between devices, local(): other_early = lax.ppermute(own_early, 'cuts', [(1, 0)])  7.51 us
    pallas_call x1, Pallas kernels, places(): pl.pallas_call(functools.partial(places_kernel, own_rows, early, late), o...  6.48 us
    pallas_call x1, Pallas kernels, late_part(): pl.pallas_call(late_kernel, out_shape=jax.ShapeDtypeStruct((rows // mine,...  5.66 us
    unnamed x12, local copies, waits for them, and re-layouts  5 us
    pallas_call x1, Pallas kernels, terms_of(): pl.pallas_call(terms_kernel, grid=(total // block,), out_shape=jax.ShapeD...  4.18 us
  transfers between devices with their start and end apart: 5, of which 4 were waited for; matrix products, arithmetic and copies ran while one was open for 3% of the time, Pallas kernels for 19%

profile of v5, /device:TPU:15, one launch (start us, length us, event | category | flops | bytes accessed | tf_op | source)
XLA Modules:
  0.0 90.1 jit_solution(13298220577621592669)
XLA Ops:
  0.0 2.3 %shard_map.48 = bf16[128,128]{1,0:T(8,128)(2,1)} custom-call(s32[4,1024]{1,0:T(4,128)} %slots_ref.1, s32[4]{0:T(128)} %counts_ref.1), custom_call_target="tpu_custom_call" | custom-call | flops 268435456 | bytes 131072 | tf_op jit(solution)/shard_map/pallas_call | solution.py:142
  2.3 6.6 %all-to-all-start.4 = ((bf16[16,8,128]{2,1,0:T(8,128)(2,1)}), bf16[16,8,128]{2,1,0:T(8,128)(2,1)S(1)}, u32[]{:S(2)}, u32[]{:S(2)}) async-start(bf16[16,8,128]{2,1,0:T(8,128)(2,1)} %bitcast.63), calls=%async_computation.4 | async-start | bytes 65536 | tf_op jit(solution)/shard_map/all_to_all | solution.py:339
  8.9 4.2 %shard_map.49 = bf16[4096,512]{1,0:T(8,128)(2,1)S(1)} custom-call(bf16[4096,512]{1,0:T(8,128)(2,1)} %bitcast.58, bf16[2,256,256]{2,1,0:T(8,128)(2,1)} %bitcast.60), custom_call_target="tpu_custom_call" | custom-call | flops 2147483648 | bytes 8388608 | tf_op jit(solution)/shard_map/pallas_call | solution.py:29
  13.1 0.0 copy-start
  13.1 2.0 %copy-done = bf16[4096,512]{1,0:T(8,128)(2,1)} copy-done((bf16[4096,512]{1,0:T(8,128)(2,1)}, bf16[4096,512]{1,0:T(8,128)(2,1)S(1)}, u32[]{:S(2)}) %copy-start) | copy-done | bytes 4194328
  15.1 0.0 all-to-all-done.4
  15.1 0.0 copy-start.1
  15.1 2.2 %copy-done.1 = bf16[4096,512]{1,0:T(8,128)(2,1)S(1)} copy-done((bf16[4096,512]{1,0:T(8,128)(2,1)S(1)}, bf16[4096,512]{1,0:T(8,128)(2,1)}, u32[]{:S(2)}) %copy-start.1) | copy-done | bytes 4194328
  17.2 2.3 %shard_map.50 = (bf16[16,64,512]{2,1,0:T(8,128)(2,1)}, bf16[16,64,512]{2,1,0:T(8,128)(2,1)S(1)}, bf16[16,64,512]{2,1,0:T(8,128)(2,1)S(1)}) custom-call(s32[1]{0:T(128)} %bitcast.20.plane_ref, bf16[128,128]{1,0:T(8,128)(2,1)S(1)} %bitcast.57, bf16[16,256,512]{2,1,0:T(8,128)(2,1)S(1)} %bitcast.49), custom_call_target="tpu_custom_call" | custom-call | flops 805306368 | bytes 8388608 | tf_op jit(solution)/shard_map/pallas_call | solution.py:200
  19.5 0.2 collective-permute-start.4
  19.7 6.3 %all-to-all-start.5 = ((bf16[16,64,512]{2,1,0:T(8,128)(2,1)}), bf16[16,64,512]{2,1,0:T(8,128)(2,1)S(1)}, u32[]{:S(2)}, u32[]{:S(2)}) async-start(bf16[16,64,512]{2,1,0:T(8,128)(2,1)} %get-tuple-element.48), calls=%async_computation.5 | async-start | bytes 2097152 | tf_op jit(solution)/shard_map/all_to_all | solution.py:339
  26.0 18.0 %collective-permute-done.4.b_ref = bf16[16,64,512]{2,1,0:T(8,128)(2,1)} collective-permute-done((bf16[16,64,512]{2,1,0:T(8,128)(2,1)S(1)}, bf16[16,64,512]{2,1,0:T(8,128)(2,1)}, u32[]{:S(2)}, u32[]{:S(2)}) %collective-permute-start.4) | collective-permute-done | bytes 1048608 | tf_op jit(solution)/shard_map/ppermute | solution.py:372
  44.0 0.0 copy-start.12
  44.0 0.0 copy-start.13
  44.0 2.5 %shard_map.51 = bf16[16,64,512]{2,1,0:T(8,128)(2,1)} custom-call(bf16[16,64,512]{2,1,0:T(8,128)(2,1)S(1)} %get-tuple-element.49.a_ref, bf16[16,64,512]{2,1,0:T(8,128)(2,1)} %collective-permute-done.4.b_ref), custom_call_target="tpu_custom_call" | custom-call | flops 17179869184 | bytes 17179869184 | tf_op jit(solution)/shard_map/pallas_call | solution.py:224
  46.5 4.4 %all-to-all-done.5 = bf16[16,64,512]{2,1,0:T(8,128)(2,1)S(1)} async-done(((bf16[16,64,512]{2,1,0:T(8,128)(2,1)}), bf16[16,64,512]{2,1,0:T(8,128)(2,1)S(1)}, u32[]{:S(2)}, u32[]{:S(2)}) %all-to-all-start.5) | async-done | bytes 1048608 | tf_op jit(solution)/shard_map/all_to_all | solution.py:339
  50.9 3.2 %collective-permute-start.5 = (bf16[1024,512]{1,0:T(8,128)(2,1)S(1)}, bf16[1024,512]{1,0:T(8,128)(2,1)S(1)}, u32[]{:S(2)}, u32[]{:S(2)}) collective-permute-start(bf16[1024,512]{1,0:T(8,128)(2,1)S(1)} %bitcast.51), channel_id=1, source_target_pairs={{16,0},{17,1},{18,2},{19,3},{20,4},{21,5},{22,6},{23,7},{24,8},{25... | collective-permute-start | bytes 3145736 | tf_op jit(solution)/shard_map/ppermute | solution.py:375
  54.1 0.0 copy-done.12
  54.1 0.0 copy-done.13
  54.1 0.1 fusion.5
  54.2 5.2 %all-to-all-start.6 = ((bf16[16,64,512]{2,1,0:T(8,128)(2,1)}), bf16[16,64,512]{2,1,0:T(8,128)(2,1)}, u32[]{:S(2)}, u32[]{:S(2)}) async-start(bf16[16,64,512]{2,1,0:T(8,128)(2,1)} %shard_map.51), calls=%async_computation.6 | async-start | bytes 2097152 | tf_op jit(solution)/shard_map/all_to_all | solution.py:339
  59.5 0.6 slice_bitcast_fusion.8
  60.1 0.1 copy.22
  60.2 0.2 reshape.43
  60.4 0.7 copy.23
  61.1 6.5 %shard_map.52 = (s32[128,128]{1,0:T(8,128)}, s32[128,128]{1,0:T(8,128)S(1)}) custom-call(s32[1]{0:T(128)} %bitcast.20.plane_ref, s32[4,512]{1,0:T(4,128)} %get-tuple-element.68.slots_ref, s32[128,16]{1,0:T(8,128)} %bitcast.62), custom_call_target="tpu_custom_call" | custom-call | flops 268435456 | bytes 262144 | tf_op jit(solution)/shard_map/pallas_call | solution.py:269
  67.6 0.6 slice_reduce_fusion
  68.9 7.5 %collective-permute-done.5.other_ref = bf16[1024,512]{1,0:T(8,128)(2,1)S(1)} collective-permute-done((bf16[1024,512]{1,0:T(8,128)(2,1)S(1)}, bf16[1024,512]{1,0:T(8,128)(2,1)S(1)}, u32[]{:S(2)}, u32[]{:S(2)}) %collective-permute-start.5) | collective-permute-done | bytes 1048608 | tf_op jit(solution)/shard_map/ppermute | solution.py:375
  76.4 0.0 copy-start.9
  76.4 0.8 copy-done.9
  77.2 0.0 copy-start.11
  77.2 3.8 %shard_map.53 = bf16[2048,512]{1,0:T(8,128)(2,1)} custom-call(s32[128,128]{1,0:T(8,128)S(1)} %copy-done.9, bf16[1024,512]{1,0:T(8,128)(2,1)S(1)} %bitcast.52, bf16[1024,512]{1,0:T(8,128)(2,1)S(1)} %collective-permute-done.5.other_ref), custom_call_target="tpu_custom_call" | custom-call | flops 17179869184 | bytes 17179869184 | tf_op jit(solution)/shard_map/pallas_call | solution.py:310
  81.0 3.5 %all-to-all-done.6 = bf16[16,64,512]{2,1,0:T(8,128)(2,1)} async-done(((bf16[16,64,512]{2,1,0:T(8,128)(2,1)}), bf16[16,64,512]{2,1,0:T(8,128)(2,1)}, u32[]{:S(2)}, u32[]{:S(2)}) %all-to-all-start.6) | async-done | bytes 1048608 | tf_op jit(solution)/shard_map/all_to_all | solution.py:339
  84.4 0.0 copy-done.11
  84.4 5.7 %conditional.1 = (bf16[512,4,512]{2,1,0:T(4,128)(2,1)}) conditional(s32[]{:T(128)} %convert_element_type.40, (bf16[16,64,512]{2,1,0:T(8,128)(2,1)}, s32[128,128]{1,0:T(8,128)S(1)}, bf16[2048,512]{1,0:T(8,128)(2,1)}) %tuple.15, (bf16[1,2,256,256]{3,2,1,0:T(8,128)(2,1)S(1)}, bf16[4096,512]{1,0:T(8,128)(2,1)}, s32[4,1024]{1,0:T(4,128)S(1)}) %tuple.33), branch_computations={%region_1.2_spmd, %region_2.3_spmd} | conditional | flops 6449790976 | bytes 70369768 | solution.py:379
  84.4 5.7 %branch_0_fun.1 = bf16[512,4,512]{2,1,0:T(4,128)(2,1)} custom-call(s32[128,128]{1,0:T(8,128)S(1)} %get-tuple-element.21.places_ref, bf16[1024,512]{1,0:T(8,128)(2,1)} %bitcast.late_ref, bf16[2048,512]{1,0:T(8,128)(2,1)} %get-tuple-element.23.early_ref), custom_call_target="tpu_custom_call" | custom-call | flops 2147483648 | bytes 2097152 | tf_op jit(solution)/shard_map/cond/branch_0_fun/pallas_call | solution.py:326
  (1 shorter events, 0.0 us)
Async XLA Ops:
  2.3 12.7 %all-to-all-start.4 = ((bf16[16,8,128]{2,1,0:T(8,128)(2,1)}), bf16[16,8,128]{2,1,0:T(8,128)(2,1)S(1)}, u32[]{:S(2)}, u32[]{:S(2)}) async-start(bf16[16,8,128]{2,1,0:T(8,128)(2,1)} %bitcast.63), calls=%async_computation.4 | async-start | bytes 65536 | tf_op jit(solution)/shard_map/all_to_all | solution.py:339
  13.1 2.0 %copy-start = (bf16[4096,512]{1,0:T(8,128)(2,1)}, bf16[4096,512]{1,0:T(8,128)(2,1)S(1)}, u32[]{:S(2)}) copy-start(bf16[4096,512]{1,0:T(8,128)(2,1)S(1)} %shard_map.49) | copy-start | bytes 12582916
  15.1 2.2 %copy-start.1 = (bf16[4096,512]{1,0:T(8,128)(2,1)S(1)}, bf16[4096,512]{1,0:T(8,128)(2,1)}, u32[]{:S(2)}) copy-start(bf16[4096,512]{1,0:T(8,128)(2,1)} %copy-done) | copy-start | bytes 12582916
  19.5 24.5 %collective-permute-start.4 = (bf16[16,64,512]{2,1,0:T(8,128)(2,1)S(1)}, bf16[16,64,512]{2,1,0:T(8,128)(2,1)}, u32[]{:S(2)}, u32[]{:S(2)}) collective-permute-start(bf16[16,64,512]{2,1,0:T(8,128)(2,1)S(1)} %get-tuple-element.50), channel_id=1, source_target_pairs={{0,16},{16,0},{1,17},{17,1},{2,18},{18,2},{3,19},{19,3},{4,20},{20... | collective-permute-start | bytes 3145736 | tf_op jit(solution)/shard_map/ppermute | solution.py:372
  19.7 31.2 %all-to-all-start.5 = ((bf16[16,64,512]{2,1,0:T(8,128)(2,1)}), bf16[16,64,512]{2,1,0:T(8,128)(2,1)S(1)}, u32[]{:S(2)}, u32[]{:S(2)}) async-start(bf16[16,64,512]{2,1,0:T(8,128)(2,1)} %get-tuple-element.48), calls=%async_computation.5 | async-start | bytes 2097152 | tf_op jit(solution)/shard_map/all_to_all | solution.py:339
  44.0 10.1 %copy-start.12 = (s32[4,1024]{1,0:T(4,128)S(1)}, s32[4,1024]{1,0:T(4,128)}, u32[]{:S(2)}) copy-start(s32[4,1024]{1,0:T(4,128)} %slots_ref.1) | copy-start | bytes 49156
  44.0 10.1 %copy-start.13 = (s32[4]{0:T(128)S(1)}, s32[4]{0:T(128)}, u32[]{:S(2)}) copy-start(s32[4]{0:T(128)} %counts_ref.1) | copy-start | bytes 52
  50.9 25.5 %collective-permute-start.5 = (bf16[1024,512]{1,0:T(8,128)(2,1)S(1)}, bf16[1024,512]{1,0:T(8,128)(2,1)S(1)}, u32[]{:S(2)}, u32[]{:S(2)}) collective-permute-start(bf16[1024,512]{1,0:T(8,128)(2,1)S(1)} %bitcast.51), channel_id=1, source_target_pairs={{16,0},{17,1},{18,2},{19,3},{20,4},{21,5},{22,6},{23,7},{24,8},{25... | collective-permute-start | bytes 3145736 | tf_op jit(solution)/shard_map/ppermute | solution.py:375
  54.2 30.2 %all-to-all-start.6 = ((bf16[16,64,512]{2,1,0:T(8,128)(2,1)}), bf16[16,64,512]{2,1,0:T(8,128)(2,1)}, u32[]{:S(2)}, u32[]{:S(2)}) async-start(bf16[16,64,512]{2,1,0:T(8,128)(2,1)} %shard_map.51), calls=%async_computation.6 | async-start | bytes 2097152 | tf_op jit(solution)/shard_map/all_to_all | solution.py:339
  76.4 0.8 copy-start.9
  77.2 7.2 %copy-start.11 = (bf16[1,2,256,256]{3,2,1,0:T(8,128)(2,1)S(1)}, bf16[1,2,256,256]{3,2,1,0:T(8,128)(2,1)}, u32[]{:S(2)}) copy-start(bf16[1,2,256,256]{3,2,1,0:T(8,128)(2,1)} %param.7) | copy-start | bytes 786436

commit v6 on v5

--- a/solution.py
+++ b/solution.py
@@ -37,7 +37,7 @@
             flops=2 * total * width * out_width, bytes_accessed=4 * rows.size, transcendentals=0
         ),
         compiler_params=pltpu.CompilerParams(vmem_limit_bytes=16 << 20),
-    )(rows, pair)
+    )(pltpu.with_memory_space_constraint(rows, pltpu.HBM), pltpu.with_memory_space_constraint(pair, pltpu.HBM))
 
 
 def select_kernel(block, share, terms_ref, slots_ref, *outs):
@@ -90,6 +90,7 @@
 
 KINDS = 8
 LANES = 128
+STEP = 4
 EARLY, LATE = 64, 64
 ADD_BYTES, EARLY_BYTES = 1<<34, 1<<34
 
@@ -247,9 +248,11 @@
     shift = plane_ref[0] * early
     group = iota((LANES, 1), 0) % mine
     lane = iota((LANES, LANES), 1)
-    in_early = jnp.full((LANES, LANES), -1, jnp.int32)
-    in_late = in_early
     for block in range(mine * share // LANES):
+        at, spot = block // STEP, block % STEP
+        if spot == 0:
+            in_early = jnp.full((LANES, LANES), -1, jnp.int32)
+            in_late = in_early
         slots = column_ref[:, block : block + 1]
         source = slots // own_rows
         row = jnp.where(slots >= 0, group * own_rows + slots % own_rows, -1)
@@ -257,10 +260,11 @@
         found = jnp.where(lane == source, looked, 0.0)
         rank = jnp.sum(found, axis=1, keepdims=True).astype(jnp.int32) + shift
         live, low = slots >= 0, rank < early
-        in_early = jnp.where((lane == block) & live & low, source * early + rank, in_early)
-        in_late = jnp.where((lane == block) & live & ~low, source * late + rank - early, in_late)
-    early_ref[...] = in_early
-    late_ref[...] = in_late
+        in_early = jnp.where((lane == spot) & live & low, source * early + rank, in_early)
+        in_late = jnp.where((lane == spot) & live & ~low, source * late + rank - early, in_late)
+        if spot == STEP - 1:
+            early_ref[at] = in_early
+            late_ref[at] = in_late
 
 
 def places(plane, own_slots, own_rows, early, late):
@@ -268,66 +272,63 @@
     vmem = pl.BlockSpec(memory_space=pltpu.VMEM)
     return pl.pallas_call(
         functools.partial(places_kernel, own_rows, early, late),
-        out_shape=[jax.ShapeDtypeStruct((LANES, LANES), jnp.int32)] * 2,
+        out_shape=[jax.ShapeDtypeStruct((own_slots.size // (STEP * LANES), LANES, LANES), jnp.int32)] * 2,
         in_specs=[pl.BlockSpec(memory_space=pltpu.SMEM), vmem, vmem],
         out_specs=[vmem] * 2,
         cost_estimate=pl.CostEstimate(flops=1 << 28, bytes_accessed=1 << 18, transcendentals=0),
     )(plane, own_slots, column)
 
 
-BLOCK = 2 * LANES
-
-
-def chosen_places(places_ref, block, total):
+def chosen_places(places_ref, total):
     columns = iota((LANES, total), 1)
-    first = block * BLOCK // LANES
-    picks = [mark(columns == places_ref[:, first + i : first + i + 1]) for i in range(BLOCK // LANES)]
-    return jnp.concatenate(picks, axis=0)
+    return jnp.concatenate([mark(columns == places_ref[0, :, i : i + 1]) for i in range(STEP)], axis=0)
 
 
 def early_kernel(places_ref, own_ref, other_ref, out_ref, table):
-    both = own_ref[...].astype(jnp.float32) + other_ref[...].astype(jnp.float32)
-    table[...] = both.astype(table.dtype)
-    for block in range(out_ref.shape[0] // BLOCK):
-        chosen = chosen_places(places_ref, block, table.shape[0])
-        out_ref[block * BLOCK : (block + 1) * BLOCK, :] = dot(chosen, table[...]).astype(out_ref.dtype)
+    @pl.when(pl.program_id(0) == 0)
+    def _():
+        both = own_ref[...].astype(jnp.float32) + other_ref[...].astype(jnp.float32)
+        table[...] = both.astype(table.dtype)
+
+    out_ref[...] = dot(chosen_places(places_ref, table.shape[0]), table[...]).astype(out_ref.dtype)
 
 
 def late_kernel(places_ref, late_ref, early_ref, out_ref):
-    rows, width = early_ref.shape
-    share, mine, _ = out_ref.shape
-    per = BLOCK // mine
-    for block in range(rows // BLOCK):
-        chosen = chosen_places(places_ref, block, late_ref.shape[0])
-        early = early_ref[block * BLOCK : (block + 1) * BLOCK, :].astype(jnp.float32)
-        total = (dot(chosen, late_ref[...]) + early).astype(out_ref.dtype)
-        out_ref[block * per : (block + 1) * per] = total.reshape(per, mine, width)
-
-
-def early_part(where, own, other, slots):
+    total = dot(chosen_places(places_ref, late_ref.shape[0]), late_ref[...]) + early_ref[...].astype(jnp.float32)
+    out_ref[...] = total.astype(out_ref.dtype).reshape(out_ref.shape)
+
+
+def early_part(where, own, other):
     rows, width = own.shape
-    vmem = pl.BlockSpec(memory_space=pltpu.VMEM)
+    blocks = where.shape[0]
+    whole = pl.BlockSpec(own.shape, lambda i: (0, 0))
+    slots = blocks * STEP * LANES
     return pl.pallas_call(
         early_kernel,
+        grid=(blocks,),
         out_shape=jax.ShapeDtypeStruct((slots, width), own.dtype),
-        in_specs=[vmem] * 3,
-        out_specs=vmem,
+        in_specs=[pl.BlockSpec((1, LANES, LANES), lambda i: (i, 0, 0)), whole, whole],
+        out_specs=pl.BlockSpec((STEP * LANES, width), lambda i: (i, 0)),
         scratch_shapes=[pltpu.VMEM((rows, width), own.dtype)],
-        cost_estimate=pl.CostEstimate(
-            flops=EARLY_BYTES, bytes_accessed=EARLY_BYTES, transcendentals=0
-        ),
+        cost_estimate=pl.CostEstimate(flops=EARLY_BYTES, bytes_accessed=EARLY_BYTES, transcendentals=0),
         compiler_params=pltpu.CompilerParams(vmem_limit_bytes=12 << 20),
     )(where, own, other)
 
 
 def late_part(where, late, early, mine):
     rows, width = early.shape
-    vmem = pl.BlockSpec(memory_space=pltpu.VMEM)
+    blocks = where.shape[0]
+    step = STEP * LANES
     return pl.pallas_call(
         late_kernel,
+        grid=(blocks,),
         out_shape=jax.ShapeDtypeStruct((rows // mine, mine, width), early.dtype),
-        in_specs=[vmem] * 3,
-        out_specs=vmem,
+        in_specs=[
+            pl.BlockSpec((1, LANES, LANES), lambda i: (i, 0, 0)),
+            pl.BlockSpec(late.shape, lambda i: (0, 0)),
+            pl.BlockSpec((step, width), lambda i: (i, 0)),
+        ],
+        out_specs=pl.BlockSpec((step // mine, mine, width), lambda i: (i, 0, 0)),
         cost_estimate=pl.CostEstimate(
             flops=2 * rows * late.shape[0] * width, bytes_accessed=4 * late.size, transcendentals=0
         ),
@@ -346,7 +347,8 @@
     slot_total = slot_rows.shape[1]
     share = slot_total // cuts
     stem = stem_blocks.reshape(group_total * own_rows, width)
-    width = 2 * cap_tensor.shape[3]
+    terms = terms_of(stem, cap_tensor[0])
+    width = terms.shape[1]
 
     positions = jnp.arange(slot_total, dtype=jnp.int32)
     marked = jnp.where(positions[None, :] < counts[:, None], slot_rows, -1)
@@ -355,15 +357,14 @@
     turned = lax.dynamic_slice_in_dim(doubled, (me + 1) * share, slot_total, 1)
 
     def all_rows():
-        terms = terms_of(stem, cap_tensor[0])
         return static_plan(terms.reshape(group_total, own_rows, width), turned, cuts)
 
-    if cuts != 2 or mine * own_rows != 2 * LANES or LANES % own_rows or groups > LANES:
+    unfit = mine * own_rows != 2 * LANES or LANES % own_rows or groups > LANES or share * mine % (STEP * LANES)
+    if cuts != 2 or unfit:
         return all_rows()
 
     early, late = EARLY, LATE
     plane = me[None]
-    terms = terms_of(stem, cap_tensor[0])
     flags = needs(slot_rows, counts, own_rows, early, late, groups)
     flags = exchange(flags.reshape(groups, KINDS, LANES))
     spilled = jnp.max(flags[:, 6, :].astype(jnp.float32)) > 0.0
@@ -375,7 +376,7 @@
     other_early = lax.ppermute(own_early, "cuts", [(1, 0)])
     own_late = exchange(summed).reshape(groups * late, width)
     where_early, where_late = places(plane, turned[:, (cuts - 1) * share :], own_rows, early, late)
-    sums = early_part(where_early, own_early, other_early, share * mine)
+    sums = early_part(where_early, own_early, other_early)
     return lax.cond(spilled, all_rows, lambda: late_part(where_late, own_late, sums, mine))
 
 

time: 90.7 us -> 89.1 us (0.982)
  the two profiles are of different devices: /device:TPU:15 before, /device:TPU:0 now
where the time goes in v6:
time: 89.1 us; the launch traced here: 87.6 us
  waiting for transfers between devices  31.3 us (35%)
  Pallas kernels  30.2 us (34%)
  starting transfers between devices  21.9 us (25%)
  local copies, waits for them, and re-layouts  2.6 us (3%)
    all_to_all x3, starting transfers between devices, exchange(): lax.all_to_all(blocks, 'group', split_axis=0, concat_axis=0, tiled=True)  19.1 us
    ppermute x1, waiting for transfers between devices, local(): other = lax.ppermute(send, 'cuts', [(0, 1), (1, 0)])  18.5 us
    ppermute x1, waiting for transfers between devices, local(): other_early = lax.ppermute(own_early, 'cuts', [(1, 0)])  9.69 us
    pallas_call x1, Pallas kernels, places(): pl.pallas_call(functools.partial(places_kernel, own_rows, early, late), o...  6.58 us
    pallas_call x1, Pallas kernels, terms_of(): pl.pallas_call(terms_kernel, grid=(total // block,), out_shape=jax.ShapeD...  5.5 us
    pallas_call x1, Pallas kernels, late_part(): pl.pallas_call(late_kernel, grid=(blocks,), out_shape=jax.ShapeDtypeStruc...  5.4 us
    pallas_call x1, Pallas kernels, early_part(): pl.pallas_call(early_kernel, grid=(blocks,), out_shape=jax.ShapeDtypeStru...  4.11 us
    pallas_call x1, Pallas kernels, pack(): pl.pallas_call(pack_kernel, grid=(groups // batch,), out_shape=shapes, in...  3.85 us
  transfers between devices with their start and end apart: 5, of which 4 were waited for; matrix products, arithmetic and copies ran while one was open for 3% of the time, Pallas kernels for 21%

profile of v6, /device:TPU:0, one launch (start us, length us, event | category | flops | bytes accessed | tf_op | source)
XLA Modules:
  0.0 87.6 jit_solution(14976911039125937236)
XLA Ops:
  0.0 2.3 %shard_map.48 = bf16[128,128]{1,0:T(8,128)(2,1)} custom-call(s32[4,1024]{1,0:T(4,128)} %slots_ref.1, s32[4]{0:T(128)} %counts_ref.1), custom_call_target="tpu_custom_call" | custom-call | flops 268435456 | bytes 131072 | tf_op jit(solution)/shard_map/pallas_call | solution.py:143
  2.3 7.4 %all-to-all-start.4 = ((bf16[16,8,128]{2,1,0:T(8,128)(2,1)}), bf16[16,8,128]{2,1,0:T(8,128)(2,1)S(1)}, u32[]{:S(2)}, u32[]{:S(2)}) async-start(bf16[16,8,128]{2,1,0:T(8,128)(2,1)} %bitcast.61), calls=%async_computation.4 | async-start | bytes 65536 | tf_op jit(solution)/shard_map/all_to_all | solution.py:340
  9.7 5.5 %shard_map.49 = bf16[4096,512]{1,0:T(8,128)(2,1)} custom-call(bf16[4096,512]{1,0:T(8,128)(2,1)} %bitcast.57, bf16[2,256,256]{2,1,0:T(8,128)(2,1)} %bitcast.59), custom_call_target="tpu_custom_call" | custom-call | flops 2147483648 | bytes 8388608 | tf_op jit(solution)/shard_map/pallas_call | solution.py:29
  15.2 1.1 %all-to-all-done.4 = bf16[16,8,128]{2,1,0:T(8,128)(2,1)S(1)} async-done(((bf16[16,8,128]{2,1,0:T(8,128)(2,1)}), bf16[16,8,128]{2,1,0:T(8,128)(2,1)S(1)}, u32[]{:S(2)}, u32[]{:S(2)}) %all-to-all-start.4) | async-done | bytes 32800 | tf_op jit(solution)/shard_map/all_to_all | solution.py:340
  16.3 3.9 %shard_map.50 = (bf16[16,64,512]{2,1,0:T(8,128)(2,1)}, bf16[16,64,512]{2,1,0:T(8,128)(2,1)S(1)}, bf16[16,64,512]{2,1,0:T(8,128)(2,1)S(1)}) custom-call(s32[1]{0:T(128)} %bitcast.19.plane_ref, bf16[128,128]{1,0:T(8,128)(2,1)S(1)} %bitcast.54, bf16[16,256,512]{2,1,0:T(8,128)(2,1)} %bitcast.55), custom_call_target="tpu_custom_call" | custom-call | flops 805306368 | bytes 8388608 | tf_op jit(solution)/shard_map/pallas_call | solution.py:201
  20.2 1.5 %collective-permute-start.4 = (bf16[16,64,512]{2,1,0:T(8,128)(2,1)S(1)}, bf16[16,64,512]{2,1,0:T(8,128)(2,1)}, u32[]{:S(2)}, u32[]{:S(2)}) collective-permute-start(bf16[16,64,512]{2,1,0:T(8,128)(2,1)S(1)} %get-tuple-element.47), channel_id=1, source_target_pairs={{0,16},{16,0},{1,17},{17,1},{2,18},{18,2},{3,19},{19,3},{4,20},{20... | collective-permute-start | bytes 3145736 | tf_op jit(solution)/shard_map/ppermute | solution.py:373
  21.7 4.9 %all-to-all-start.5 = ((bf16[16,64,512]{2,1,0:T(8,128)(2,1)}), bf16[16,64,512]{2,1,0:T(8,128)(2,1)S(1)}, u32[]{:S(2)}, u32[]{:S(2)}) async-start(bf16[16,64,512]{2,1,0:T(8,128)(2,1)} %get-tuple-element.45), calls=%async_computation.5 | async-start | bytes 2097152 | tf_op jit(solution)/shard_map/all_to_all | solution.py:340
  26.6 18.5 %collective-permute-done.4.b_ref = bf16[16,64,512]{2,1,0:T(8,128)(2,1)} collective-permute-done((bf16[16,64,512]{2,1,0:T(8,128)(2,1)S(1)}, bf16[16,64,512]{2,1,0:T(8,128)(2,1)}, u32[]{:S(2)}, u32[]{:S(2)}) %collective-permute-start.4) | collective-permute-done | bytes 1048608 | tf_op jit(solution)/shard_map/ppermute | solution.py:373
  45.1 0.0 copy-start.9
  45.1 0.0 copy-start.10
  45.1 2.5 %shard_map.51 = bf16[16,64,512]{2,1,0:T(8,128)(2,1)} custom-call(bf16[16,64,512]{2,1,0:T(8,128)(2,1)S(1)} %get-tuple-element.46.a_ref, bf16[16,64,512]{2,1,0:T(8,128)(2,1)} %collective-permute-done.4.b_ref), custom_call_target="tpu_custom_call" | custom-call | flops 17179869184 | bytes 17179869184 | tf_op jit(solution)/shard_map/pallas_call | solution.py:225
  47.5 2.0 %all-to-all-done.5 = bf16[16,64,512]{2,1,0:T(8,128)(2,1)S(1)} async-done(((bf16[16,64,512]{2,1,0:T(8,128)(2,1)}), bf16[16,64,512]{2,1,0:T(8,128)(2,1)S(1)}, u32[]{:S(2)}, u32[]{:S(2)}) %all-to-all-start.5) | async-done | bytes 1048608 | tf_op jit(solution)/shard_map/all_to_all | solution.py:340
  49.5 1.3 %collective-permute-start.5 = (bf16[1024,512]{1,0:T(8,128)(2,1)S(1)}, bf16[1024,512]{1,0:T(8,128)(2,1)S(1)}, u32[]{:S(2)}, u32[]{:S(2)}) collective-permute-start(bf16[1024,512]{1,0:T(8,128)(2,1)S(1)} %bitcast.48), channel_id=1, source_target_pairs={{16,0},{17,1},{18,2},{19,3},{20,4},{21,5},{22,6},{23,7},{24,8},{25... | collective-permute-start | bytes 3145736 | tf_op jit(solution)/shard_map/ppermute | solution.py:376
  50.8 0.0 copy-done.9
  50.8 0.0 copy-done.10
  50.9 0.1 fusion.5
  51.0 6.9 %all-to-all-start.6 = ((bf16[16,64,512]{2,1,0:T(8,128)(2,1)}), bf16[16,64,512]{2,1,0:T(8,128)(2,1)S(1)}, u32[]{:S(2)}, u32[]{:S(2)}) async-start(bf16[16,64,512]{2,1,0:T(8,128)(2,1)} %shard_map.51), calls=%async_computation.6 | async-start | bytes 2097152 | tf_op jit(solution)/shard_map/all_to_all | solution.py:340
  57.8 0.6 slice_bitcast_fusion.8
  58.4 0.1 copy.22
  58.6 0.2 reshape.43
  58.8 0.7 copy.23
  59.5 6.6 %shard_map.52 = (s32[4,128,128]{2,1,0:T(8,128)}, s32[4,128,128]{2,1,0:T(8,128)S(1)}) custom-call(s32[1]{0:T(128)} %bitcast.19.plane_ref, s32[4,512]{1,0:T(4,128)} %get-tuple-element.65.slots_ref, s32[128,16]{1,0:T(8,128)} %bitcast.60), custom_call_target="tpu_custom_call" | custom-call | flops 268435456 | bytes 262144 | tf_op jit(solution)/shard_map/pallas_call | solution.py:273
  66.1 0.7 slice_reduce_fusion
  67.4 9.7 %collective-permute-done.5.other_ref = bf16[1024,512]{1,0:T(8,128)(2,1)S(1)} collective-permute-done((bf16[1024,512]{1,0:T(8,128)(2,1)S(1)}, bf16[1024,512]{1,0:T(8,128)(2,1)S(1)}, u32[]{:S(2)}, u32[]{:S(2)}) %collective-permute-start.5) | collective-permute-done | bytes 1048608 | tf_op jit(solution)/shard_map/ppermute | solution.py:376
  77.1 0.0 copy-start.7
  77.1 0.9 %copy-done.7 = s32[4,128,128]{2,1,0:T(8,128)S(1)} copy-done((s32[4,128,128]{2,1,0:T(8,128)S(1)}, s32[4,128,128]{2,1,0:T(8,128)}, u32[]{:S(2)}) %copy-start.7) | copy-done | bytes 262168
  78.0 4.1 %shard_map.53 = bf16[2048,512]{1,0:T(8,128)(2,1)} custom-call(s32[4,128,128]{2,1,0:T(8,128)S(1)} %copy-done.7, bf16[1024,512]{1,0:T(8,128)(2,1)S(1)} %bitcast.49, bf16[1024,512]{1,0:T(8,128)(2,1)S(1)} %collective-permute-done.5.other_ref), custom_call_target="tpu_custom_call" | custom-call | flops 17179869184 | bytes 17179869184 | tf_op jit(solution)/shard_map/pallas_call | solution.py:306
  82.2 0.0 all-to-all-done.6
  82.2 5.4 %conditional.1 = (bf16[512,4,512]{2,1,0:T(4,128)(2,1)}) conditional(s32[]{:T(128)} %convert_element_type.40, (bf16[16,64,512]{2,1,0:T(8,128)(2,1)S(1)}, s32[4,128,128]{2,1,0:T(8,128)S(1)}, bf16[2048,512]{1,0:T(8,128)(2,1)}) %tuple.15, (bf16[4096,512]{1,0:T(8,128)(2,1)}, s32[4,1024]{1,0:T(4,128)S(1)}) %tuple.16), branch_computations={%region_1.2_spmd, %region_2.3_spmd} | conditional | flops 4302307328 | bytes 61981160 | solution.py:380
  82.2 5.4 %branch_0_fun.1 = bf16[512,4,512]{2,1,0:T(4,128)(2,1)} custom-call(s32[4,128,128]{2,1,0:T(8,128)S(1)} %get-tuple-element.19.places_ref, bf16[1024,512]{1,0:T(8,128)(2,1)S(1)} %bitcast.58, bf16[2048,512]{1,0:T(8,128)(2,1)} %get-tuple-element.21.early_ref), custom_call_target="tpu_custom_call" | custom-call | flops 2147483648 | bytes 2097152 | tf_op jit(solution)/shard_map/cond/branch_0_fun/pallas_call | solution.py:322
  (1 shorter events, 0.0 us)
Async XLA Ops:
  2.3 14.0 %all-to-all-start.4 = ((bf16[16,8,128]{2,1,0:T(8,128)(2,1)}), bf16[16,8,128]{2,1,0:T(8,128)(2,1)S(1)}, u32[]{:S(2)}, u32[]{:S(2)}) async-start(bf16[16,8,128]{2,1,0:T(8,128)(2,1)} %bitcast.61), calls=%async_computation.4 | async-start | bytes 65536 | tf_op jit(solution)/shard_map/all_to_all | solution.py:340
  20.2 24.9 %collective-permute-start.4 = (bf16[16,64,512]{2,1,0:T(8,128)(2,1)S(1)}, bf16[16,64,512]{2,1,0:T(8,128)(2,1)}, u32[]{:S(2)}, u32[]{:S(2)}) collective-permute-start(bf16[16,64,512]{2,1,0:T(8,128)(2,1)S(1)} %get-tuple-element.47), channel_id=1, source_target_pairs={{0,16},{16,0},{1,17},{17,1},{2,18},{18,2},{3,19},{19,3},{4,20},{20... | collective-permute-start | bytes 3145736 | tf_op jit(solution)/shard_map/ppermute | solution.py:373
  21.7 27.8 %all-to-all-start.5 = ((bf16[16,64,512]{2,1,0:T(8,128)(2,1)}), bf16[16,64,512]{2,1,0:T(8,128)(2,1)S(1)}, u32[]{:S(2)}, u32[]{:S(2)}) async-start(bf16[16,64,512]{2,1,0:T(8,128)(2,1)} %get-tuple-element.45), calls=%async_computation.5 | async-start | bytes 2097152 | tf_op jit(solution)/shard_map/all_to_all | solution.py:340
  45.1 5.8 %copy-start.9 = (s32[4,1024]{1,0:T(4,128)S(1)}, s32[4,1024]{1,0:T(4,128)}, u32[]{:S(2)}) copy-start(s32[4,1024]{1,0:T(4,128)} %slots_ref.1) | copy-start | bytes 49156
  45.1 5.8 %copy-start.10 = (s32[4]{0:T(128)S(1)}, s32[4]{0:T(128)}, u32[]{:S(2)}) copy-start(s32[4]{0:T(128)} %counts_ref.1) | copy-start | bytes 52
  49.5 27.6 %collective-permute-start.5 = (bf16[1024,512]{1,0:T(8,128)(2,1)S(1)}, bf16[1024,512]{1,0:T(8,128)(2,1)S(1)}, u32[]{:S(2)}, u32[]{:S(2)}) collective-permute-start(bf16[1024,512]{1,0:T(8,128)(2,1)S(1)} %bitcast.48), channel_id=1, source_target_pairs={{16,0},{17,1},{18,2},{19,3},{20,4},{21,5},{22,6},{23,7},{24,8},{25... | collective-permute-start | bytes 3145736 | tf_op jit(solution)/shard_map/ppermute | solution.py:376
  51.0 31.2 %all-to-all-start.6 = ((bf16[16,64,512]{2,1,0:T(8,128)(2,1)}), bf16[16,64,512]{2,1,0:T(8,128)(2,1)S(1)}, u32[]{:S(2)}, u32[]{:S(2)}) async-start(bf16[16,64,512]{2,1,0:T(8,128)(2,1)} %shard_map.51), calls=%async_computation.6 | async-start | bytes 2097152 | tf_op jit(solution)/shard_map/all_to_all | solution.py:340
  77.1 1.0 %copy-start.7 = (s32[4,128,128]{2,1,0:T(8,128)S(1)}, s32[4,128,128]{2,1,0:T(8,128)}, u32[]{:S(2)}) copy-start(s32[4,128,128]{2,1,0:T(8,128)} %get-tuple-element.50.places_ref) | copy-start | bytes 786436

commit v7 on v6

--- a/solution.py
+++ b/solution.py
@@ -90,8 +90,9 @@
 
 KINDS = 8
 LANES = 128
-STEP = 4
-EARLY, LATE = 64, 64
+STEP = 2
+UNROLL = 4
+LADDER = (56, 56), (56, 64), (72, 72)
 ADD_BYTES, EARLY_BYTES = 1<<34, 1<<34
 
 
@@ -111,7 +112,7 @@
     return jnp.where(condition, 1.0, 0.0).astype(jnp.bfloat16)
 
 
-def needs_kernel(own_rows, early, late, slots_ref, counts_ref, flags_ref):
+def needs_kernel(own_rows, slots_ref, counts_ref, flags_ref):
     mine, slot_total = slots_ref.shape
     side = flags_ref.shape[0]
     hits = jnp.zeros((side, LANES), jnp.float32)
@@ -134,14 +135,16 @@
     sums = dot(flags.astype(jnp.bfloat16), jnp.ones((LANES, LANES), jnp.bfloat16))
     counted = dot(mark(first | second), sums.astype(jnp.bfloat16))
     kind = iota((side, LANES), 0) % KINDS
-    room = jnp.where(kind == 4, 1.0 * (early + late), 1.0 * late)
-    spill = jnp.max(jnp.where((kind == 4) | (kind == 5), counted - room, 0.0))
-    flags_ref[...] = jnp.where(kind == 6, jnp.where(spill > 0.0, 1.0, 0.0), flags).astype(flags_ref.dtype)
-
-
-def needs(slot_rows, counts, own_rows, early, late, groups):
-    return pl.pallas_call(
-        functools.partial(needs_kernel, own_rows, early, late),
+    level = jnp.zeros((side, LANES), jnp.float32)
+    for early, late in LADDER:
+        room = jnp.where(kind == 4, 1.0 * (early + late), jnp.where(kind == 5, 1.0 * late, 1.0 * LANES * KINDS))
+        level = level + jnp.where(counted > room, 1.0, 0.0)
+    flags_ref[...] = jnp.where(kind == 6, jnp.max(level), flags).astype(flags_ref.dtype)
+
+
+def needs(slot_rows, counts, own_rows, groups):
+    return pl.pallas_call(
+        functools.partial(needs_kernel, own_rows),
         out_shape=jax.ShapeDtypeStruct((groups * KINDS, LANES), jnp.bfloat16),
         in_specs=[pl.BlockSpec(memory_space=pltpu.VMEM), pl.BlockSpec(memory_space=pltpu.SMEM)],
         out_specs=pl.BlockSpec(memory_space=pltpu.VMEM),
@@ -166,49 +169,65 @@
     return jnp.concatenate([mark(rank == upper), mark(rank == lower)], axis=1)
 
 
-def pack_kernel(plane_ref, flags_ref, terms_ref, early_ref, send_ref, keep_ref, keys_ref):
-    batch, early, _ = early_ref.shape
+def pack_kernel(plane_ref, flags_ref, terms_ref, early_ref, send_ref, keep_ref, rows, packed_early, keys_ref, came, went):
+    groups, early, _ = packed_early.shape
     late = send_ref.shape[1]
-    step = pl.program_id(0)
-
-    @pl.when(step == 0)
-    def _():
-        keys_ref[...] = keys_of(flags_ref[...])
-
+
+    def arrival(d):
+        return pltpu.make_async_copy(terms_ref.at[d], rows.at[d], came.at[d])
+
+    def departure(d):
+        return pltpu.make_async_copy(packed_early.at[d], early_ref.at[d], went.at[d])
+
+    @pl.loop(0, groups)
+    def _(d):
+        arrival(d).start()
+
+    keys_ref[...] = keys_of(flags_ref[...])
     plane = plane_ref[0]
-    for i in range(batch):
-        keys = keys_ref[pl.ds((step * batch + i) * KINDS, KINDS), :]
+
+    def one(d):
+        keys = keys_ref[pl.ds(pl.multiple_of(d * KINDS, KINDS), KINDS), :]
         second = keys[2:3], keys[3:4]
         beyond = keys[0:1] - early, keys[1:2] - early
         sent = [jnp.where(plane == 0, b, a) for a, b in zip(beyond, second)]
         kept = [jnp.where(plane == 0, a, b) for a, b in zip(beyond, second)]
         chosen = [chosen_rows(late, *sent), chosen_rows(late, *kept), chosen_rows(early, keys[0:1], keys[1:2])]
-        packed = dot(jnp.concatenate(chosen, axis=0), terms_ref[i]).astype(early_ref.dtype)
-        send_ref[i] = packed[:late]
-        keep_ref[i] = packed[late : 2 * late]
-        early_ref[i] = packed[2 * late :]
+        arrival(d).wait()
+        packed = dot(jnp.concatenate(chosen, axis=0), rows[d]).astype(packed_early.dtype)
+        send_ref[d] = packed[:late]
+        keep_ref[d] = packed[late : 2 * late]
+        packed_early[d] = packed[2 * late :]
+        departure(d).start()
+
+    unroll = UNROLL if groups % UNROLL == 0 else 1
+
+    @pl.loop(0, groups // unroll)
+    def _(step):
+        for i in range(unroll):
+            one(step * unroll + i)
+
+    @pl.loop(0, groups)
+    def _(d):
+        departure(d).wait()
 
 
 def pack(plane, flags, terms, early, late):
     groups, rows, width = terms.shape
-    batch = 8 if groups % 8 == 0 else 1
-
-    def out(capacity):
-        block = pl.BlockSpec((batch, capacity, width), lambda i: (i, 0, 0))
-        return jax.ShapeDtypeStruct((groups, capacity, width), terms.dtype), block
-
-    shapes, blocks = zip(out(early), out(late), out(late))
+    vmem, hbm = pl.BlockSpec(memory_space=pltpu.VMEM), pl.BlockSpec(memory_space=pltpu.HBM)
+    shapes = [jax.ShapeDtypeStruct((groups, capacity, width), terms.dtype) for capacity in (early, late, late)]
     return pl.pallas_call(
         pack_kernel,
-        grid=(groups // batch,),
         out_shape=shapes,
-        in_specs=[
-            pl.BlockSpec(memory_space=pltpu.SMEM),
-            pl.BlockSpec(flags.shape, lambda i: (0, 0)),
-            pl.BlockSpec((batch, rows, width), lambda i: (i, 0, 0)),
+        in_specs=[pl.BlockSpec(memory_space=pltpu.SMEM), vmem, hbm],
+        out_specs=[hbm, vmem, vmem],
+        scratch_shapes=[
+            pltpu.VMEM(terms.shape, terms.dtype),
+            pltpu.VMEM((groups, early, width), terms.dtype),
+            pltpu.VMEM(flags.shape, jnp.float32),
+            pltpu.SemaphoreType.DMA((groups,)),
+            pltpu.SemaphoreType.DMA((groups,)),
         ],
-        out_specs=blocks,
-        scratch_shapes=[pltpu.VMEM(flags.shape, jnp.float32)],
         cost_estimate=pl.CostEstimate(
             flops=2 * groups * (early + 2 * late) * rows * width, bytes_accessed=4 * terms.size, transcendentals=0
         ),
@@ -279,61 +298,105 @@
     )(plane, own_slots, column)
 
 
-def chosen_places(places_ref, total):
+def chosen_places(places_ref, block, total):
     columns = iota((LANES, total), 1)
-    return jnp.concatenate([mark(columns == places_ref[0, :, i : i + 1]) for i in range(STEP)], axis=0)
-
-
-def early_kernel(places_ref, own_ref, other_ref, out_ref, table):
-    @pl.when(pl.program_id(0) == 0)
-    def _():
-        both = own_ref[...].astype(jnp.float32) + other_ref[...].astype(jnp.float32)
-        table[...] = both.astype(table.dtype)
-
-    out_ref[...] = dot(chosen_places(places_ref, table.shape[0]), table[...]).astype(out_ref.dtype)
-
-
-def late_kernel(places_ref, late_ref, early_ref, out_ref):
-    total = dot(chosen_places(places_ref, late_ref.shape[0]), late_ref[...]) + early_ref[...].astype(jnp.float32)
-    out_ref[...] = total.astype(out_ref.dtype).reshape(out_ref.shape)
+    held = places_ref[block]
+    return jnp.concatenate([mark(columns == held[:, i : i + 1]) for i in range(STEP)], axis=0)
+
+
+def rows_of(block, ref):
+    return ref.at[pl.ds(pl.multiple_of(block * STEP * LANES, STEP * LANES), STEP * LANES)]
+
+
+def early_kernel(places_ref, own_ref, other_ref, out_ref, table, chosen_sums, went):
+    both = own_ref[...].astype(jnp.float32) + other_ref[...].astype(jnp.float32)
+    table[...] = both.astype(table.dtype)
+    blocks = places_ref.shape[0]
+
+    def departure(block):
+        return pltpu.make_async_copy(rows_of(block, chosen_sums), rows_of(block, out_ref), went.at[block])
+
+    @pl.loop(0, blocks)
+    def _(block):
+        chosen = chosen_places(places_ref, block, table.shape[0])
+        rows_of(block, chosen_sums)[...] = dot(chosen, table[...]).astype(chosen_sums.dtype)
+        departure(block).start()
+
+    @pl.loop(0, blocks)
+    def _(block):
+        departure(block).wait()
+
+
+def late_kernel(places_ref, late_ref, early_ref, out_ref, early, sums, came, went):
+    blocks = places_ref.shape[0]
+    share, mine, width = out_ref.shape
+    per = share // blocks
+
+    def arrival(block):
+        return pltpu.make_async_copy(rows_of(block, early_ref), rows_of(block, early), came.at[block])
+
+    def departure(block):
+        at = pl.ds(block * per, per)
+        return pltpu.make_async_copy(sums.at[at], out_ref.at[at], went.at[block])
+
+    @pl.loop(0, blocks)
+    def _(block):
+        arrival(block).start()
+
+    @pl.loop(0, blocks)
+    def _(block):
+        total = dot(chosen_places(places_ref, block, late_ref.shape[0]), late_ref[...])
+        arrival(block).wait()
+        total = total + rows_of(block, early)[...].astype(jnp.float32)
+        sums[pl.ds(block * per, per)] = total.astype(sums.dtype).reshape(per, mine, width)
+        departure(block).start()
+
+    @pl.loop(0, blocks)
+    def _(block):
+        departure(block).wait()
 
 
 def early_part(where, own, other):
     rows, width = own.shape
     blocks = where.shape[0]
-    whole = pl.BlockSpec(own.shape, lambda i: (0, 0))
     slots = blocks * STEP * LANES
+    vmem, hbm = pl.BlockSpec(memory_space=pltpu.VMEM), pl.BlockSpec(memory_space=pltpu.HBM)
     return pl.pallas_call(
         early_kernel,
-        grid=(blocks,),
-        out_shape=jax.ShapeDtypeStruct((slots, width), own.dtype),
-        in_specs=[pl.BlockSpec((1, LANES, LANES), lambda i: (i, 0, 0)), whole, whole],
-        out_specs=pl.BlockSpec((STEP * LANES, width), lambda i: (i, 0)),
-        scratch_shapes=[pltpu.VMEM((rows, width), own.dtype)],
+        out_shape=pltpu.HBM((slots, width), own.dtype),
+        in_specs=[vmem] * 3,
+        out_specs=hbm,
+        scratch_shapes=[
+            pltpu.VMEM((rows, width), own.dtype),
+            pltpu.VMEM((slots, width), own.dtype),
+            pltpu.SemaphoreType.DMA((blocks,)),
+        ],
         cost_estimate=pl.CostEstimate(flops=EARLY_BYTES, bytes_accessed=EARLY_BYTES, transcendentals=0),
         compiler_params=pltpu.CompilerParams(vmem_limit_bytes=12 << 20),
-    )(where, own, other)
+    )(pltpu.with_memory_space_constraint(where, pltpu.HBM), own, other)
 
 
 def late_part(where, late, early, mine):
     rows, width = early.shape
     blocks = where.shape[0]
-    step = STEP * LANES
+    vmem, hbm = pl.BlockSpec(memory_space=pltpu.VMEM), pl.BlockSpec(memory_space=pltpu.HBM)
+    out = jax.ShapeDtypeStruct((rows // mine, mine, width), early.dtype)
     return pl.pallas_call(
         late_kernel,
-        grid=(blocks,),
-        out_shape=jax.ShapeDtypeStruct((rows // mine, mine, width), early.dtype),
-        in_specs=[
-            pl.BlockSpec((1, LANES, LANES), lambda i: (i, 0, 0)),
-            pl.BlockSpec(late.shape, lambda i: (0, 0)),
-            pl.BlockSpec((step, width), lambda i: (i, 0)),
+        out_shape=out,
+        in_specs=[vmem, vmem, hbm],
+        out_specs=hbm,
+        scratch_shapes=[
+            pltpu.VMEM(early.shape, early.dtype),
+            pltpu.VMEM(out.shape, out.dtype),
+            pltpu.SemaphoreType.DMA((blocks,)),
+            pltpu.SemaphoreType.DMA((blocks,)),
         ],
-        out_specs=pl.BlockSpec((step // mine, mine, width), lambda i: (i, 0, 0)),
         cost_estimate=pl.CostEstimate(
             flops=2 * rows * late.shape[0] * width, bytes_accessed=4 * late.size, transcendentals=0
         ),
         compiler_params=pltpu.CompilerParams(vmem_limit_bytes=12 << 20),
-    )(where, late, early)
+    )(pltpu.with_memory_space_constraint(where, pltpu.HBM), late, pltpu.with_memory_space_constraint(early, pltpu.HBM))
 
 
 def exchange(blocks):
@@ -363,21 +426,27 @@
     if cuts != 2 or unfit:
         return all_rows()
 
-    early, late = EARLY, LATE
     plane = me[None]
-    flags = needs(slot_rows, counts, own_rows, early, late, groups)
+    flags = needs(slot_rows, counts, own_rows, groups)
     flags = exchange(flags.reshape(groups, KINDS, LANES))
-    spilled = jnp.max(flags[:, 6, :].astype(jnp.float32)) > 0.0
+    level = jnp.max(flags[:, 6, :].astype(jnp.float32)).astype(jnp.int32)
+    flags = flags.reshape(groups * KINDS, LANES)
     by_owner = terms.reshape(groups, mine * own_rows, width)
-    first, send, keep = pack(plane, flags.reshape(groups * KINDS, LANES), by_owner, early, late)
-    other = lax.ppermute(send, "cuts", [(0, 1), (1, 0)])
-    own_early = exchange(first).reshape(groups * early, width)
-    own_early, summed = lax.optimization_barrier((own_early, add(keep, other)))
-    other_early = lax.ppermute(own_early, "cuts", [(1, 0)])
-    own_late = exchange(summed).reshape(groups * late, width)
-    where_early, where_late = places(plane, turned[:, (cuts - 1) * share :], own_rows, early, late)
-    sums = early_part(where_early, own_early, other_early)
-    return lax.cond(spilled, all_rows, lambda: late_part(where_late, own_late, sums, mine))
+    own_slots = turned[:, (cuts - 1) * share :]
+
+    def needed_rows(early, late):
+        first, send, keep = pack(plane, flags, by_owner, early, late)
+        other = lax.ppermute(send, "cuts", [(0, 1), (1, 0)])
+        own_early = exchange(first).reshape(groups * early, width)
+        own_early, summed = lax.optimization_barrier((own_early, add(keep, other)))
+        other_early = lax.ppermute(own_early, "cuts", [(1, 0)])
+        own_late = exchange(summed).reshape(groups * late, width)
+        where_early, where_late = places(plane, own_slots, own_rows, early, late)
+        sums = early_part(where_early, own_early, other_early)
+        return late_part(where_late, own_late, sums, mine)
+
+    plans = [functools.partial(needed_rows, *sizes) for sizes in LADDER]
+    return lax.switch(level, plans + [all_rows])
 
 
 def solution(mesh):

time: 89.1 us -> 91.9 us (1.031)
  Pallas kernels: 30.2 us -> 36.3 us
  waiting for transfers between devices: 31.3 us -> 27.2 us
  local copies, waits for them, and re-layouts: 2.6 us -> 1.64 us
    pallas_call x4, Pallas kernels: 15.7 us -> 21.4 us  [the longest x1 7.69 us: late_part(): pl.pallas_call(late_kernel, out_shape=out, in_specs=[vmem, vmem, hbm], ou...]
    all_to_all x3, waiting for transfers between devices: 3.16 us -> 0.63 us  [exchange(): lax.all_to_all(blocks, 'group', split_axis=0, concat_axis=0, tiled=True)]
    ppermute x2, waiting for transfers between devices: 28.1 us -> 26.6 us  [the longest x1 18 us: needed_rows(): other = lax.ppermute(send, 'cuts', [(0, 1), (1, 0)])]
    unnamed x6 -> x0, local copies, waits for them, and re-layouts: 0.96 us -> none
  transfers between devices with their start and end apart: 5 -> 5, of which waited for: 4 -> 4; matrix products, arithmetic and copies ran while one was open for 3% -> 3% of each run, Pallas kernels for 21% -> 23%
where the time goes in v7:
time: 91.9 us; the launch traced here: 90.2 us
  Pallas kernels  36.3 us (39%)
  waiting for transfers between devices  27.2 us (30%)
  starting transfers between devices  22.2 us (24%)
  local copies, waits for them, and re-layouts  1.64 us (2%)
  other arithmetic  1.44 us (2%)
    all_to_all x3, starting transfers between devices, exchange(): lax.all_to_all(blocks, 'group', split_axis=0, concat_axis=0, tiled=True)  19.3 us
    ppermute x1, waiting for transfers between devices, needed_rows(): other = lax.ppermute(send, 'cuts', [(0, 1), (1, 0)])  18 us
    ppermute x1, waiting for transfers between devices, needed_rows(): other_early = lax.ppermute(own_early, 'cuts', [(1, 0)])  8.57 us
    pallas_call x1, Pallas kernels, late_part(): pl.pallas_call(late_kernel, out_shape=out, in_specs=[vmem, vmem, hbm], ou...  7.69 us
    pallas_call x1, Pallas kernels, places(): pl.pallas_call(functools.partial(places_kernel, own_rows, early, late), o...  6.87 us
    pallas_call x1, Pallas kernels, early_part(): pl.pallas_call(early_kernel, out_shape=pltpu.HBM((slots, width), own.dtyp...  6.13 us
    pallas_call x1, Pallas kernels, terms_of(): pl.pallas_call(terms_kernel, grid=(total // block,), out_shape=jax.ShapeD...  5.52 us
    pallas_call x1, Pallas kernels, pack(): pl.pallas_call(pack_kernel, out_shape=shapes, in_specs=[pl.BlockSpec(memo...  5.29 us
  transfers between devices with their start and end apart: 5, of which 4 were waited for; matrix products, arithmetic and copies ran while one was open for 3% of the time, Pallas kernels for 23%

profile of v7, /device:TPU:0, one launch (start us, length us, event | category | flops | bytes accessed | tf_op | source)
XLA Modules:
  0.0 90.2 jit_solution(5578624000123805382)
XLA Ops:
  0.0 2.3 %shard_map.50 = bf16[128,128]{1,0:T(8,128)(2,1)} custom-call(s32[4,1024]{1,0:T(4,128)} %slots_ref.1, s32[4]{0:T(128)} %counts_ref.1), custom_call_target="tpu_custom_call" | custom-call | flops 268435456 | bytes 131072 | tf_op jit(solution)/shard_map/pallas_call | solution.py:146
  2.3 7.4 %all-to-all-start.10 = ((bf16[16,8,128]{2,1,0:T(8,128)(2,1)}), bf16[16,8,128]{2,1,0:T(8,128)(2,1)S(1)}, u32[]{:S(2)}, u32[]{:S(2)}) async-start(bf16[16,8,128]{2,1,0:T(8,128)(2,1)} %bitcast.89), calls=%async_computation.10 | async-start | bytes 65536 | tf_op jit(solution)/shard_map/all_to_all | solution.py:403
  9.7 0.8 fusion.5
  10.5 5.5 %shard_map.51 = bf16[4096,512]{1,0:T(8,128)(2,1)} custom-call(bf16[4096,512]{1,0:T(8,128)(2,1)} %bitcast.81, bf16[2,256,256]{2,1,0:T(8,128)(2,1)} %bitcast.85), custom_call_target="tpu_custom_call" | custom-call | flops 2147483648 | bytes 8388608 | tf_op jit(solution)/shard_map/pallas_call | solution.py:29
  16.1 0.3 all-to-all-done.10
  16.3 0.6 slice_reduce_fusion
  17.6 72.4 %conditional.1 = (bf16[512,4,512]{2,1,0:T(4,128)(2,1)}) conditional(s32[]{:T(128)} %clamp.3, (s32[]{:T(128)}, s32[4,1024]{1,0:T(4,128)S(1)}, bf16[16,8,128]{2,1,0:T(8,128)(2,1)S(1)}, bf16[4096,512]{1,0:T(8,128)(2,1)}) %tuple.22, (s32[]{:T(128)}, s32[4,1024]{1,0:T(4,128)S(1)}, bf16[16,8,128]{2,1,0:T(8,128)(2,1)S(1)}, ...), branch_computations={%region_1.2_spmd, %region_2.3_spmd, %region_3.4_spmd, %region_4.5_... | conditional | flops 37950062592 | bytes 34387468288 | solution.py:449
  17.6 5.3 %branch_1_fun.6 = (bf16[16,56,512]{2,1,0:T(8,128)(2,1)}, bf16[16,64,512]{2,1,0:T(8,128)(2,1)S(1)}, bf16[16,64,512]{2,1,0:T(8,128)(2,1)S(1)}) custom-call(s32[1]{0:T(128)} %bitcast.7.plane_ref, bf16[128,128]{1,0:T(8,128)(2,1)S(1)} %bitcast.83, bf16[16,256,512]{2,1,0:T(8,128)(2,1)} %bitcast.78), custom_call_target="tpu_custom_call" | custom-call | flops 771751936 | bytes 8388608 | tf_op jit(solution)/shard_map/cond/branch_1_fun/pallas_call | solution.py:219
  22.9 1.6 %collective-permute-start.2 = (bf16[16,64,512]{2,1,0:T(8,128)(2,1)S(1)}, bf16[16,64,512]{2,1,0:T(8,128)(2,1)}, u32[]{:S(2)}, u32[]{:S(2)}) collective-permute-start(bf16[16,64,512]{2,1,0:T(8,128)(2,1)S(1)} %get-tuple-element.68), channel_id=1, source_target_pairs={{0,16},{16,0},{1,17},{17,1},{2,18},{18,2},{3,19},{19,3},{4,20},{20... | collective-permute-start | bytes 3145736 | tf_op jit(solution)/shard_map/cond/branch_1_fun/ppermute | solution.py:439
  24.5 5.7 %all-to-all-start.2 = ((bf16[16,56,512]{2,1,0:T(8,128)(2,1)}), bf16[16,56,512]{2,1,0:T(8,128)(2,1)S(1)}, u32[]{:S(2)}, u32[]{:S(2)}) async-start(bf16[16,56,512]{2,1,0:T(8,128)(2,1)} %get-tuple-element.66), calls=%async_computation.2 | async-start | bytes 1835008 | tf_op jit(solution)/shard_map/cond/branch_1_fun/all_to_all | solution.py:403
  30.3 18.0 %collective-permute-done.2.b_ref = bf16[16,64,512]{2,1,0:T(8,128)(2,1)} collective-permute-done((bf16[16,64,512]{2,1,0:T(8,128)(2,1)S(1)}, bf16[16,64,512]{2,1,0:T(8,128)(2,1)}, u32[]{:S(2)}, u32[]{:S(2)}) %collective-permute-start.2) | collective-permute-done | bytes 1048608 | tf_op jit(solution)/shard_map/cond/branch_1_fun/ppermute | solution.py:439
  48.3 2.4 %branch_1_fun.7 = bf16[16,64,512]{2,1,0:T(8,128)(2,1)} custom-call(bf16[16,64,512]{2,1,0:T(8,128)(2,1)S(1)} %get-tuple-element.67.a_ref, bf16[16,64,512]{2,1,0:T(8,128)(2,1)} %collective-permute-done.2.b_ref), custom_call_target="tpu_custom_call" | custom-call | flops 17179869184 | bytes 17179869184 | tf_op jit(solution)/shard_map/cond/branch_1_fun/pallas_call | solution.py:244
  50.7 0.3 all-to-all-done.2
  51.1 1.3 %collective-permute-start.3 = (bf16[896,512]{1,0:T(8,128)(2,1)S(1)}, bf16[896,512]{1,0:T(8,128)(2,1)S(1)}, u32[]{:S(2)}, u32[]{:S(2)}) collective-permute-start(bf16[896,512]{1,0:T(8,128)(2,1)S(1)} %bitcast.74), channel_id=1, source_target_pairs={{16,0},{17,1},{18,2},{19,3},{20,4},{21,5},{22,6},{23,7},{24,8},{25... | collective-permute-start | bytes 2752520 | tf_op jit(solution)/shard_map/cond/branch_1_fun/ppermute | solution.py:442
  52.4 6.2 %all-to-all-start.3 = ((bf16[16,64,512]{2,1,0:T(8,128)(2,1)}), bf16[16,64,512]{2,1,0:T(8,128)(2,1)S(1)}, u32[]{:S(2)}, u32[]{:S(2)}) async-start(bf16[16,64,512]{2,1,0:T(8,128)(2,1)} %branch_1_fun.7), calls=%async_computation.3 | async-start | bytes 2097152 | tf_op jit(solution)/shard_map/cond/branch_1_fun/all_to_all | solution.py:403
  58.6 0.6 slice_bitcast_fusion.1
  59.2 0.1 copy.20
  59.3 0.2 reshape.52
  59.5 0.7 copy.21
  60.2 6.9 %branch_1_fun.5 = (s32[8,128,128]{2,1,0:T(8,128)}, s32[8,128,128]{2,1,0:T(8,128)}) custom-call(s32[1]{0:T(128)} %bitcast.7.plane_ref, s32[4,512]{1,0:T(4,128)} %get-tuple-element.110.slots_ref, s32[128,16]{1,0:T(8,128)} %bitcast.87), custom_call_target="tpu_custom_call" | custom-call | flops 268435456 | bytes 262144 | tf_op jit(solution)/shard_map/cond/branch_1_fun/pallas_call | solution.py:292
  67.1 8.6 %collective-permute-done.3.other_ref = bf16[896,512]{1,0:T(8,128)(2,1)S(1)} collective-permute-done((bf16[896,512]{1,0:T(8,128)(2,1)S(1)}, bf16[896,512]{1,0:T(8,128)(2,1)S(1)}, u32[]{:S(2)}, u32[]{:S(2)}) %collective-permute-start.3) | collective-permute-done | bytes 917536 | tf_op jit(solution)/shard_map/cond/branch_1_fun/ppermute | solution.py:442
  75.7 6.1 %branch_1_fun.8.early_ref = bf16[2048,512]{1,0:T(8,128)(2,1)} custom-call(s32[8,128,128]{2,1,0:T(8,128)} %get-tuple-element.70.places_ref, bf16[896,512]{1,0:T(8,128)(2,1)S(1)} %bitcast.75, bf16[896,512]{1,0:T(8,128)(2,1)S(1)} %collective-permute-done.3.other_ref), custom_call_target="tpu_custom_call" | custom-call | flops 17179869184 | bytes 17179869184 | tf_op jit(solution)/shard_map/cond/branch_1_fun/pallas_call | solution.py:364
  81.8 0.0 all-to-all-done.3
  81.8 7.7 %branch_1_fun.9 = bf16[512,4,512]{2,1,0:T(4,128)(2,1)} custom-call(s32[8,128,128]{2,1,0:T(8,128)} %get-tuple-element.63.places_ref, bf16[1024,512]{1,0:T(8,128)(2,1)S(1)} %bitcast.69, bf16[2048,512]{1,0:T(8,128)(2,1)} %branch_1_fun.8.early_ref), custom_call_target="tpu_custom_call" | custom-call | flops 2147483648 | bytes 2097152 | tf_op jit(solution)/shard_map/cond/branch_1_fun/pallas_call | solution.py:384
  (1 shorter events, 0.0 us)
Async XLA Ops:
  2.3 14.0 %all-to-all-start.10 = ((bf16[16,8,128]{2,1,0:T(8,128)(2,1)}), bf16[16,8,128]{2,1,0:T(8,128)(2,1)S(1)}, u32[]{:S(2)}, u32[]{:S(2)}) async-start(bf16[16,8,128]{2,1,0:T(8,128)(2,1)} %bitcast.89), calls=%async_computation.10 | async-start | bytes 65536 | tf_op jit(solution)/shard_map/all_to_all | solution.py:403
  22.9 25.4 %collective-permute-start.2 = (bf16[16,64,512]{2,1,0:T(8,128)(2,1)S(1)}, bf16[16,64,512]{2,1,0:T(8,128)(2,1)}, u32[]{:S(2)}, u32[]{:S(2)}) collective-permute-start(bf16[16,64,512]{2,1,0:T(8,128)(2,1)S(1)} %get-tuple-element.68), channel_id=1, source_target_pairs={{0,16},{16,0},{1,17},{17,1},{2,18},{18,2},{3,19},{19,3},{4,20},{20... | collective-permute-start | bytes 3145736 | tf_op jit(solution)/shard_map/cond/branch_1_fun/ppermute | solution.py:439
  24.5 26.6 %all-to-all-start.2 = ((bf16[16,56,512]{2,1,0:T(8,128)(2,1)}), bf16[16,56,512]{2,1,0:T(8,128)(2,1)S(1)}, u32[]{:S(2)}, u32[]{:S(2)}) async-start(bf16[16,56,512]{2,1,0:T(8,128)(2,1)} %get-tuple-element.66), calls=%async_computation.2 | async-start | bytes 1835008 | tf_op jit(solution)/shard_map/cond/branch_1_fun/all_to_all | solution.py:403
  51.1 24.6 %collective-permute-start.3 = (bf16[896,512]{1,0:T(8,128)(2,1)S(1)}, bf16[896,512]{1,0:T(8,128)(2,1)S(1)}, u32[]{:S(2)}, u32[]{:S(2)}) collective-permute-start(bf16[896,512]{1,0:T(8,128)(2,1)S(1)} %bitcast.74), channel_id=1, source_target_pairs={{16,0},{17,1},{18,2},{19,3},{20,4},{21,5},{22,6},{23,7},{24,8},{25... | collective-permute-start | bytes 2752520 | tf_op jit(solution)/shard_map/cond/branch_1_fun/ppermute | solution.py:442
  52.4 29.4 %all-to-all-start.3 = ((bf16[16,64,512]{2,1,0:T(8,128)(2,1)}), bf16[16,64,512]{2,1,0:T(8,128)(2,1)S(1)}, u32[]{:S(2)}, u32[]{:S(2)}) async-start(bf16[16,64,512]{2,1,0:T(8,128)(2,1)} %branch_1_fun.7), calls=%async_computation.3 | async-start | bytes 2097152 | tf_op jit(solution)/shard_map/cond/branch_1_fun/all_to_all | solution.py:403

commit v8 on v6

--- a/solution.py
+++ b/solution.py
@@ -90,7 +90,8 @@
 
 KINDS = 8
 LANES = 128
-STEP = 4
+STEP = 8
+PART = 2
 EARLY, LATE = 64, 64
 ADD_BYTES, EARLY_BYTES = 1<<34, 1<<34
 
@@ -279,40 +280,46 @@
     )(plane, own_slots, column)
 
 
-def chosen_places(places_ref, total):
+def chosen_places(places, part, total):
     columns = iota((LANES, total), 1)
-    return jnp.concatenate([mark(columns == places_ref[0, :, i : i + 1]) for i in range(STEP)], axis=0)
+    first = part * PART
+    return jnp.concatenate([mark(columns == places[:, first + i : first + i + 1]) for i in range(PART)], axis=0)
 
 
 def early_kernel(places_ref, own_ref, other_ref, out_ref, table):
-    @pl.when(pl.program_id(0) == 0)
-    def _():
-        both = own_ref[...].astype(jnp.float32) + other_ref[...].astype(jnp.float32)
-        table[...] = both.astype(table.dtype)
-
-    out_ref[...] = dot(chosen_places(places_ref, table.shape[0]), table[...]).astype(out_ref.dtype)
+    both = own_ref[...].astype(jnp.float32) + other_ref[...].astype(jnp.float32)
+    table[...] = both.astype(table.dtype)
+    size = PART * LANES
+    for block in range(places_ref.shape[0]):
+        for part in range(STEP // PART):
+            chosen = chosen_places(places_ref.at[block], part, table.shape[0])
+            at = (block * STEP + part * PART) * LANES
+            out_ref[at : at + size, :] = dot(chosen, table[...]).astype(out_ref.dtype)
 
 
 def late_kernel(places_ref, late_ref, early_ref, out_ref):
-    total = dot(chosen_places(places_ref, late_ref.shape[0]), late_ref[...]) + early_ref[...].astype(jnp.float32)
-    out_ref[...] = total.astype(out_ref.dtype).reshape(out_ref.shape)
+    size = PART * LANES
+    per = out_ref.shape[0] // (STEP // PART)
+    for part in range(STEP // PART):
+        chosen = chosen_places(places_ref.at[0], part, late_ref.shape[0])
+        early = early_ref[part * size : (part + 1) * size, :].astype(jnp.float32)
+        total = (dot(chosen, late_ref[...]) + early).astype(out_ref.dtype)
+        out_ref[part * per : (part + 1) * per] = total.reshape(per, *out_ref.shape[1:])
 
 
 def early_part(where, own, other):
     rows, width = own.shape
-    blocks = where.shape[0]
-    whole = pl.BlockSpec(own.shape, lambda i: (0, 0))
-    slots = blocks * STEP * LANES
+    slots = where.shape[0] * STEP * LANES
+    vmem = pl.BlockSpec(memory_space=pltpu.VMEM)
     return pl.pallas_call(
         early_kernel,
-        grid=(blocks,),
         out_shape=jax.ShapeDtypeStruct((slots, width), own.dtype),
-        in_specs=[pl.BlockSpec((1, LANES, LANES), lambda i: (i, 0, 0)), whole, whole],
-        out_specs=pl.BlockSpec((STEP * LANES, width), lambda i: (i, 0)),
+        in_specs=[vmem] * 3,
+        out_specs=vmem,
         scratch_shapes=[pltpu.VMEM((rows, width), own.dtype)],
         cost_estimate=pl.CostEstimate(flops=EARLY_BYTES, bytes_accessed=EARLY_BYTES, transcendentals=0),
         compiler_params=pltpu.CompilerParams(vmem_limit_bytes=12 << 20),
-    )(where, own, other)
+    )(pltpu.with_memory_space_constraint(where, pltpu.HBM), own, other)
 
 
 def late_part(where, late, early, mine):
@@ -333,7 +340,7 @@
             flops=2 * rows * late.shape[0] * width, bytes_accessed=4 * late.size, transcendentals=0
         ),
         compiler_params=pltpu.CompilerParams(vmem_limit_bytes=12 << 20),
-    )(where, late, early)
+    )(pltpu.with_memory_space_constraint(where, pltpu.HBM), late, early)
 
 
 def exchange(blocks):
@@ -373,7 +380,7 @@
     other = lax.ppermute(send, "cuts", [(0, 1), (1, 0)])
     own_early = exchange(first).reshape(groups * early, width)
     own_early, summed = lax.optimization_barrier((own_early, add(keep, other)))
-    other_early = lax.ppermute(own_early, "cuts", [(1, 0)])
+    other_early = lax.ppermute(own_early, "cuts", [(0, 1), (1, 0)])
     own_late = exchange(summed).reshape(groups * late, width)
     where_early, where_late = places(plane, turned[:, (cuts - 1) * share :], own_rows, early, late)
     sums = early_part(where_early, own_early, other_early)

time: 89.1 us -> 86.5 us (0.971)
  local copies, waits for them, and re-layouts: 2.6 us -> 1.63 us
  waiting for transfers between devices: 31.3 us -> 30.4 us
    ppermute x1, waiting for transfers between devices: 9.69 us -> 8.69 us  [local(): other_early = lax.ppermute(own_early, 'cuts', [(0, 1), (1, 0)])]
    unnamed x6 -> x4, local copies, waits for them, and re-layouts: 0.96 us -> 0.01 us
  transfers between devices with their start and end apart: 5 -> 5, of which waited for: 4 -> 5; matrix products, arithmetic and copies ran while one was open for 3% -> 3% of each run, Pallas kernels for 21% -> 23%
where the time goes in v8:
time: 86.5 us; the launch traced here: 84.9 us
  waiting for transfers between devices  30.4 us (35%)
  Pallas kernels  30.3 us (35%)
  starting transfers between devices  21.1 us (24%)
  local copies, waits for them, and re-layouts  1.63 us (2%)
    all_to_all x3, starting transfers between devices, exchange(): lax.all_to_all(blocks, 'group', split_axis=0, concat_axis=0, tiled=True)  19.1 us
    ppermute x1, waiting for transfers between devices, local(): other = lax.ppermute(send, 'cuts', [(0, 1), (1, 0)])  18.5 us
    ppermute x1, waiting for transfers between devices, local(): other_early = lax.ppermute(own_early, 'cuts', [(0, 1), (1, 0)])  8.69 us
    pallas_call x1, Pallas kernels, places(): pl.pallas_call(functools.partial(places_kernel, own_rows, early, late), o...  6.56 us
    pallas_call x1, Pallas kernels, terms_of(): pl.pallas_call(terms_kernel, grid=(total // block,), out_shape=jax.ShapeD...  5.51 us
    pallas_call x1, Pallas kernels, late_part(): pl.pallas_call(late_kernel, grid=(blocks,), out_shape=jax.ShapeDtypeStruc...  4.88 us
    pallas_call x1, Pallas kernels, early_part(): pl.pallas_call(early_kernel, out_shape=jax.ShapeDtypeStruct((slots, width...  4.68 us
    pallas_call x1, Pallas kernels, pack(): pl.pallas_call(pack_kernel, grid=(groups // batch,), out_shape=shapes, in...  3.85 us
  transfers between devices with their start and end apart: 5, of which 5 were waited for; matrix products, arithmetic and copies ran while one was open for 3% of the time, Pallas kernels for 23%

profile of v8, /device:TPU:0, one launch (start us, length us, event | category | flops | bytes accessed | tf_op | source)
XLA Modules:
  0.0 84.9 jit_solution(10614840365167366640)
XLA Ops:
  0.0 2.3 %shard_map.48 = bf16[128,128]{1,0:T(8,128)(2,1)} custom-call(s32[4,1024]{1,0:T(4,128)} %slots_ref.1, s32[4]{0:T(128)} %counts_ref.1), custom_call_target="tpu_custom_call" | custom-call | flops 268435456 | bytes 131072 | tf_op jit(solution)/shard_map/pallas_call | solution.py:144
  2.3 7.4 %all-to-all-start.4 = ((bf16[16,8,128]{2,1,0:T(8,128)(2,1)}), bf16[16,8,128]{2,1,0:T(8,128)(2,1)S(1)}, u32[]{:S(2)}, u32[]{:S(2)}) async-start(bf16[16,8,128]{2,1,0:T(8,128)(2,1)} %bitcast.61), calls=%async_computation.4 | async-start | bytes 65536 | tf_op jit(solution)/shard_map/all_to_all | solution.py:347
  9.7 5.5 %shard_map.49 = bf16[4096,512]{1,0:T(8,128)(2,1)} custom-call(bf16[4096,512]{1,0:T(8,128)(2,1)} %bitcast.57, bf16[2,256,256]{2,1,0:T(8,128)(2,1)} %bitcast.59), custom_call_target="tpu_custom_call" | custom-call | flops 2147483648 | bytes 8388608 | tf_op jit(solution)/shard_map/pallas_call | solution.py:29
  15.2 1.1 %all-to-all-done.4 = bf16[16,8,128]{2,1,0:T(8,128)(2,1)S(1)} async-done(((bf16[16,8,128]{2,1,0:T(8,128)(2,1)}), bf16[16,8,128]{2,1,0:T(8,128)(2,1)S(1)}, u32[]{:S(2)}, u32[]{:S(2)}) %all-to-all-start.4) | async-done | bytes 32800 | tf_op jit(solution)/shard_map/all_to_all | solution.py:347
  16.3 3.9 %shard_map.50 = (bf16[16,64,512]{2,1,0:T(8,128)(2,1)}, bf16[16,64,512]{2,1,0:T(8,128)(2,1)S(1)}, bf16[16,64,512]{2,1,0:T(8,128)(2,1)S(1)}) custom-call(s32[1]{0:T(128)} %bitcast.19.plane_ref, bf16[128,128]{1,0:T(8,128)(2,1)S(1)} %bitcast.54, bf16[16,256,512]{2,1,0:T(8,128)(2,1)} %bitcast.55), custom_call_target="tpu_custom_call" | custom-call | flops 805306368 | bytes 8388608 | tf_op jit(solution)/shard_map/pallas_call | solution.py:202
  20.2 1.5 %collective-permute-start.4 = (bf16[16,64,512]{2,1,0:T(8,128)(2,1)S(1)}, bf16[16,64,512]{2,1,0:T(8,128)(2,1)}, u32[]{:S(2)}, u32[]{:S(2)}) collective-permute-start(bf16[16,64,512]{2,1,0:T(8,128)(2,1)S(1)} %get-tuple-element.47), channel_id=1, source_target_pairs={{0,16},{16,0},{1,17},{17,1},{2,18},{18,2},{3,19},{19,3},{4,20},{20... | collective-permute-start | bytes 3145736 | tf_op jit(solution)/shard_map/ppermute | solution.py:380
  21.7 4.9 %all-to-all-start.5 = ((bf16[16,64,512]{2,1,0:T(8,128)(2,1)}), bf16[16,64,512]{2,1,0:T(8,128)(2,1)S(1)}, u32[]{:S(2)}, u32[]{:S(2)}) async-start(bf16[16,64,512]{2,1,0:T(8,128)(2,1)} %get-tuple-element.45), calls=%async_computation.5 | async-start | bytes 2097152 | tf_op jit(solution)/shard_map/all_to_all | solution.py:347
  26.6 18.5 %collective-permute-done.4.b_ref = bf16[16,64,512]{2,1,0:T(8,128)(2,1)} collective-permute-done((bf16[16,64,512]{2,1,0:T(8,128)(2,1)S(1)}, bf16[16,64,512]{2,1,0:T(8,128)(2,1)}, u32[]{:S(2)}, u32[]{:S(2)}) %collective-permute-start.4) | collective-permute-done | bytes 1048608 | tf_op jit(solution)/shard_map/ppermute | solution.py:380
  45.1 0.0 copy-start.8
  45.1 0.0 copy-start.9
  45.1 2.4 %shard_map.51 = bf16[16,64,512]{2,1,0:T(8,128)(2,1)} custom-call(bf16[16,64,512]{2,1,0:T(8,128)(2,1)S(1)} %get-tuple-element.46.a_ref, bf16[16,64,512]{2,1,0:T(8,128)(2,1)} %collective-permute-done.4.b_ref), custom_call_target="tpu_custom_call" | custom-call | flops 17179869184 | bytes 17179869184 | tf_op jit(solution)/shard_map/pallas_call | solution.py:226
  47.5 2.0 %all-to-all-done.5 = bf16[16,64,512]{2,1,0:T(8,128)(2,1)S(1)} async-done(((bf16[16,64,512]{2,1,0:T(8,128)(2,1)}), bf16[16,64,512]{2,1,0:T(8,128)(2,1)S(1)}, u32[]{:S(2)}, u32[]{:S(2)}) %all-to-all-start.5) | async-done | bytes 1048608 | tf_op jit(solution)/shard_map/all_to_all | solution.py:347
  49.5 0.5 collective-permute-start.5
  50.0 0.0 copy-done.8
  50.1 0.0 copy-done.9
  50.1 0.1 fusion.5
  50.2 6.9 %all-to-all-start.6 = ((bf16[16,64,512]{2,1,0:T(8,128)(2,1)}), bf16[16,64,512]{2,1,0:T(8,128)(2,1)S(1)}, u32[]{:S(2)}, u32[]{:S(2)}) async-start(bf16[16,64,512]{2,1,0:T(8,128)(2,1)} %shard_map.51), calls=%async_computation.6 | async-start | bytes 2097152 | tf_op jit(solution)/shard_map/all_to_all | solution.py:347
  57.0 0.6 slice_bitcast_fusion.8
  57.6 0.1 copy.22
  57.8 0.2 reshape.43
  58.0 0.7 copy.23
  58.7 6.6 %shard_map.52 = (s32[2,128,128]{2,1,0:T(8,128)}, s32[2,128,128]{2,1,0:T(8,128)}) custom-call(s32[1]{0:T(128)} %bitcast.19.plane_ref, s32[4,512]{1,0:T(4,128)} %get-tuple-element.65.slots_ref, s32[128,16]{1,0:T(8,128)} %bitcast.60), custom_call_target="tpu_custom_call" | custom-call | flops 268435456 | bytes 262144 | tf_op jit(solution)/shard_map/pallas_call | solution.py:274
  65.2 0.6 slice_reduce_fusion
  66.5 8.7 %collective-permute-done.5.other_ref = bf16[1024,512]{1,0:T(8,128)(2,1)S(1)} collective-permute-done((bf16[1024,512]{1,0:T(8,128)(2,1)S(1)}, bf16[1024,512]{1,0:T(8,128)(2,1)S(1)}, u32[]{:S(2)}, u32[]{:S(2)}) %collective-permute-start.5) | collective-permute-done | bytes 1048608 | tf_op jit(solution)/shard_map/ppermute | solution.py:383
  75.2 4.7 %shard_map.53 = bf16[2048,512]{1,0:T(8,128)(2,1)} custom-call(s32[2,128,128]{2,1,0:T(8,128)} %get-tuple-element.50.places_ref, bf16[1024,512]{1,0:T(8,128)(2,1)S(1)} %bitcast.49, bf16[1024,512]{1,0:T(8,128)(2,1)S(1)} %collective-permute-done.5.other_ref), custom_call_target="tpu_custom_call" | custom-call | flops 17179869184 | bytes 17179869184 | tf_op jit(solution)/shard_map/pallas_call | solution.py:314
  79.9 0.1 all-to-all-done.6
  80.0 4.9 %conditional.1 = (bf16[512,4,512]{2,1,0:T(4,128)(2,1)}) conditional(s32[]{:T(128)} %convert_element_type.40, (bf16[16,64,512]{2,1,0:T(8,128)(2,1)S(1)}, s32[2,128,128]{2,1,0:T(8,128)}, bf16[2048,512]{1,0:T(8,128)(2,1)}) %tuple.15, (bf16[4096,512]{1,0:T(8,128)(2,1)}, s32[4,1024]{1,0:T(4,128)S(1)}) %tuple.16), branch_computations={%region_1.2_spmd, %region_2.3_spmd} | conditional | flops 4302307328 | bytes 61981160 | solution.py:387
  80.0 4.9 %branch_0_fun.1 = bf16[512,4,512]{2,1,0:T(4,128)(2,1)} custom-call(s32[2,128,128]{2,1,0:T(8,128)} %get-tuple-element.19.places_ref, bf16[1024,512]{1,0:T(8,128)(2,1)S(1)} %bitcast.58, bf16[2048,512]{1,0:T(8,128)(2,1)} %get-tuple-element.21.early_ref), custom_call_target="tpu_custom_call" | custom-call | flops 2147483648 | bytes 2097152 | tf_op jit(solution)/shard_map/cond/branch_0_fun/pallas_call | solution.py:329
  (1 shorter events, 0.0 us)
Async XLA Ops:
  2.3 14.0 %all-to-all-start.4 = ((bf16[16,8,128]{2,1,0:T(8,128)(2,1)}), bf16[16,8,128]{2,1,0:T(8,128)(2,1)S(1)}, u32[]{:S(2)}, u32[]{:S(2)}) async-start(bf16[16,8,128]{2,1,0:T(8,128)(2,1)} %bitcast.61), calls=%async_computation.4 | async-start | bytes 65536 | tf_op jit(solution)/shard_map/all_to_all | solution.py:347
  20.2 24.9 %collective-permute-start.4 = (bf16[16,64,512]{2,1,0:T(8,128)(2,1)S(1)}, bf16[16,64,512]{2,1,0:T(8,128)(2,1)}, u32[]{:S(2)}, u32[]{:S(2)}) collective-permute-start(bf16[16,64,512]{2,1,0:T(8,128)(2,1)S(1)} %get-tuple-element.47), channel_id=1, source_target_pairs={{0,16},{16,0},{1,17},{17,1},{2,18},{18,2},{3,19},{19,3},{4,20},{20... | collective-permute-start | bytes 3145736 | tf_op jit(solution)/shard_map/ppermute | solution.py:380
  21.7 27.8 %all-to-all-start.5 = ((bf16[16,64,512]{2,1,0:T(8,128)(2,1)}), bf16[16,64,512]{2,1,0:T(8,128)(2,1)S(1)}, u32[]{:S(2)}, u32[]{:S(2)}) async-start(bf16[16,64,512]{2,1,0:T(8,128)(2,1)} %get-tuple-element.45), calls=%async_computation.5 | async-start | bytes 2097152 | tf_op jit(solution)/shard_map/all_to_all | solution.py:347
  45.1 5.0 %copy-start.8 = (s32[4,1024]{1,0:T(4,128)S(1)}, s32[4,1024]{1,0:T(4,128)}, u32[]{:S(2)}) copy-start(s32[4,1024]{1,0:T(4,128)} %slots_ref.1) | copy-start | bytes 49156
  45.1 5.0 %copy-start.9 = (s32[4]{0:T(128)S(1)}, s32[4]{0:T(128)}, u32[]{:S(2)}) copy-start(s32[4]{0:T(128)} %counts_ref.1) | copy-start | bytes 52
  49.5 25.7 %collective-permute-start.5 = (bf16[1024,512]{1,0:T(8,128)(2,1)S(1)}, bf16[1024,512]{1,0:T(8,128)(2,1)S(1)}, u32[]{:S(2)}, u32[]{:S(2)}) collective-permute-start(bf16[1024,512]{1,0:T(8,128)(2,1)S(1)} %bitcast.48), channel_id=1, source_target_pairs={{0,16},{16,0},{1,17},{17,1},{2,18},{18,2},{3,19},{19,3},{4,20},{20... | collective-permute-start | bytes 3145736 | tf_op jit(solution)/shard_map/ppermute | solution.py:383
  50.2 29.8 %all-to-all-start.6 = ((bf16[16,64,512]{2,1,0:T(8,128)(2,1)}), bf16[16,64,512]{2,1,0:T(8,128)(2,1)S(1)}, u32[]{:S(2)}, u32[]{:S(2)}) async-start(bf16[16,64,512]{2,1,0:T(8,128)(2,1)} %shard_map.51), calls=%async_computation.6 | async-start | bytes 2097152 | tf_op jit(solution)/shard_map/all_to_all | solution.py:347

commit v9 on v8

--- a/solution.py
+++ b/solution.py
@@ -8,16 +8,19 @@
 from jax.sharding import PartitionSpec as P
 
 
+def build_matrix(pair_ref, matrix):
+    half = pair_ref.shape[1]
+    real_part, imag_part = pair_ref[0], pair_ref[1]
+    matrix[:half, :half] = real_part
+    matrix[:half, half:] = imag_part
+    matrix[half:, :half] = -imag_part
+    matrix[half:, half:] = real_part
+
+
 def terms_kernel(rows_ref, pair_ref, out_ref, matrix):
-    half = pair_ref.shape[1]
-
     @pl.when(pl.program_id(0) == 0)
     def _():
-        real_part, imag_part = pair_ref[0], pair_ref[1]
-        matrix[:half, :half] = real_part
-        matrix[:half, half:] = imag_part
-        matrix[half:, :half] = -imag_part
-        matrix[half:, half:] = real_part
+        build_matrix(pair_ref, matrix)
 
     out_ref[...] = dot(rows_ref[...], matrix[...]).astype(out_ref.dtype)
 
@@ -128,16 +131,12 @@
         lane_key = slots % own_rows + (k % per) * own_rows
         hits = hits + dot_nt(mark(down == row_key), mark(across == lane_key))
     flags = jnp.minimum(hits, 1.0)
-    row, column = iota((side, side), 0), iota((side, side), 1)
-    kind, back = row % KINDS, row - column
-    first = (kind == 4) & ((back == 4) | (back == 3))
-    second = (kind == 5) & ((back == 3) | (back == 2))
-    sums = dot(flags.astype(jnp.bfloat16), jnp.ones((LANES, LANES), jnp.bfloat16))
-    counted = dot(mark(first | second), sums.astype(jnp.bfloat16))
-    kind = iota((side, LANES), 0) % KINDS
-    room = jnp.where(kind == 4, 1.0 * (early + late), 1.0 * late)
-    spill = jnp.max(jnp.where((kind == 4) | (kind == 5), counted - room, 0.0))
-    flags_ref[...] = jnp.where(kind == 6, jnp.where(spill > 0.0, 1.0, 0.0), flags).astype(flags_ref.dtype)
+    sums = jnp.sum(flags, axis=1, keepdims=True)
+    pairs = sums + jnp.concatenate([sums[1:], sums[:1]], axis=0)
+    kind = iota((side, 1), 0) % KINDS
+    over = jnp.where(kind == 0, pairs - (early + late), jnp.where(kind == 2, pairs - late, 0.0))
+    spill = jnp.where(jnp.max(over) > 0.0, 1.0, 0.0)
+    flags_ref[...] = jnp.where(iota((side, LANES), 0) % KINDS == 6, spill, flags).astype(flags_ref.dtype)
 
 
 def needs(slot_rows, counts, own_rows, early, late, groups):
@@ -167,54 +166,63 @@
     return jnp.concatenate([mark(rank == upper), mark(rank == lower)], axis=1)
 
 
-def pack_kernel(plane_ref, flags_ref, terms_ref, early_ref, send_ref, keep_ref, keys_ref):
-    batch, early, _ = early_ref.shape
-    late = send_ref.shape[1]
+def pack_kernel(lists, early, plane_ref, flags_ref, stem_ref, pair_ref, *refs):
+    outs, (keys_ref, matrix, picked) = refs[: len(lists)], refs[len(lists) :]
+    batch = stem_ref.shape[0]
     step = pl.program_id(0)
 
     @pl.when(step == 0)
     def _():
         keys_ref[...] = keys_of(flags_ref[...])
+        build_matrix(pair_ref, matrix)
 
     plane = plane_ref[0]
+    total = sum(out.shape[1] for out in outs)
     for i in range(batch):
         keys = keys_ref[pl.ds((step * batch + i) * KINDS, KINDS), :]
         second = keys[2:3], keys[3:4]
         beyond = keys[0:1] - early, keys[1:2] - early
-        sent = [jnp.where(plane == 0, b, a) for a, b in zip(beyond, second)]
-        kept = [jnp.where(plane == 0, a, b) for a, b in zip(beyond, second)]
-        chosen = [chosen_rows(late, *sent), chosen_rows(late, *kept), chosen_rows(early, keys[0:1], keys[1:2])]
-        packed = dot(jnp.concatenate(chosen, axis=0), terms_ref[i]).astype(early_ref.dtype)
-        send_ref[i] = packed[:late]
-        keep_ref[i] = packed[late : 2 * late]
-        early_ref[i] = packed[2 * late :]
-
-
-def pack(plane, flags, terms, early, late):
-    groups, rows, width = terms.shape
+        keyed = {
+            "first": (keys[0:1], keys[1:2]),
+            "send": [jnp.where(plane == 0, b, a) for a, b in zip(beyond, second)],
+            "keep": [jnp.where(plane == 0, a, b) for a, b in zip(beyond, second)],
+        }
+        chosen = [chosen_rows(out.shape[1], *keyed[name]) for name, out in zip(lists, outs)]
+        picked[i * total : (i + 1) * total, :] = dot(jnp.concatenate(chosen, axis=0), stem_ref[i]).astype(picked.dtype)
+    terms = dot(picked[...], matrix[...]).astype(picked.dtype)
+    at = 0
+    for i in range(batch):
+        for out in outs:
+            out[i] = terms[at : at + out.shape[1]]
+            at += out.shape[1]
+
+
+def pack(lists, plane, flags, stem, pair, early, late):
+    groups, rows, width = stem.shape
     batch = 8 if groups % 8 == 0 else 1
-
-    def out(capacity):
-        block = pl.BlockSpec((batch, capacity, width), lambda i: (i, 0, 0))
-        return jax.ShapeDtypeStruct((groups, capacity, width), terms.dtype), block
-
-    shapes, blocks = zip(out(early), out(late), out(late))
-    return pl.pallas_call(
-        pack_kernel,
+    out_width = 2 * pair.shape[2]
+    sizes = [early if name == "first" else late for name in lists]
+    return pl.pallas_call(
+        functools.partial(pack_kernel, lists, early),
         grid=(groups // batch,),
-        out_shape=shapes,
+        out_shape=[jax.ShapeDtypeStruct((groups, size, out_width), stem.dtype) for size in sizes],
         in_specs=[
             pl.BlockSpec(memory_space=pltpu.SMEM),
             pl.BlockSpec(flags.shape, lambda i: (0, 0)),
             pl.BlockSpec((batch, rows, width), lambda i: (i, 0, 0)),
+            pl.BlockSpec(pair.shape, lambda i: (0, 0, 0)),
         ],
-        out_specs=blocks,
-        scratch_shapes=[pltpu.VMEM(flags.shape, jnp.float32)],
+        out_specs=[pl.BlockSpec((batch, size, out_width), lambda i: (i, 0, 0)) for size in sizes],
+        scratch_shapes=[
+            pltpu.VMEM(flags.shape, jnp.float32),
+            pltpu.VMEM((width, out_width), stem.dtype),
+            pltpu.VMEM((batch * sum(sizes), width), stem.dtype),
+        ],
         cost_estimate=pl.CostEstimate(
-            flops=2 * groups * (early + 2 * late) * rows * width, bytes_accessed=4 * terms.size, transcendentals=0
+            flops=2 * groups * sum(sizes) * (rows + out_width) * width, bytes_accessed=3 * stem.size, transcendentals=0
         ),
-        compiler_params=pltpu.CompilerParams(vmem_limit_bytes=16 << 20),
-    )(plane, flags, terms)
+        compiler_params=pltpu.CompilerParams(vmem_limit_bytes=20 << 20),
+    )(plane, flags, pltpu.with_memory_space_constraint(stem, pltpu.HBM), pltpu.with_memory_space_constraint(pair, pltpu.HBM))
 
 
 def add_kernel(a_ref, b_ref, out_ref):
@@ -354,8 +362,7 @@
     slot_total = slot_rows.shape[1]
     share = slot_total // cuts
     stem = stem_blocks.reshape(group_total * own_rows, width)
-    terms = terms_of(stem, cap_tensor[0])
-    width = terms.shape[1]
+    pair = cap_tensor[0]
 
     positions = jnp.arange(slot_total, dtype=jnp.int32)
     marked = jnp.where(positions[None, :] < counts[:, None], slot_rows, -1)
@@ -364,7 +371,8 @@
     turned = lax.dynamic_slice_in_dim(doubled, (me + 1) * share, slot_total, 1)
 
     def all_rows():
-        return static_plan(terms.reshape(group_total, own_rows, width), turned, cuts)
+        terms = terms_of(stem, pair)
+        return static_plan(terms.reshape(group_total, own_rows, terms.shape[1]), turned, cuts)
 
     unfit = mine * own_rows != 2 * LANES or LANES % own_rows or groups > LANES or share * mine % (STEP * LANES)
     if cuts != 2 or unfit:
@@ -375,13 +383,15 @@
     flags = needs(slot_rows, counts, own_rows, early, late, groups)
     flags = exchange(flags.reshape(groups, KINDS, LANES))
     spilled = jnp.max(flags[:, 6, :].astype(jnp.float32)) > 0.0
-    by_owner = terms.reshape(groups, mine * own_rows, width)
-    first, send, keep = pack(plane, flags.reshape(groups * KINDS, LANES), by_owner, early, late)
+    flags = flags.reshape(groups * KINDS, LANES)
+    by_owner = stem.reshape(groups, mine * own_rows, width)
+    first, send = pack(("first", "send"), plane, flags, by_owner, pair, early, late)
+    (keep,) = pack(("keep",), plane, flags, by_owner, pair, early, late)
     other = lax.ppermute(send, "cuts", [(0, 1), (1, 0)])
-    own_early = exchange(first).reshape(groups * early, width)
+    own_early = exchange(first).reshape(groups * early, first.shape[2])
     own_early, summed = lax.optimization_barrier((own_early, add(keep, other)))
     other_early = lax.ppermute(own_early, "cuts", [(0, 1), (1, 0)])
-    own_late = exchange(summed).reshape(groups * late, width)
+    own_late = exchange(summed).reshape(groups * late, summed.shape[2])
     where_early, where_late = places(plane, turned[:, (cuts - 1) * share :], own_rows, early, late)
     sums = early_part(where_early, own_early, other_early)
     return lax.cond(spilled, all_rows, lambda: late_part(where_late, own_late, sums, mine))

time: 86.5 us -> 85.7 us (level)
  waiting for transfers between devices: 30.4 us -> 33.4 us
  Pallas kernels: 30.3 us -> 27.6 us
  starting transfers between devices: 21.1 us -> 19.9 us
    all_to_all x3, waiting for transfers between devices: 3.25 us -> 8.8 us  [exchange(): lax.all_to_all(blocks, 'group', split_axis=0, concat_axis=0, tiled=True)]
    ppermute x1, waiting for transfers between devices: 18.5 us -> 16 us  [local(): other = lax.ppermute(send, 'cuts', [(0, 1), (1, 0)])]
    all_to_all x3, starting transfers between devices: 19.1 us -> 17.8 us  [exchange(): lax.all_to_all(blocks, 'group', split_axis=0, concat_axis=0, tiled=True)]
    pallas_call x1, Pallas kernels: 2.44 us -> 1.23 us  [add(): pl.pallas_call(add_kernel, out_shape=jax.ShapeDtypeStruct(a.shape, a.dtyp...]
    pallas_call x2, Pallas kernels: 9.36 us -> 8.2 us  [pack(): pl.pallas_call(functools.partial(pack_kernel, lists, early), grid=(groups...]
  transfers between devices with their start and end apart: 5 -> 5, of which waited for: 5 -> 5; matrix products, arithmetic and copies ran while one was open for 3% -> 3% of each run, Pallas kernels for 23% -> 19%
where the time goes in v9:
time: 85.7 us; the launch traced here: 84.1 us
  waiting for transfers between devices  33.4 us (39%)
  Pallas kernels  27.6 us (32%)
  starting transfers between devices  19.9 us (23%)
  local copies, waits for them, and re-layouts  1.64 us (2%)
    all_to_all x3, starting transfers between devices, exchange(): lax.all_to_all(blocks, 'group', split_axis=0, concat_axis=0, tiled=True)  17.8 us
    ppermute x1, waiting for transfers between devices, local(): other = lax.ppermute(send, 'cuts', [(0, 1), (1, 0)])  16 us
    all_to_all x3, waiting for transfers between devices, exchange(): lax.all_to_all(blocks, 'group', split_axis=0, concat_axis=0, tiled=True)  8.8 us
    ppermute x1, waiting for transfers between devices, local(): other_early = lax.ppermute(own_early, 'cuts', [(0, 1), (1, 0)])  8.61 us
    pallas_call x2, Pallas kernels, pack(): pl.pallas_call(functools.partial(pack_kernel, lists, early), grid=(groups...  8.2 us
    pallas_call x1, Pallas kernels, places(): pl.pallas_call(functools.partial(places_kernel, own_rows, early, late), o...  6.58 us
    pallas_call x1, Pallas kernels, late_part(): pl.pallas_call(late_kernel, grid=(blocks,), out_shape=jax.ShapeDtypeStruc...  4.88 us
    pallas_call x1, Pallas kernels, early_part(): pl.pallas_call(early_kernel, out_shape=jax.ShapeDtypeStruct((slots, width...  4.66 us
  transfers between devices with their start and end apart: 5, of which 5 were waited for; matrix products, arithmetic and copies ran while one was open for 3% of the time, Pallas kernels for 19%

profile of v9, /device:TPU:0, one launch (start us, length us, event | category | flops | bytes accessed | tf_op | source)
XLA Modules:
  0.0 84.1 jit_solution(3806579260966598137)
XLA Ops:
  0.0 2.1 %shard_map.48 = bf16[128,128]{1,0:T(8,128)(2,1)} custom-call(s32[4,1024]{1,0:T(4,128)} %slots_ref.1, s32[4]{0:T(128)} %counts_ref.1), custom_call_target="tpu_custom_call" | custom-call | flops 268435456 | bytes 131072 | tf_op jit(solution)/shard_map/pallas_call | solution.py:143
  2.1 7.4 %all-to-all-start.4 = ((bf16[16,8,128]{2,1,0:T(8,128)(2,1)}), bf16[16,8,128]{2,1,0:T(8,128)(2,1)S(1)}, u32[]{:S(2)}, u32[]{:S(2)}) async-start(bf16[16,8,128]{2,1,0:T(8,128)(2,1)} %bitcast.65), calls=%async_computation.4 | async-start | bytes 65536 | tf_op jit(solution)/shard_map/all_to_all | solution.py:355
  9.5 6.6 %all-to-all-done.4 = bf16[16,8,128]{2,1,0:T(8,128)(2,1)S(1)} async-done(((bf16[16,8,128]{2,1,0:T(8,128)(2,1)}), bf16[16,8,128]{2,1,0:T(8,128)(2,1)S(1)}, u32[]{:S(2)}, u32[]{:S(2)}) %all-to-all-start.4) | async-done | bytes 32800 | tf_op jit(solution)/shard_map/all_to_all | solution.py:355
  16.1 4.7 %shard_map.49 = (bf16[16,64,512]{2,1,0:T(8,128)(2,1)}, bf16[16,64,512]{2,1,0:T(8,128)(2,1)S(1)}) custom-call(s32[1]{0:T(128)} %bitcast.20.plane_ref, bf16[128,128]{1,0:T(8,128)(2,1)S(1)} %bitcast.55, bf16[16,256,512]{2,1,0:T(8,128)(2,1)} %bitcast.57, bf16[2,256,256]{2,1,0:T(8,128)(2,1)} %bitcast.60), custom_call_target="tpu_custom_call" | custom-call | flops 1610612736 | bytes 6291456 | tf_op jit(solution)/shard_map/pallas_call | solution.py:205
  20.8 1.5 %collective-permute-start.4 = (bf16[16,64,512]{2,1,0:T(8,128)(2,1)S(1)}, bf16[16,64,512]{2,1,0:T(8,128)(2,1)S(1)}, u32[]{:S(2)}, u32[]{:S(2)}) collective-permute-start(bf16[16,64,512]{2,1,0:T(8,128)(2,1)S(1)} %get-tuple-element.49), channel_id=1, source_target_pairs={{0,16},{16,0},{1,17},{17,1},{2,18},{18,2},{3,19},{19,3},{4,20},{20... | collective-permute-start | bytes 3145736 | tf_op jit(solution)/shard_map/ppermute | solution.py:390
  22.3 3.7 %all-to-all-start.5 = ((bf16[16,64,512]{2,1,0:T(8,128)(2,1)}), bf16[16,64,512]{2,1,0:T(8,128)(2,1)S(1)}, u32[]{:S(2)}, u32[]{:S(2)}) async-start(bf16[16,64,512]{2,1,0:T(8,128)(2,1)} %get-tuple-element.48), calls=%async_computation.5 | async-start | bytes 2097152 | tf_op jit(solution)/shard_map/all_to_all | solution.py:355
  25.9 3.5 %shard_map.50.a_ref = bf16[16,64,512]{2,1,0:T(8,128)(2,1)S(1)} custom-call(s32[1]{0:T(128)} %bitcast.20.plane_ref, bf16[128,128]{1,0:T(8,128)(2,1)S(1)} %bitcast.56, bf16[16,256,512]{2,1,0:T(8,128)(2,1)} %bitcast.58, bf16[2,256,256]{2,1,0:T(8,128)(2,1)} %bitcast.61), custom_call_target="tpu_custom_call" | custom-call | flops 805306368 | bytes 6291456 | tf_op jit(solution)/shard_map/pallas_call | solution.py:205
  29.5 0.0 copy-start.8
  29.5 0.0 copy-start.9
  29.5 16.0 %collective-permute-done.4.b_ref = bf16[16,64,512]{2,1,0:T(8,128)(2,1)S(1)} collective-permute-done((bf16[16,64,512]{2,1,0:T(8,128)(2,1)S(1)}, bf16[16,64,512]{2,1,0:T(8,128)(2,1)S(1)}, u32[]{:S(2)}, u32[]{:S(2)}) %collective-permute-start.4) | collective-permute-done | bytes 1048608 | tf_op jit(solution)/shard_map/ppermute | solution.py:390
  45.5 1.2 %shard_map.51 = bf16[16,64,512]{2,1,0:T(8,128)(2,1)} custom-call(bf16[16,64,512]{2,1,0:T(8,128)(2,1)S(1)} %shard_map.50.a_ref, bf16[16,64,512]{2,1,0:T(8,128)(2,1)S(1)} %collective-permute-done.4.b_ref), custom_call_target="tpu_custom_call" | custom-call | flops 17179869184 | bytes 17179869184 | tf_op jit(solution)/shard_map/pallas_call | solution.py:234
  46.7 2.1 %all-to-all-done.5 = bf16[16,64,512]{2,1,0:T(8,128)(2,1)S(1)} async-done(((bf16[16,64,512]{2,1,0:T(8,128)(2,1)}), bf16[16,64,512]{2,1,0:T(8,128)(2,1)S(1)}, u32[]{:S(2)}, u32[]{:S(2)}) %all-to-all-start.5) | async-done | bytes 1048608 | tf_op jit(solution)/shard_map/all_to_all | solution.py:355
  48.8 0.5 collective-permute-start.5
  49.3 0.0 copy-done.8
  49.3 0.0 copy-done.9
  49.3 0.1 fusion.5
  49.4 6.8 %all-to-all-start.6 = ((bf16[16,64,512]{2,1,0:T(8,128)(2,1)}), bf16[16,64,512]{2,1,0:T(8,128)(2,1)S(1)}, u32[]{:S(2)}, u32[]{:S(2)}) async-start(bf16[16,64,512]{2,1,0:T(8,128)(2,1)} %shard_map.51), calls=%async_computation.6 | async-start | bytes 2097152 | tf_op jit(solution)/shard_map/all_to_all | solution.py:355
  56.3 0.6 slice_bitcast_fusion.8
  56.9 0.1 copy.22
  57.0 0.2 reshape.39
  57.2 0.7 copy.23
  57.9 6.6 %shard_map.52 = (s32[2,128,128]{2,1,0:T(8,128)}, s32[2,128,128]{2,1,0:T(8,128)}) custom-call(s32[1]{0:T(128)} %bitcast.20.plane_ref, s32[4,512]{1,0:T(4,128)} %get-tuple-element.67.slots_ref, s32[128,16]{1,0:T(8,128)} %bitcast.64), custom_call_target="tpu_custom_call" | custom-call | flops 268435456 | bytes 262144 | tf_op jit(solution)/shard_map/pallas_call | solution.py:282
  64.5 0.7 slice_reduce_fusion
  65.9 8.6 %collective-permute-done.5.other_ref = bf16[1024,512]{1,0:T(8,128)(2,1)S(1)} collective-permute-done((bf16[1024,512]{1,0:T(8,128)(2,1)S(1)}, bf16[1024,512]{1,0:T(8,128)(2,1)S(1)}, u32[]{:S(2)}, u32[]{:S(2)}) %collective-permute-start.5) | collective-permute-done | bytes 1048608 | tf_op jit(solution)/shard_map/ppermute | solution.py:393
  74.5 4.7 %shard_map.53 = bf16[2048,512]{1,0:T(8,128)(2,1)} custom-call(s32[2,128,128]{2,1,0:T(8,128)} %get-tuple-element.52.places_ref, bf16[1024,512]{1,0:T(8,128)(2,1)S(1)} %bitcast.50, bf16[1024,512]{1,0:T(8,128)(2,1)S(1)} %collective-permute-done.5.other_ref), custom_call_target="tpu_custom_call" | custom-call | flops 17179869184 | bytes 17179869184 | tf_op jit(solution)/shard_map/pallas_call | solution.py:322
  79.1 0.1 all-to-all-done.6
  79.2 4.9 %conditional.1 = (bf16[512,4,512]{2,1,0:T(4,128)(2,1)}) conditional(s32[]{:T(128)} %convert_element_type.40, (bf16[16,64,512]{2,1,0:T(8,128)(2,1)S(1)}, s32[2,128,128]{2,1,0:T(8,128)}, bf16[2048,512]{1,0:T(8,128)(2,1)}) %tuple.15, (bf16[1,64,64,512]{3,2,1,0:T(8,128)(2,1)}, bf16[2,256,256]{2,1,0:T(8,128)(2,1)}, s32[4,1024]{1,0:T(4,128)S(1)}) %tuple.32), branch_computations={%region_1.2_spmd, %region_2.3_spmd} | conditional | flops 6449790976 | bytes 70369768 | solution.py:397
  79.2 4.9 %branch_0_fun.1 = bf16[512,4,512]{2,1,0:T(4,128)(2,1)} custom-call(s32[2,128,128]{2,1,0:T(8,128)} %get-tuple-element.22.places_ref, bf16[1024,512]{1,0:T(8,128)(2,1)S(1)} %bitcast.63, bf16[2048,512]{1,0:T(8,128)(2,1)} %get-tuple-element.24.early_ref), custom_call_target="tpu_custom_call" | custom-call | flops 2147483648 | bytes 2097152 | tf_op jit(solution)/shard_map/cond/branch_0_fun/pallas_call | solution.py:337
  (1 shorter events, 0.0 us)
Async XLA Ops:
  2.1 14.0 %all-to-all-start.4 = ((bf16[16,8,128]{2,1,0:T(8,128)(2,1)}), bf16[16,8,128]{2,1,0:T(8,128)(2,1)S(1)}, u32[]{:S(2)}, u32[]{:S(2)}) async-start(bf16[16,8,128]{2,1,0:T(8,128)(2,1)} %bitcast.65), calls=%async_computation.4 | async-start | bytes 65536 | tf_op jit(solution)/shard_map/all_to_all | solution.py:355
  20.8 24.8 %collective-permute-start.4 = (bf16[16,64,512]{2,1,0:T(8,128)(2,1)S(1)}, bf16[16,64,512]{2,1,0:T(8,128)(2,1)S(1)}, u32[]{:S(2)}, u32[]{:S(2)}) collective-permute-start(bf16[16,64,512]{2,1,0:T(8,128)(2,1)S(1)} %get-tuple-element.49), channel_id=1, source_target_pairs={{0,16},{16,0},{1,17},{17,1},{2,18},{18,2},{3,19},{19,3},{4,20},{20... | collective-permute-start | bytes 3145736 | tf_op jit(solution)/shard_map/ppermute | solution.py:390
  22.3 26.6 %all-to-all-start.5 = ((bf16[16,64,512]{2,1,0:T(8,128)(2,1)}), bf16[16,64,512]{2,1,0:T(8,128)(2,1)S(1)}, u32[]{:S(2)}, u32[]{:S(2)}) async-start(bf16[16,64,512]{2,1,0:T(8,128)(2,1)} %get-tuple-element.48), calls=%async_computation.5 | async-start | bytes 2097152 | tf_op jit(solution)/shard_map/all_to_all | solution.py:355
  29.5 19.9 %copy-start.8 = (s32[4,1024]{1,0:T(4,128)S(1)}, s32[4,1024]{1,0:T(4,128)}, u32[]{:S(2)}) copy-start(s32[4,1024]{1,0:T(4,128)} %slots_ref.1) | copy-start | bytes 49156
  29.5 19.9 %copy-start.9 = (s32[4]{0:T(128)S(1)}, s32[4]{0:T(128)}, u32[]{:S(2)}) copy-start(s32[4]{0:T(128)} %counts_ref.1) | copy-start | bytes 52
  48.8 25.6 %collective-permute-start.5 = (bf16[1024,512]{1,0:T(8,128)(2,1)S(1)}, bf16[1024,512]{1,0:T(8,128)(2,1)S(1)}, u32[]{:S(2)}, u32[]{:S(2)}) collective-permute-start(bf16[1024,512]{1,0:T(8,128)(2,1)S(1)} %bitcast.49), channel_id=1, source_target_pairs={{0,16},{16,0},{1,17},{17,1},{2,18},{18,2},{3,19},{19,3},{4,20},{20... | collective-permute-start | bytes 3145736 | tf_op jit(solution)/shard_map/ppermute | solution.py:393
  49.4 29.8 %all-to-all-start.6 = ((bf16[16,64,512]{2,1,0:T(8,128)(2,1)}), bf16[16,64,512]{2,1,0:T(8,128)(2,1)S(1)}, u32[]{:S(2)}, u32[]{:S(2)}) async-start(bf16[16,64,512]{2,1,0:T(8,128)(2,1)} %shard_map.51), calls=%async_computation.6 | async-start | bytes 2097152 | tf_op jit(solution)/shard_map/all_to_all | solution.py:355

commit v10 on v9

--- a/solution.py
+++ b/solution.py
@@ -27,7 +27,7 @@
 
 def terms_of(rows, pair):
     total, width = rows.shape
-    block = min(2048, total)
+    block = min(512, total)
     out_width = 2 * pair.shape[2]
     return pl.pallas_call(
         terms_kernel,
@@ -46,7 +46,10 @@
 def select_kernel(block, share, terms_ref, slots_ref, *outs):
     columns = iota((block, terms_ref.shape[0]), 1)
     for part, out in enumerate(outs):
-        for start in range(0, share, block):
+
+        @pl.loop(0, share // block)
+        def _(step):
+            start = pl.multiple_of(step * block, block)
             chosen = mark(columns == slots_ref[pl.ds(part * share + start, block), :])
             out[pl.ds(start, block), :] = dot(chosen, terms_ref[...]).astype(out.dtype)
 
@@ -95,7 +98,8 @@
 LANES = 128
 STEP = 8
 PART = 2
-EARLY, LATE = 64, 64
+EARLY = 56
+LATES = 56, 64, 72
 ADD_BYTES, EARLY_BYTES = 1<<34, 1<<34
 
 
@@ -115,7 +119,7 @@
     return jnp.where(condition, 1.0, 0.0).astype(jnp.bfloat16)
 
 
-def needs_kernel(own_rows, early, late, slots_ref, counts_ref, flags_ref):
+def needs_kernel(own_rows, slots_ref, counts_ref, flags_ref):
     mine, slot_total = slots_ref.shape
     side = flags_ref.shape[0]
     hits = jnp.zeros((side, LANES), jnp.float32)
@@ -134,14 +138,14 @@
     sums = jnp.sum(flags, axis=1, keepdims=True)
     pairs = sums + jnp.concatenate([sums[1:], sums[:1]], axis=0)
     kind = iota((side, 1), 0) % KINDS
-    over = jnp.where(kind == 0, pairs - (early + late), jnp.where(kind == 2, pairs - late, 0.0))
-    spill = jnp.where(jnp.max(over) > 0.0, 1.0, 0.0)
-    flags_ref[...] = jnp.where(iota((side, LANES), 0) % KINDS == 6, spill, flags).astype(flags_ref.dtype)
-
-
-def needs(slot_rows, counts, own_rows, early, late, groups):
-    return pl.pallas_call(
-        functools.partial(needs_kernel, own_rows, early, late),
+    most = jnp.max(jnp.where(kind == 0, pairs - EARLY, jnp.where(kind == 2, pairs, 0.0)), axis=0, keepdims=True)
+    level = sum(jnp.where(most > late, 1.0, 0.0) for late in LATES)
+    flags_ref[...] = jnp.where(iota((side, LANES), 0) % KINDS == 6, level, flags).astype(flags_ref.dtype)
+
+
+def needs(slot_rows, counts, own_rows, groups):
+    return pl.pallas_call(
+        functools.partial(needs_kernel, own_rows),
         out_shape=jax.ShapeDtypeStruct((groups * KINDS, LANES), jnp.bfloat16),
         in_specs=[pl.BlockSpec(memory_space=pltpu.VMEM), pl.BlockSpec(memory_space=pltpu.SMEM)],
         out_specs=pl.BlockSpec(memory_space=pltpu.VMEM),
@@ -225,19 +229,21 @@
     )(plane, flags, pltpu.with_memory_space_constraint(stem, pltpu.HBM), pltpu.with_memory_space_constraint(pair, pltpu.HBM))
 
 
-def add_kernel(a_ref, b_ref, out_ref):
-    out_ref[...] = (a_ref[...].astype(jnp.float32) + b_ref[...].astype(jnp.float32)).astype(out_ref.dtype)
-
-
-def add(a, b):
+def add_kernel(a_ref, b_ref, *outs):
+    total = a_ref[...].astype(jnp.float32) + b_ref[...].astype(jnp.float32)
+    for out in outs:
+        out[...] = total[:, : out.shape[1]].astype(out.dtype)
+
+
+def add(a, b, sizes):
     vmem = pl.BlockSpec(memory_space=pltpu.VMEM)
     return pl.pallas_call(
         add_kernel,
-        out_shape=jax.ShapeDtypeStruct(a.shape, a.dtype),
+        out_shape=[jax.ShapeDtypeStruct((a.shape[0], size, a.shape[2]), a.dtype) for size in sizes],
         in_specs=[vmem] * 2,
-        out_specs=vmem,
+        out_specs=[vmem] * len(sizes),
         cost_estimate=pl.CostEstimate(flops=ADD_BYTES, bytes_accessed=ADD_BYTES, transcendentals=0),
-        compiler_params=pltpu.CompilerParams(vmem_limit_bytes=8 << 20),
+        compiler_params=pltpu.CompilerParams(vmem_limit_bytes=12 << 20),
     )(a, b)
 
 
@@ -321,7 +327,7 @@
     vmem = pl.BlockSpec(memory_space=pltpu.VMEM)
     return pl.pallas_call(
         early_kernel,
-        out_shape=jax.ShapeDtypeStruct((slots, width), own.dtype),
+        out_shape=pltpu.HBM((slots, width), own.dtype),
         in_specs=[vmem] * 3,
         out_specs=vmem,
         scratch_shapes=[pltpu.VMEM((rows, width), own.dtype)],
@@ -348,7 +354,7 @@
             flops=2 * rows * late.shape[0] * width, bytes_accessed=4 * late.size, transcendentals=0
         ),
         compiler_params=pltpu.CompilerParams(vmem_limit_bytes=12 << 20),
-    )(pltpu.with_memory_space_constraint(where, pltpu.HBM), late, early)
+    )(pltpu.with_memory_space_constraint(where, pltpu.HBM), late, pltpu.with_memory_space_constraint(early, pltpu.HBM))
 
 
 def exchange(blocks):
@@ -364,37 +370,43 @@
     stem = stem_blocks.reshape(group_total * own_rows, width)
     pair = cap_tensor[0]
 
-    positions = jnp.arange(slot_total, dtype=jnp.int32)
-    marked = jnp.where(positions[None, :] < counts[:, None], slot_rows, -1)
     me = lax.axis_index("cuts").astype(jnp.int32)
-    doubled = jnp.concatenate([marked, marked], axis=1)
-    turned = lax.dynamic_slice_in_dim(doubled, (me + 1) * share, slot_total, 1)
+
+    def turned_slots():
+        positions = jnp.arange(slot_total, dtype=jnp.int32)
+        marked = jnp.where(positions[None, :] < counts[:, None], slot_rows, -1)
+        doubled = jnp.concatenate([marked, marked], axis=1)
+        return lax.dynamic_slice_in_dim(doubled, (me + 1) * share, slot_total, 1)
 
     def all_rows():
         terms = terms_of(stem, pair)
-        return static_plan(terms.reshape(group_total, own_rows, terms.shape[1]), turned, cuts)
+        return static_plan(terms.reshape(group_total, own_rows, terms.shape[1]), turned_slots(), cuts)
 
     unfit = mine * own_rows != 2 * LANES or LANES % own_rows or groups > LANES or share * mine % (STEP * LANES)
     if cuts != 2 or unfit:
         return all_rows()
 
-    early, late = EARLY, LATE
     plane = me[None]
-    flags = needs(slot_rows, counts, own_rows, early, late, groups)
+    flags = needs(slot_rows, counts, own_rows, groups)
     flags = exchange(flags.reshape(groups, KINDS, LANES))
-    spilled = jnp.max(flags[:, 6, :].astype(jnp.float32)) > 0.0
+    level = jnp.max(flags[:, 6, :].astype(jnp.float32)).astype(jnp.int32)
     flags = flags.reshape(groups * KINDS, LANES)
     by_owner = stem.reshape(groups, mine * own_rows, width)
-    first, send = pack(("first", "send"), plane, flags, by_owner, pair, early, late)
-    (keep,) = pack(("keep",), plane, flags, by_owner, pair, early, late)
+    first, send = pack(("first", "send"), plane, flags, by_owner, pair, EARLY, LATES[-1])
+    (keep,) = pack(("keep",), plane, flags, by_owner, pair, EARLY, LATES[-1])
     other = lax.ppermute(send, "cuts", [(0, 1), (1, 0)])
-    own_early = exchange(first).reshape(groups * early, first.shape[2])
-    own_early, summed = lax.optimization_barrier((own_early, add(keep, other)))
-    other_early = lax.ppermute(own_early, "cuts", [(0, 1), (1, 0)])
-    own_late = exchange(summed).reshape(groups * late, summed.shape[2])
-    where_early, where_late = places(plane, turned[:, (cuts - 1) * share :], own_rows, early, late)
-    sums = early_part(where_early, own_early, other_early)
-    return lax.cond(spilled, all_rows, lambda: late_part(where_late, own_late, sums, mine))
+    own_early = exchange(first).reshape(groups * EARLY, first.shape[2])
+    own_early, sums = lax.optimization_barrier((own_early, add(keep, other, LATES)))
+
+    def rest(summed):
+        late = summed.shape[1]
+        other_early = lax.ppermute(own_early, "cuts", [(0, 1), (1, 0)])
+        own_late = exchange(summed).reshape(groups * late, summed.shape[2])
+        own_slots = turned_slots()[:, (cuts - 1) * share :]
+        where_early, where_late = places(plane, own_slots, own_rows, EARLY, late)
+        return late_part(where_late, own_late, early_part(where_early, own_early, other_early), mine)
+
+    return lax.switch(level, [functools.partial(rest, summed) for summed in sums] + [all_rows])
 
 
 def solution(mesh):

time: 85.7 us -> 82.2 us (0.959)
  starting transfers between devices: 19.9 us -> 17.7 us
  waiting for transfers between devices: 33.4 us -> 32 us
    all_to_all x3, starting transfers between devices: 17.8 us -> 14.6 us  [exchange(): lax.all_to_all(blocks, 'group', split_axis=0, concat_axis=0, tiled=True)]
    all_to_all x3, waiting for transfers between devices: 8.8 us -> 6.89 us  [exchange(): lax.all_to_all(blocks, 'group', split_axis=0, concat_axis=0, tiled=True)]
    ppermute x1, waiting for transfers between devices: 16 us -> 17.6 us  [local(): other = lax.ppermute(send, 'cuts', [(0, 1), (1, 0)])]
    ppermute x1, starting transfers between devices: 0.51 us -> 1.58 us  [rest(): other_early = lax.ppermute(own_early, 'cuts', [(0, 1), (1, 0)])]
    ppermute x1, waiting for transfers between devices: 8.61 us -> 7.56 us  [rest(): other_early = lax.ppermute(own_early, 'cuts', [(0, 1), (1, 0)])]
  transfers between devices with their start and end apart: 5 -> 5, of which waited for: 5 -> 4; matrix products, arithmetic and copies ran while one was open for 3% -> 3% of each run, Pallas kernels for 19% -> 21%
where the time goes in v10:
time: 82.2 us; the launch traced here: 81.1 us
  waiting for transfers between devices  32 us (39%)
  Pallas kernels  28.3 us (34%)
  starting transfers between devices  17.7 us (22%)
  other arithmetic  1.29 us (2%)
  local copies, waits for them, and re-layouts  1.05 us (1%)
    ppermute x1, waiting for transfers between devices, local(): other = lax.ppermute(send, 'cuts', [(0, 1), (1, 0)])  17.6 us
    all_to_all x3, starting transfers between devices, exchange(): lax.all_to_all(blocks, 'group', split_axis=0, concat_axis=0, tiled=True)  14.6 us
    pallas_call x2, Pallas kernels, pack(): pl.pallas_call(functools.partial(pack_kernel, lists, early), grid=(groups...  8.27 us
    ppermute x1, waiting for transfers between devices, rest(): other_early = lax.ppermute(own_early, 'cuts', [(0, 1), (1, 0)])  7.56 us
    all_to_all x3, waiting for transfers between devices, exchange(): lax.all_to_all(blocks, 'group', split_axis=0, concat_axis=0, tiled=True)  6.89 us
    pallas_call x1, Pallas kernels, places(): pl.pallas_call(functools.partial(places_kernel, own_rows, early, late), o...  6.56 us
    pallas_call x1, Pallas kernels, late_part(): pl.pallas_call(late_kernel, grid=(blocks,), out_shape=jax.ShapeDtypeStruc...  4.88 us
    pallas_call x1, Pallas kernels, early_part(): pl.pallas_call(early_kernel, out_shape=pltpu.HBM((slots, width), own.dtyp...  4.64 us
  transfers between devices with their start and end apart: 5, of which 4 were waited for; matrix products, arithmetic and copies ran while one was open for 3% of the time, Pallas kernels for 21%

profile of v10, /device:TPU:0, one launch (start us, length us, event | category | flops | bytes accessed | tf_op | source)
XLA Modules:
  0.0 81.1 jit_solution(3851894775114178642)
XLA Ops:
  0.0 2.0 %shard_map.50 = bf16[128,128]{1,0:T(8,128)(2,1)} custom-call(s32[4,1024]{1,0:T(4,128)} %slots_ref.1, s32[4]{0:T(128)} %counts_ref.1), custom_call_target="tpu_custom_call" | custom-call | flops 268435456 | bytes 131072 | tf_op jit(solution)/shard_map/pallas_call | solution.py:147
  2.0 7.4 %all-to-all-start.7 = ((bf16[16,8,128]{2,1,0:T(8,128)(2,1)}), bf16[16,8,128]{2,1,0:T(8,128)(2,1)S(1)}, u32[]{:S(2)}, u32[]{:S(2)}) async-start(bf16[16,8,128]{2,1,0:T(8,128)(2,1)} %bitcast.78), calls=%async_computation.7 | async-start | bytes 65536 | tf_op jit(solution)/shard_map/all_to_all | solution.py:361
  9.4 6.6 %all-to-all-done.7 = bf16[16,8,128]{2,1,0:T(8,128)(2,1)S(1)} async-done(((bf16[16,8,128]{2,1,0:T(8,128)(2,1)}), bf16[16,8,128]{2,1,0:T(8,128)(2,1)S(1)}, u32[]{:S(2)}, u32[]{:S(2)}) %all-to-all-start.7) | async-done | bytes 32800 | tf_op jit(solution)/shard_map/all_to_all | solution.py:361
  16.0 4.7 %shard_map.51 = (bf16[16,56,512]{2,1,0:T(8,128)(2,1)}, bf16[16,72,512]{2,1,0:T(8,128)(2,1)S(1)}) custom-call(s32[1]{0:T(128)} %bitcast.28.plane_ref, bf16[128,128]{1,0:T(8,128)(2,1)S(1)} %bitcast.64, bf16[16,256,512]{2,1,0:T(8,128)(2,1)} %bitcast.66, bf16[2,256,256]{2,1,0:T(8,128)(2,1)} %bitcast.69), custom_call_target="tpu_custom_call" | custom-call | flops 1610612736 | bytes 6291456 | tf_op jit(solution)/shard_map/pallas_call | solution.py:209
  20.7 1.5 %collective-permute-start.7 = (bf16[16,72,512]{2,1,0:T(8,128)(2,1)S(1)}, bf16[16,72,512]{2,1,0:T(8,128)(2,1)S(1)}, u32[]{:S(2)}, u32[]{:S(2)}) collective-permute-start(bf16[16,72,512]{2,1,0:T(8,128)(2,1)S(1)} %get-tuple-element.110), channel_id=1, source_target_pairs={{0,16},{16,0},{1,17},{17,1},{2,18},{18,2},{3,19},{19,3},{4,20},{20... | collective-permute-start | bytes 3538952 | tf_op jit(solution)/shard_map/ppermute | solution.py:397
  22.2 3.6 %all-to-all-start.8 = ((bf16[16,56,512]{2,1,0:T(8,128)(2,1)}), bf16[16,56,512]{2,1,0:T(8,128)(2,1)S(1)}, u32[]{:S(2)}, u32[]{:S(2)}) async-start(bf16[16,56,512]{2,1,0:T(8,128)(2,1)} %get-tuple-element.109), calls=%async_computation.8 | async-start | bytes 1835008 | tf_op jit(solution)/shard_map/all_to_all | solution.py:361
  25.9 0.6 slice_reduce_fusion
  27.0 3.6 %shard_map.52.a_ref = bf16[16,72,512]{2,1,0:T(8,128)(2,1)S(1)} custom-call(s32[1]{0:T(128)} %bitcast.28.plane_ref, bf16[128,128]{1,0:T(8,128)(2,1)S(1)} %bitcast.65, bf16[16,256,512]{2,1,0:T(8,128)(2,1)} %bitcast.67, bf16[2,256,256]{2,1,0:T(8,128)(2,1)} %bitcast.70), custom_call_target="tpu_custom_call" | custom-call | flops 905969664 | bytes 6291456 | tf_op jit(solution)/shard_map/pallas_call | solution.py:209
  30.6 0.0 copy-start.7
  30.6 0.0 copy-start.8
  30.7 17.6 %collective-permute-done.7.b_ref = bf16[16,72,512]{2,1,0:T(8,128)(2,1)S(1)} collective-permute-done((bf16[16,72,512]{2,1,0:T(8,128)(2,1)S(1)}, bf16[16,72,512]{2,1,0:T(8,128)(2,1)S(1)}, u32[]{:S(2)}, u32[]{:S(2)}) %collective-permute-start.7) | collective-permute-done | bytes 1179680 | tf_op jit(solution)/shard_map/ppermute | solution.py:397
  48.3 1.9 %shard_map.53 = (bf16[16,56,512]{2,1,0:T(8,128)(2,1)}, bf16[16,64,512]{2,1,0:T(8,128)(2,1)}, bf16[16,72,512]{2,1,0:T(8,128)(2,1)}) custom-call(bf16[16,72,512]{2,1,0:T(8,128)(2,1)S(1)} %shard_map.52.a_ref, bf16[16,72,512]{2,1,0:T(8,128)(2,1)S(1)} %collective-permute-done.7.b_ref), custom_call_target="tpu_custom_call" | custom-call | flops 17179869184 | bytes 17179869184 | tf_op jit(solution)/shard_map/pallas_call | solution.py:240
  50.2 0.0 all-to-all-done.8
  50.2 0.0 copy-done.7
  50.2 0.0 copy-done.8
  50.2 30.9 %conditional.1 = (bf16[512,4,512]{2,1,0:T(4,128)(2,1)}) conditional(s32[]{:T(128)} %clamp.3, (s32[4]{0:T(128)S(1)}, s32[4,1024]{1,0:T(4,128)S(1)}, s32[]{:T(128)}, s32[1]{0:T(128)}, bf16[16,56,512]{2,1,0:T(8,128)(2,1)}, /*index=5*/bf16[896,512]{1,0:T(8,128)(2,1)S(1)}) %tuple.57, (s32[4]{0:T(128)S(1)}, ...), branch_computations={%region_1.2_spmd, %region_2.3_spmd, %region_3.4_spmd, %region_4.5_... | conditional | flops 19864236032 | bytes 17189830656 | solution.py:409
  50.2 1.6 %collective-permute-start.4 = (bf16[896,512]{1,0:T(8,128)(2,1)S(1)}, bf16[896,512]{1,0:T(8,128)(2,1)S(1)}, u32[]{:S(2)}, u32[]{:S(2)}) collective-permute-start(bf16[896,512]{1,0:T(8,128)(2,1)S(1)} %get-tuple-element.64.own_ref), channel_id=1, source_target_pairs={{0,16},{16,0},{1,17},{17,1},{2,18},{18,2},{3,19},{19,3},{4,20},{20... | collective-permute-start | bytes 2752520 | tf_op jit(solution)/shard_map/cond/branch_0_fun/ppermute | solution.py:403
  51.8 3.6 %all-to-all-start.4 = ((bf16[16,56,512]{2,1,0:T(8,128)(2,1)}), bf16[16,56,512]{2,1,0:T(8,128)(2,1)S(1)}, u32[]{:S(2)}, u32[]{:S(2)}) async-start(bf16[16,56,512]{2,1,0:T(8,128)(2,1)} %get-tuple-element.62), calls=%async_computation.4 | async-start | bytes 1835008 | tf_op jit(solution)/shard_map/cond/branch_0_fun/all_to_all | solution.py:361
  55.5 0.1 fusion
  55.5 0.1 copy.17
  55.7 0.2 reshape.35
  55.9 0.7 copy.18
  56.6 0.6 fusion.1.slots_ref
  57.2 6.6 %branch_0_fun.3 = (s32[2,128,128]{2,1,0:T(8,128)}, s32[2,128,128]{2,1,0:T(8,128)}) custom-call(s32[1]{0:T(128)} %get-tuple-element.56.plane_ref, s32[4,512]{1,0:T(4,128)} %fusion.1.slots_ref, s32[128,16]{1,0:T(8,128)} %bitcast.75), custom_call_target="tpu_custom_call" | custom-call | flops 268435456 | bytes 262144 | tf_op jit(solution)/shard_map/cond/branch_0_fun/pallas_call | solution.py:288
  63.8 7.6 %collective-permute-done.4.other_ref = bf16[896,512]{1,0:T(8,128)(2,1)S(1)} collective-permute-done((bf16[896,512]{1,0:T(8,128)(2,1)S(1)}, bf16[896,512]{1,0:T(8,128)(2,1)S(1)}, u32[]{:S(2)}, u32[]{:S(2)}) %collective-permute-start.4) | collective-permute-done | bytes 917536 | tf_op jit(solution)/shard_map/cond/branch_0_fun/ppermute | solution.py:403
  71.3 4.6 %branch_0_fun.4.early_ref = bf16[2048,512]{1,0:T(8,128)(2,1)} custom-call(s32[2,128,128]{2,1,0:T(8,128)} %get-tuple-element.63.places_ref, bf16[896,512]{1,0:T(8,128)(2,1)S(1)} %get-tuple-element.64.own_ref, bf16[896,512]{1,0:T(8,128)(2,1)S(1)} %collective-permute-done.4.other_ref), custom_call_target="tpu_custom_call" | custom-call | flops 17179869184 | bytes 17179869184 | tf_op jit(solution)/shard_map/cond/branch_0_fun/pallas_call | solution.py:328
  76.0 0.3 all-to-all-done.4
  76.2 4.9 %branch_0_fun.5 = bf16[512,4,512]{2,1,0:T(4,128)(2,1)} custom-call(s32[2,128,128]{2,1,0:T(8,128)} %get-tuple-element.61.places_ref, bf16[896,512]{1,0:T(8,128)(2,1)S(1)} %bitcast.63, bf16[2048,512]{1,0:T(8,128)(2,1)} %branch_0_fun.4.early_ref), custom_call_target="tpu_custom_call" | custom-call | flops 1879048192 | bytes 1835008 | tf_op jit(solution)/shard_map/cond/branch_0_fun/pallas_call | solution.py:343
  (1 shorter events, 0.0 us)
Async XLA Ops:
  2.0 14.0 %all-to-all-start.7 = ((bf16[16,8,128]{2,1,0:T(8,128)(2,1)}), bf16[16,8,128]{2,1,0:T(8,128)(2,1)S(1)}, u32[]{:S(2)}, u32[]{:S(2)}) async-start(bf16[16,8,128]{2,1,0:T(8,128)(2,1)} %bitcast.78), calls=%async_computation.7 | async-start | bytes 65536 | tf_op jit(solution)/shard_map/all_to_all | solution.py:361
  20.7 27.5 %collective-permute-start.7 = (bf16[16,72,512]{2,1,0:T(8,128)(2,1)S(1)}, bf16[16,72,512]{2,1,0:T(8,128)(2,1)S(1)}, u32[]{:S(2)}, u32[]{:S(2)}) collective-permute-start(bf16[16,72,512]{2,1,0:T(8,128)(2,1)S(1)} %get-tuple-element.110), channel_id=1, source_target_pairs={{0,16},{16,0},{1,17},{17,1},{2,18},{18,2},{3,19},{19,3},{4,20},{20... | collective-permute-start | bytes 3538952 | tf_op jit(solution)/shard_map/ppermute | solution.py:397
  22.2 28.0 %all-to-all-start.8 = ((bf16[16,56,512]{2,1,0:T(8,128)(2,1)}), bf16[16,56,512]{2,1,0:T(8,128)(2,1)S(1)}, u32[]{:S(2)}, u32[]{:S(2)}) async-start(bf16[16,56,512]{2,1,0:T(8,128)(2,1)} %get-tuple-element.109), calls=%async_computation.8 | async-start | bytes 1835008 | tf_op jit(solution)/shard_map/all_to_all | solution.py:361
  30.6 19.6 %copy-start.7 = (s32[4,1024]{1,0:T(4,128)S(1)}, s32[4,1024]{1,0:T(4,128)}, u32[]{:S(2)}) copy-start(s32[4,1024]{1,0:T(4,128)} %slots_ref.1) | copy-start | bytes 49156
  30.6 19.6 %copy-start.8 = (s32[4]{0:T(128)S(1)}, s32[4]{0:T(128)}, u32[]{:S(2)}) copy-start(s32[4]{0:T(128)} %counts_ref.1) | copy-start | bytes 52
  50.2 21.1 %collective-permute-start.4 = (bf16[896,512]{1,0:T(8,128)(2,1)S(1)}, bf16[896,512]{1,0:T(8,128)(2,1)S(1)}, u32[]{:S(2)}, u32[]{:S(2)}) collective-permute-start(bf16[896,512]{1,0:T(8,128)(2,1)S(1)} %get-tuple-element.64.own_ref), channel_id=1, source_target_pairs={{0,16},{16,0},{1,17},{17,1},{2,18},{18,2},{3,19},{19,3},{4,20},{20... | collective-permute-start | bytes 2752520 | tf_op jit(solution)/shard_map/cond/branch_0_fun/ppermute | solution.py:403
  51.8 24.4 %all-to-all-start.4 = ((bf16[16,56,512]{2,1,0:T(8,128)(2,1)}), bf16[16,56,512]{2,1,0:T(8,128)(2,1)S(1)}, u32[]{:S(2)}, u32[]{:S(2)}) async-start(bf16[16,56,512]{2,1,0:T(8,128)(2,1)} %get-tuple-element.62), calls=%async_computation.4 | async-start | bytes 1835008 | tf_op jit(solution)/shard_map/cond/branch_0_fun/all_to_all | solution.py:361
